TPU v7x, 256 devices: a whole 4x4x8 slice. The times are simulated.
256 devices in a mesh: dp: 4 (over z_lo, core), seq: 64 (over y, z_hi, x).
Axes of the slice: x: 4, y: 4, z: 8 (z_hi: 4, z_lo: 2; z = z_hi * 2 + z_lo), core: 2. Of those that a mesh axis runs over, the one named last changes fastest.
Arguments:
- activations: bfloat16 [4, 8192, 768], P('dp', 'seq'), may hold values from -600 to 600
- conv_weight: bfloat16 [3840, 768], replicated, may hold values from -0.09375 to 0.09375
- head_first: bfloat16 [768, 768], replicated, may hold values from -0.21875 to 0.21875
- head_second: bfloat16 [768], replicated, may hold values from -5 to 5
- hidden_cotangent: bfloat16 [4, 8192, 768], P('dp', 'seq'), may hold values from -3 to 3
- score_cotangent: float32 [4, 8192], P('dp', 'seq'), may hold values from -5 to 5
- donor_row: int32 [4, 8192], P('dp', 'seq'), may hold values from 0 to 127
- acceptor_owner: int32 [4, 8192, 1], P('dp', 'seq'), may hold values from 0 to 63; in each aligned block of 128 rows (0 to 127, 128 to 255, ..., all dimensions but the last counted through in order) at most 4 rows name the same one
- acceptor_row: int32 [4, 8192], P('dp', 'seq'), may hold values from 0 to 127
Outputs:
- input_grad: bfloat16 [4, 8192, 768], P('dp', 'seq')
- weight_grads: float32 [4608, 768], P('seq', 'dp')
Inputs may be any that keep to these rules, and one draw needn't show every extreme that they name: `acceptor_owner`: among the 128 pairs of one block of positions, no block index is named by more than 4 pairs, a bound that some block reaches in every draw.
All inputs are finite; a program needn't handle non-finite values.
Results may differ from a plain program's by a relative error of at most 0.01.
Values may be sent and summed in bfloat16 or wider, within the bound.
No kernel may reach another device: no remote copies, remote signals or barrier semaphores. Data moves between devices by JAX's collectives and lax.ppermute only.
A program may use at most 64 MiB of HBM per device.

v0:
```python
import math

import jax
import jax.numpy as jnp
from jax import lax
from jax.sharding import PartitionSpec as P

DILATION = 8


def with_halo(cells, sides, width):
    for axis, dim in sides:
        count = lax.axis_size(axis)
        ends = count - 1
        head = lax.slice_in_dim(cells, 0, width, axis=dim)
        tail = lax.slice_in_dim(cells, cells.shape[dim] - width, cells.shape[dim], axis=dim)
        cells = jnp.concatenate(
            [
                lax.ppermute(tail, axis, [(i, (i + 1) % count) for i in range(ends)]),
                cells,
                lax.ppermute(head, axis, [((i + 1) % count, i) for i in range(ends)]),
            ],
            axis=dim,
        )
    return cells


def gelu_slope(values):
    normal_cdf = 0.5 * (1.0 + lax.erf(values * (1.0 / math.sqrt(2.0))))
    density = jnp.exp(-0.5 * values * values) * (1.0 / math.sqrt(2.0 * math.pi))
    return normal_cdf + values * density


def contract_rows(left_side, right_side):
    return lax.dot_general(
        left_side, right_side, (((0,), (0,)), ((), ())), preferred_element_type=jnp.float32
    )


def widened(field, reach_rows):
    return with_halo(field, (("seq", 0),), reach_rows)


def per_device(
    activations,
    conv_weight,
    head_first,
    head_second,
    hidden_cotangent,
    score_cotangent,
    donor_row,
    acceptor_owner,
    acceptor_row,
):
    row_count = activations.shape[1]
    chan_count = activations.shape[2]
    out_count = conv_weight.shape[1]
    tap_count = conv_weight.shape[0] // chan_count
    reach_rows = (tap_count - 1) // 2 * DILATION
    shards = lax.axis_size("seq")
    batch_total = lax.axis_size("dp") * activations.shape[0]
    pair_count = donor_row.shape[1]
    capacity = max(2, 2 * pair_count // shards)
    input_values = activations[0].astype(jnp.float32)
    norm_inverse = lax.rsqrt(jnp.mean(input_values * input_values, axis=1, keepdims=True) + 1e-05)
    normed = (input_values * norm_inverse).astype(jnp.bfloat16)
    padded = widened(normed, reach_rows)
    columns = jnp.concatenate(
        [
            padded[tap_index * DILATION : tap_index * DILATION + row_count]
            for tap_index in range(tap_count)
        ],
        axis=1,
    )
    preact = jnp.dot(columns, conv_weight, preferred_element_type=jnp.float32)
    hidden = jax.nn.gelu(preact, approximate=False).astype(jnp.bfloat16)
    owner_index = acceptor_owner[0, :, 0]
    owner_hits = (owner_index[:, None] == jnp.arange(shards, dtype=jnp.int32)[None, :]).astype(
        jnp.int32
    )
    earlier = jnp.cumsum(owner_hits, axis=0) - owner_hits
    slot_index = jnp.sum(earlier * owner_hits, axis=1)
    target = owner_index * capacity + slot_index
    request = (
        jnp.full((shards * capacity,), -1, jnp.int32)
        .at[target]
        .set(acceptor_row[0])
        .reshape(shards, capacity)
    )
    asked_rows = lax.all_to_all(request, "seq", split_axis=0, concat_axis=0, tiled=True)
    picked = jnp.take(hidden, jnp.maximum(asked_rows, 0), axis=0)
    returned = lax.all_to_all(picked, "seq", split_axis=0, concat_axis=0, tiled=True)
    accept_feat = returned.reshape(shards * capacity, out_count)[target]
    donor_feat = hidden[donor_row[0]]
    accept_values = accept_feat.astype(jnp.float32)
    donor_values = donor_feat.astype(jnp.float32)
    pair_feature = (donor_values * accept_values).astype(jnp.bfloat16)
    head_preact = jnp.dot(pair_feature, head_first, preferred_element_type=jnp.float32)
    head_delta = (
        score_cotangent[0][:, None]
        * head_second.astype(jnp.float32)[None, :]
        * gelu_slope(head_preact)
    ).astype(jnp.bfloat16)
    feature_grad = lax.dot_general(
        head_delta, head_first, (((1,), (1,)), ((), ())), preferred_element_type=jnp.float32
    )
    donor_grad = (feature_grad * accept_values).astype(jnp.bfloat16)
    accept_grad = (feature_grad * donor_values).astype(jnp.bfloat16)
    outgoing = (
        jnp.zeros((shards * capacity, out_count), jnp.bfloat16)
        .at[target]
        .set(accept_grad)
        .reshape(shards, capacity, out_count)
    )
    incoming = lax.all_to_all(outgoing, "seq", split_axis=0, concat_axis=0, tiled=True)
    row_ids = jnp.arange(row_count, dtype=jnp.int32)
    accept_hits = (asked_rows.reshape(-1)[:, None] == row_ids[None, :]).astype(jnp.bfloat16)
    donor_hits = (donor_row[0][:, None] == row_ids[None, :]).astype(jnp.bfloat16)
    hidden_grad = hidden_cotangent[0].astype(jnp.float32) + contract_rows(donor_hits, donor_grad)
    hidden_grad = hidden_grad + contract_rows(
        accept_hits, incoming.reshape(shards * capacity, out_count)
    )
    preact_grad = (hidden_grad * gelu_slope(preact)).astype(jnp.bfloat16)
    grad_padded = widened(preact_grad, reach_rows)
    spread = lax.dot_general(
        grad_padded, conv_weight, (((1,), (1,)), ((), ())), preferred_element_type=jnp.float32
    )
    normed_grad = spread[2 * reach_rows : 2 * reach_rows + row_count, 0:chan_count]
    for tap_index in range(1, tap_count):
        first_row = 2 * reach_rows - tap_index * DILATION
        normed_grad = (
            normed_grad
            + spread[
                first_row : first_row + row_count,
                tap_index * chan_count : (tap_index + 1) * chan_count,
            ]
        )
    input_grad = norm_inverse * normed_grad - input_values * norm_inverse**3 * jnp.mean(
        normed_grad * input_values, axis=1, keepdims=True
    )
    conv_term = contract_rows(columns, preact_grad) * (
        1.0 / math.sqrt(batch_total * row_count * shards)
    )
    head_term = contract_rows(pair_feature, head_delta) * (
        1.0 / math.sqrt(batch_total * pair_count * shards)
    )
    grad_term = jnp.concatenate([conv_term, head_term], axis=0)
    row_share = lax.psum_scatter(grad_term, "seq", scatter_dimension=0, tiled=True)
    weight_grads = lax.psum_scatter(
        row_share.astype(jnp.bfloat16), "dp", scatter_dimension=1, tiled=True
    ).astype(jnp.float32)
    return (input_grad.astype(jnp.bfloat16)[None], weight_grads)


def solution(mesh):
    placed = (
        P("dp", "seq", None),
        P(),
        P(),
        P(),
        P("dp", "seq", None),
        P("dp", "seq"),
        P("dp", "seq"),
        P("dp", "seq", None),
        P("dp", "seq"),
    )
    return jax.shard_map(
        per_device,
        mesh=mesh,
        in_specs=placed,
        out_specs=(P("dp", "seq", None), P("seq", "dp")),
        check_vma=False,
    )
```

profile of v0, /device:TPU:24, one launch (start us, length us, event | category | flops | bytes accessed | tf_op | source)
XLA Modules:
  0.0 413.5 jit_solution(3529426373660581315)
XLA Ops:
  9.7 1.1 scatter_custom_fusion
  11.5 14.5 %all-to-all-start = ((s32[64,1,4]{2,1,0:T(1,128)}), s32[64,1,4]{2,1,0:T(1,128)S(1)}, u32[]{:S(2)}, u32[]{:S(2)}) async-start(s32[64,1,4]{2,1,0:T(1,128)} %bitcast.12), calls=%async_computation | async-start | bytes 65536 | tf_op jit(solution)/shard_map/all_to_all | solution.py:90
  28.2 7.9 %collective-permute-start.1 = (bf16[16,768]{1,0:T(8,128)(2,1)S(1)}, bf16[16,768]{1,0:T(8,128)(2,1)S(1)}, u32[]{:S(2)}, u32[]{:S(2)}) collective-permute-start(bf16[16,768]{1,0:T(8,128)(2,1)S(1)} %get-tuple-element.8), channel_id=1, source_target_pairs={{1,0},{2,1},{3,2},{4,3},{5,4},{6,5},{7,6},{8,7},{9,8},{10,9},{11,1... | collective-permute-start | bytes 73736 | tf_op jit(solution)/shard_map/ppermute | solution.py:21
  36.1 1.9 collective-permute-start
  39.7 7.2 %collective-permute-done = bf16[16,768]{1,0:T(8,128)(2,1)S(1)} collective-permute-done((bf16[16,768]{1,0:T(8,128)(2,1)S(1)}, bf16[16,768]{1,0:T(8,128)(2,1)S(1)}, u32[]{:S(2)}, u32[]{:S(2)}) %collective-permute-start) | collective-permute-done | bytes 24608 | tf_op jit(solution)/shard_map/ppermute | solution.py:19
  48.0 5.5 %fusion.7 = (bf16[128,768]{1,0:T(8,128)(2,1)S(1)}, f32[128,768]{1,0:T(8,128)}) fusion(bf16[128,3840]{1,0:T(8,128)(2,1)S(1)} %fusion.45, bf16[3840,768]{1,0:T(8,128)(2,1)} %param.10), kind=kOutput, calls=%fused_computation.27 | convolution fusion | flops 761364480 | bytes 7471104 | tf_op jit(solution)/shard_map/dot_general | solution.py:75
  53.5 1.2 gather_fusion.1
  55.9 6.3 %all-to-all-start.1 = ((bf16[64,4,768]{2,1,0:T(4,128)(2,1)}), bf16[64,4,768]{2,1,0:T(4,128)(2,1)S(1)}, u32[]{:S(2)}, u32[]{:S(2)}) async-start(bf16[64,4,768]{2,1,0:T(4,128)(2,1)} %broadcast_select_fusion), calls=%async_computation.1 | async-start | bytes 786432 | tf_op jit(solution)/shard_map/all_to_all | solution.py:92
  63.1 12.7 %all-to-all-done.1 = bf16[64,4,768]{2,1,0:T(4,128)(2,1)S(1)} async-done(((bf16[64,4,768]{2,1,0:T(4,128)(2,1)}), bf16[64,4,768]{2,1,0:T(4,128)(2,1)S(1)}, u32[]{:S(2)}, u32[]{:S(2)}) %all-to-all-start.1) | async-done | bytes 393248 | tf_op jit(solution)/shard_map/all_to_all | solution.py:92
  78.4 1.3 scatter_custom_fusion.1
  80.5 7.6 %all-to-all-start.2 = ((bf16[64,4,768]{2,1,0:T(4,128)(2,1)}), bf16[64,4,768]{2,1,0:T(4,128)(2,1)}, u32[]{:S(2)}, u32[]{:S(2)}) async-start(bf16[64,4,768]{2,1,0:T(4,128)(2,1)} %reshape.124), calls=%async_computation.2 | async-start | bytes 786432 | tf_op jit(solution)/shard_map/all_to_all | solution.py:115
  88.5 1.1 convolution_add_fusion.1
  89.6 1.6 convolution_multiply_fusion.1
  91.2 9.6 %all-to-all-done.2 = bf16[64,4,768]{2,1,0:T(4,128)(2,1)} async-done(((bf16[64,4,768]{2,1,0:T(4,128)(2,1)}), bf16[64,4,768]{2,1,0:T(4,128)(2,1)}, u32[]{:S(2)}, u32[]{:S(2)}) %all-to-all-start.2) | async-done | bytes 393248 | tf_op jit(solution)/shard_map/all_to_all | solution.py:115
  100.8 1.8 reshape.125
  102.6 1.6 fusion.1
  104.9 2.9 convolution_multiply_fusion
  107.8 5.4 %pad_maximum_fusion = f32[4608,768]{1,0:T(8,128)} fusion(f32[768,768]{1,0:T(8,128)S(1)} %convolution_multiply_fusion.1, f32[3840,768]{1,0:T(8,128)S(1)} %convolution_multiply_fusion), kind=kLoop, calls=%fused_computation.5 | loop fusion | flops 3538944 | bytes 28311552 | tf_op jit(solution)/shard_map/concatenate | solution.py:147
  114.2 2.8 collective-permute-start.2
  117.0 8.2 %collective-permute-start.3 = (bf16[16,768]{1,0:T(8,128)(2,1)S(1)}, bf16[16,768]{1,0:T(8,128)(2,1)S(1)}, u32[]{:S(2)}, u32[]{:S(2)}) collective-permute-start(bf16[16,768]{1,0:T(8,128)(2,1)S(1)} %get-tuple-element.7), channel_id=1, source_target_pairs={{1,0},{2,1},{3,2},{4,3},{5,4},{6,5},{7,6},{8,7},{9,8},{10,9},{11,1... | collective-permute-start | bytes 73736 | tf_op jit(solution)/shard_map/ppermute | solution.py:21
  125.2 1.5 collective-permute-done.3
  126.6 4.8 %fusion.31 = f32[160,3840]{1,0:T(8,128)S(1)} fusion(bf16[3840,768]{1,0:T(8,128)(2,1)} %param.10, bf16[16,768]{1,0:T(8,128)(2,1)S(1)} %collective-permute-done.3, bf16[128,768]{1,0:T(8,128)(2,1)S(1)} %copy-done.6, bf16[16,768]{1,0:T(8,128)(2,1)S(1)} %collective-permute-done.2), kind=kOutput, calls=%fused_computation.64 | convolution fusion | flops 944455680 | bytes 8601600 | tf_op jit(solution)/shard_map/dot_general | solution.py:125
  131.7 253.4 %reduce-scatter.5.cloned.1.call-done = f32[72,768]{1,0:T(8,128)} async-done(((f32[4608,768]{1,0:T(8,128)}), f32[72,768]{1,0:T(8,128)}) %reduce-scatter.5.cloned.1.call-update) | async-done | bytes 221200 | tf_op jit(solution)/shard_map/reduce_scatter | solution.py:148
  387.7 17.4 %reduce-scatter.7.cloned.1.call-done = bf16[192,72]{1,0:T(8,128)(2,1)} async-done(((bf16[768,72]{1,0:T(8,128)(2,1)}), bf16[192,72]{1,0:T(8,128)(2,1)}) %reduce-scatter.7.cloned.1.call-update) | async-done | bytes 27664
  (72 shorter events, 19.8 us)
Async XLA Ops:
  7.2 69.6 %copy-start = (bf16[768,768]{1,0:T(8,128)(2,1)S(1)}, bf16[768,768]{1,0:T(8,128)(2,1)}, u32[]{:S(2)}) copy-start(bf16[768,768]{1,0:T(8,128)(2,1)} %param.11) | copy-start | bytes 3538948
  11.5 26.5 %all-to-all-start = ((s32[64,1,4]{2,1,0:T(1,128)}), s32[64,1,4]{2,1,0:T(1,128)S(1)}, u32[]{:S(2)}, u32[]{:S(2)}) async-start(s32[64,1,4]{2,1,0:T(1,128)} %bitcast.12), calls=%async_computation | async-start | bytes 65536 | tf_op jit(solution)/shard_map/all_to_all | solution.py:90
  28.2 19.8 %collective-permute-start.1 = (bf16[16,768]{1,0:T(8,128)(2,1)S(1)}, bf16[16,768]{1,0:T(8,128)(2,1)S(1)}, u32[]{:S(2)}, u32[]{:S(2)}) collective-permute-start(bf16[16,768]{1,0:T(8,128)(2,1)S(1)} %get-tuple-element.8), channel_id=1, source_target_pairs={{1,0},{2,1},{3,2},{4,3},{5,4},{6,5},{7,6},{8,7},{9,8},{10,9},{11,1... | collective-permute-start | bytes 73736 | tf_op jit(solution)/shard_map/ppermute | solution.py:21
  36.1 10.8 %collective-permute-start = (bf16[16,768]{1,0:T(8,128)(2,1)S(1)}, bf16[16,768]{1,0:T(8,128)(2,1)S(1)}, u32[]{:S(2)}, u32[]{:S(2)}) collective-permute-start(bf16[16,768]{1,0:T(8,128)(2,1)S(1)} %get-tuple-element.9), channel_id=1, source_target_pairs={{0,1},{1,2},{2,3},{3,4},{4,5},{5,6},{6,7},{7,8},{8,9},{9,10},{10,1... | collective-permute-start | bytes 73736 | tf_op jit(solution)/shard_map/ppermute | solution.py:19
  48.0 5.5 %copy-start.2 = (bf16[128,3840]{1,0:T(8,128)(2,1)}, bf16[128,3840]{1,0:T(8,128)(2,1)S(1)}, u32[]{:S(2)}) copy-start(bf16[128,3840]{1,0:T(8,128)(2,1)S(1)} %fusion.45) | copy-start | bytes 2949124
  53.5 8.6 %copy-start.9 = (bf16[768]{0:T(1024)(128)(2,1)S(1)}, bf16[768]{0:T(1024)(128)(2,1)}, u32[]{:S(2)}) copy-start(bf16[768]{0:T(1024)(128)(2,1)} %param.12) | copy-start | bytes 4612
  53.5 8.6 %copy-start.10 = (s32[1,128]{1,0:T(1,128)S(1)}, s32[1,128]{1,0:T(1,128)}, u32[]{:S(2)}) copy-start(s32[1,128]{1,0:T(1,128)} %param.15) | copy-start | bytes 1540
  53.5 23.2 %copy-start.11 = (f32[1,128]{1,0:T(1,128)S(1)}, f32[1,128]{1,0:T(1,128)}, u32[]{:S(2)}) copy-start(f32[1,128]{1,0:T(1,128)} %param.14) | copy-start | bytes 1540
  55.9 32.7 %copy-start.8 = (bf16[1,128,768]{2,1,0:T(8,128)(2,1)S(1)}, bf16[1,128,768]{2,1,0:T(8,128)(2,1)}, u32[]{:S(2)}) copy-start(bf16[1,128,768]{2,1,0:T(8,128)(2,1)} %param.13) | copy-start | bytes 589828
  55.9 19.9 %all-to-all-start.1 = ((bf16[64,4,768]{2,1,0:T(4,128)(2,1)}), bf16[64,4,768]{2,1,0:T(4,128)(2,1)S(1)}, u32[]{:S(2)}, u32[]{:S(2)}) async-start(bf16[64,4,768]{2,1,0:T(4,128)(2,1)} %broadcast_select_fusion), calls=%async_computation.1 | async-start | bytes 786432 | tf_op jit(solution)/shard_map/all_to_all | solution.py:92
  63.0 25.4 %copy-start.3 = (bf16[128,768]{1,0:T(8,128)(2,1)}, bf16[128,768]{1,0:T(8,128)(2,1)S(1)}, u32[]{:S(2)}) copy-start(bf16[128,768]{1,0:T(8,128)(2,1)S(1)} %gather_fusion) | copy-start | bytes 589828
  76.8 11.7 %copy-start.4 = (bf16[128,768]{1,0:T(8,128)(2,1)}, bf16[128,768]{1,0:T(8,128)(2,1)S(1)}, u32[]{:S(2)}) copy-start(bf16[128,768]{1,0:T(8,128)(2,1)S(1)} %gather_fusion.2) | copy-start | bytes 589828
  77.2 0.7 copy-start.7
  80.5 20.2 %all-to-all-start.2 = ((bf16[64,4,768]{2,1,0:T(4,128)(2,1)}), bf16[64,4,768]{2,1,0:T(4,128)(2,1)}, u32[]{:S(2)}, u32[]{:S(2)}) async-start(bf16[64,4,768]{2,1,0:T(4,128)(2,1)} %reshape.124), calls=%async_computation.2 | async-start | bytes 786432 | tf_op jit(solution)/shard_map/all_to_all | solution.py:115
  88.1 297.0 %reduce-scatter.5.cloned.1.call-start = ((), (), s32[]{:S(2)}) async-start(), calls=%async_computation.5 | async-start | bytes 14376960 | tf_op jit(solution)/shard_map/reduce_scatter | solution.py:148
  104.2 0.7 copy-start.5
  113.2 0.9 copy-start.6
  113.3 18.2 %copy-start.1 = (bf16[1,128,768]{2,1,0:T(8,128)(2,1)S(1)}, bf16[1,128,768]{2,1,0:T(8,128)(2,1)}, u32[]{:S(2)}) copy-start(bf16[1,128,768]{2,1,0:T(8,128)(2,1)} %param.9) | copy-start | bytes 589828
  113.3 291.9 %reduce-scatter.7.cloned.1.call-start = ((), (), s32[]{:S(2)}) async-start(), calls=%async_computation.6 | async-start | bytes 245760
  114.2 11.0 %collective-permute-start.2 = (bf16[16,768]{1,0:T(8,128)(2,1)S(1)}, bf16[16,768]{1,0:T(8,128)(2,1)S(1)}, u32[]{:S(2)}, u32[]{:S(2)}) collective-permute-start(bf16[16,768]{1,0:T(8,128)(2,1)S(1)} %get-tuple-element.6), channel_id=1, source_target_pairs={{0,1},{1,2},{2,3},{3,4},{4,5},{5,6},{6,7},{7,8},{8,9},{9,10},{10,1... | collective-permute-start | bytes 73736 | tf_op jit(solution)/shard_map/ppermute | solution.py:19
  117.0 9.7 %collective-permute-start.3 = (bf16[16,768]{1,0:T(8,128)(2,1)S(1)}, bf16[16,768]{1,0:T(8,128)(2,1)S(1)}, u32[]{:S(2)}, u32[]{:S(2)}) collective-permute-start(bf16[16,768]{1,0:T(8,128)(2,1)S(1)} %get-tuple-element.7), channel_id=1, source_target_pairs={{1,0},{2,1},{3,2},{4,3},{5,4},{6,5},{7,6},{8,7},{9,8},{10,9},{11,1... | collective-permute-start | bytes 73736 | tf_op jit(solution)/shard_map/ppermute | solution.py:21
Sparse Core Ops, SparseCore 0:
  113.4 271.6 reduce-scatter.4
  387.6 17.4 reduce-scatter.6
where the time goes:
time: 416 us; the launch traced here: 414 us
  waiting for transfers between devices  302 us (73%)
  starting transfers between devices  49.4 us (12%)
  matrix products  18.4 us (4%)
  other arithmetic  16.9 us (4%)
  between operations  14.4 us (3%)
  local copies, waits for them, and re-layouts  12.5 us (3%)
    reduce_scatter x1, waiting for transfers between devices, per_device(): lax.psum_scatter(grad_term, 'seq', scatter_dimension=0, tiled=True)  253 us
    unnamed x3, waiting for transfers between devices  17.4 us
    ppermute x2, starting transfers between devices, with_halo(): lax.ppermute(head, axis, [((i + 1) % count, i) for i in range(ends)])  16 us
    all_to_all x1, starting transfers between devices, per_device(): lax.all_to_all(request, 'seq', split_axis=0, concat_axis=0, tiled=True)  14.5 us
    all_to_all x1, waiting for transfers between devices, per_device(): lax.all_to_all(picked, 'seq', split_axis=0, concat_axis=0, tiled=True)  12.7 us
    all_to_all x1, waiting for transfers between devices, per_device(): lax.all_to_all(outgoing, 'seq', split_axis=0, concat_axis=0, tiled=True)  9.55 us
  transfers between devices with their start and end apart: 9, of which 6 were waited for; matrix products, arithmetic and copies ran while one was open for 3% of the time, Pallas kernels for 0%

commit v1 on v0

v1 whole, which is shorter than its diff:
```python
import math

import jax
import jax.numpy as jnp
from jax import lax
from jax.sharding import PartitionSpec as P

DILATION = 8


def gelu_slope(values):
    normal_cdf = 0.5 * (1.0 + lax.erf(values * (1.0 / math.sqrt(2.0))))
    density = jnp.exp(-0.5 * values * values) * (1.0 / math.sqrt(2.0 * math.pi))
    return normal_cdf + values * density


def contract_rows(left_side, right_side):
    return lax.dot_general(
        left_side, right_side, (((0,), (0,)), ((), ())), preferred_element_type=jnp.float32
    )


def seq_halo(cells, width):
    count = lax.axis_size("seq")
    above = lax.ppermute(cells[-width:], "seq", [(i, i + 1) for i in range(count - 1)])
    below = lax.ppermute(cells[:width], "seq", [(i + 1, i) for i in range(count - 1)])
    return above, below


def swap_core(field):
    return lax.ppermute(field, "dp", [(0, 1), (1, 0), (2, 3), (3, 2)])


def swap_z(field):
    return lax.ppermute(field, "dp", [(0, 2), (1, 3), (2, 0), (3, 1)])


def dp_peers(field):
    core = swap_core(field)
    z_side = swap_z(field)
    return field, core, z_side, swap_core(z_side)


def dp_columns(field, width):
    index = lax.axis_index("dp")
    found = []
    for flip in range(4):
        piece = lax.dynamic_slice_in_dim(field, (index ^ flip) * width, width, axis=1)
        if flip:
            piece = lax.ppermute(piece, "dp", [(i, i ^ flip) for i in range(4)])
        found.append(piece)
    return found


def per_device(
    activations,
    conv_weight,
    head_first,
    head_second,
    hidden_cotangent,
    score_cotangent,
    donor_row,
    acceptor_owner,
    acceptor_row,
):
    row_count = activations.shape[1]
    chan_count = activations.shape[2]
    out_count = conv_weight.shape[1]
    tap_count = conv_weight.shape[0] // chan_count
    reach_rows = (tap_count - 1) // 2 * DILATION
    shards = lax.axis_size("seq")
    dp_count = lax.axis_size("dp")
    pair_count = donor_row.shape[1]
    capacity = max(2, 2 * pair_count // shards)
    slots = shards * capacity
    col_width = out_count // dp_count

    above, below = seq_halo(activations[0], reach_rows)
    owner = acceptor_owner[0, :, 0]
    pair_ids = jnp.arange(pair_count, dtype=jnp.int32)
    rank = jnp.sum(
        ((owner[:, None] == owner[None, :]) & (pair_ids[None, :] < pair_ids[:, None])).astype(
            jnp.int32
        ),
        axis=1,
    )
    target = owner * capacity + rank
    placed = target[:, None] == jnp.arange(slots, dtype=jnp.int32)[None, :]

    def to_slots(values, empty):
        return jnp.sum(jnp.where(placed, (values - empty)[:, None], 0.0), axis=0) + empty

    score_slot = jnp.sum(jnp.where(placed, score_cotangent[0][:, None], 0.0), axis=0)
    accept_slot = to_slots(acceptor_row[0].astype(jnp.float32), -1.0)
    donor_slot = to_slots(donor_row[0].astype(jnp.float32), -1.0)
    ask = jnp.concatenate(
        [accept_slot.reshape(shards, capacity), score_slot.reshape(shards, capacity)], axis=1
    )
    asked = lax.all_to_all(ask, "seq", split_axis=0, concat_axis=0, tiled=True)

    padded_input = jnp.concatenate([above, activations[0], below], axis=0)
    padded_peers = dp_peers(padded_input)

    def normalise(field):
        values = field.astype(jnp.float32)
        inverse = lax.rsqrt(jnp.mean(values * values, axis=1, keepdims=True) + 1e-05)
        return values, inverse, (values * inverse).astype(jnp.bfloat16)

    padded_values, padded_inverse, padded = normalise(padded_input)
    input_values = padded_values[reach_rows : reach_rows + row_count]
    norm_inverse = padded_inverse[reach_rows : reach_rows + row_count]

    def tap_columns(field):
        return jnp.concatenate(
            [field[k * DILATION : k * DILATION + row_count] for k in range(tap_count)], axis=1
        )

    columns = tap_columns(padded)
    preact = jnp.dot(columns, conv_weight, preferred_element_type=jnp.float32)
    hidden = jax.nn.gelu(preact, approximate=False).astype(jnp.bfloat16)

    row_ids = jnp.arange(row_count, dtype=jnp.int32).astype(jnp.float32)
    own_rows = jnp.concatenate(
        [donor_slot.reshape(shards, capacity), asked[:, :capacity]], axis=1
    ).reshape(2 * slots)
    own_scores = jnp.concatenate(
        [score_slot.reshape(shards, capacity), asked[:, capacity:]], axis=1
    ).reshape(2 * slots)
    hits = (row_ids[:, None] == own_rows[None, :]).astype(jnp.bfloat16)
    sent = contract_rows(hits, hidden).astype(jnp.bfloat16)
    got = lax.all_to_all(
        sent.reshape(shards, 2 * capacity, out_count), "seq", split_axis=0, concat_axis=0, tiled=True
    )
    partner = jnp.concatenate([got[:, capacity:], got[:, :capacity]], axis=1).reshape(
        2 * slots, out_count
    )
    partner_values = partner.astype(jnp.float32)
    pair_feature = (sent.astype(jnp.float32) * partner_values).astype(jnp.bfloat16)

    def own_pairs(field):
        halves = field.reshape(shards, 2 * capacity, out_count)[:, :capacity].reshape(
            slots, out_count
        )
        return jnp.dot(placed.astype(jnp.bfloat16), halves, preferred_element_type=jnp.float32).astype(
            jnp.bfloat16
        )

    feature_peers = dp_peers(own_pairs(pair_feature))
    head_preact = jnp.dot(pair_feature, head_first, preferred_element_type=jnp.float32)
    head_delta = (
        own_scores[:, None] * head_second.astype(jnp.float32)[None, :] * gelu_slope(head_preact)
    ).astype(jnp.bfloat16)
    delta_peers = dp_columns(own_pairs(head_delta), col_width)
    feature_grad = lax.dot_general(
        head_delta, head_first, (((1,), (1,)), ((), ())), preferred_element_type=jnp.float32
    )
    row_grad = (feature_grad * partner_values).astype(jnp.bfloat16)
    hidden_grad = hidden_cotangent[0].astype(jnp.float32) + jnp.dot(
        hits, row_grad, preferred_element_type=jnp.float32
    )
    preact_grad = (hidden_grad * gelu_slope(preact)).astype(jnp.bfloat16)

    grad_peers = dp_columns(preact_grad, col_width)
    grad_above, grad_below = seq_halo(preact_grad, reach_rows)

    columns_all = jnp.concatenate(
        [columns] + [tap_columns(normalise(peer)[2]) for peer in padded_peers[1:]], axis=0
    )
    conv_term = contract_rows(columns_all, jnp.concatenate(grad_peers, axis=0)) * (
        1.0 / math.sqrt(dp_count * row_count * shards)
    )
    head_term = contract_rows(
        jnp.concatenate(feature_peers, axis=0), jnp.concatenate(delta_peers, axis=0)
    ) * (1.0 / math.sqrt(dp_count * pair_count * shards))
    term = jnp.concatenate([conv_term.astype(jnp.bfloat16), head_term.astype(jnp.bfloat16)], axis=0)
    share = term.shape[0] // shards
    terms = lax.all_to_all(
        term.reshape(shards, share, col_width), "seq", split_axis=0, concat_axis=0, tiled=True
    )
    weight_grads = jnp.sum(terms.astype(jnp.float32), axis=0)

    grad_padded = jnp.concatenate([grad_above, preact_grad, grad_below], axis=0)
    spread = lax.dot_general(
        grad_padded, conv_weight, (((1,), (1,)), ((), ())), preferred_element_type=jnp.float32
    )
    normed_grad = spread[2 * reach_rows : 2 * reach_rows + row_count, 0:chan_count]
    for tap_index in range(1, tap_count):
        first_row = 2 * reach_rows - tap_index * DILATION
        normed_grad = (
            normed_grad
            + spread[
                first_row : first_row + row_count,
                tap_index * chan_count : (tap_index + 1) * chan_count,
            ]
        )
    input_grad = norm_inverse * normed_grad - input_values * norm_inverse**3 * jnp.mean(
        normed_grad * input_values, axis=1, keepdims=True
    )
    return (input_grad.astype(jnp.bfloat16)[None], weight_grads)


def solution(mesh):
    placed = (
        P("dp", "seq", None),
        P(),
        P(),
        P(),
        P("dp", "seq", None),
        P("dp", "seq"),
        P("dp", "seq"),
        P("dp", "seq", None),
        P("dp", "seq"),
    )
    return jax.shard_map(
        per_device,
        mesh=mesh,
        in_specs=placed,
        out_specs=(P("dp", "seq", None), P("seq", "dp")),
        check_vma=False,
    )
```

time: 416 us -> 177 us (0.43)
  waiting for transfers between devices: 302 us -> 79.1 us
  between operations: 14.4 us -> 1.27 us
  starting transfers between devices: 49.4 us -> 56 us
  other arithmetic: 16.9 us -> 11.4 us
  local copies, waits for them, and re-layouts: 12.5 us -> 8.24 us
    reduce_scatter x1 -> x0, waiting for transfers between devices: 253 us -> none  [per_device(): lax.psum_scatter(grad_term, 'seq', scatter_dimension=0, tiled=True)]
    ppermute x4 -> x16, waiting for transfers between devices: 8.65 us -> 50.6 us  [the longest x2 39.8 us: seq_halo(): lax.ppermute(cells[:width], 'seq', [(i + 1, i) for i in range(count - 1)])]
    unnamed x3 -> x0, waiting for transfers between devices: 17.4 us -> none
    ppermute x4 -> x16, starting transfers between devices: 20.7 us -> 29.8 us  [the longest x2 18.4 us: seq_halo(): lax.ppermute(cells[:width], 'seq', [(i + 1, i) for i in range(count - 1)])]
    all_to_all x3, waiting for transfers between devices: 22.3 us -> 28.5 us  [the longest x1 19.5 us: per_device(): lax.all_to_all(sent.reshape(shards, 2 * capacity, out_count), 'seq', spli...]
    concatenate x2 -> x4, other arithmetic: 5.43 us -> 0.97 us  [the longest x1 0.7 us: per_device(): jnp.concatenate([accept_slot.reshape(shards, capacity), score_slot.reshap...]
  transfers between devices with their start and end apart: 9 -> 19, of which waited for: 6 -> 8; matrix products, arithmetic and copies ran while one was open for 3% -> 16% of each run, Pallas kernels for 0% -> 0%
where the time goes in v1:
time: 177 us; the launch traced here: 176 us
  waiting for transfers between devices  79.1 us (45%)
  starting transfers between devices  56 us (32%)
  matrix products  19.9 us (11%)
  other arithmetic  11.4 us (6%)
  local copies, waits for them, and re-layouts  8.24 us (5%)
    ppermute x2, waiting for transfers between devices, seq_halo(): lax.ppermute(cells[:width], 'seq', [(i + 1, i) for i in range(count - 1)])  39.8 us
    all_to_all x1, waiting for transfers between devices, per_device(): lax.all_to_all(sent.reshape(shards, 2 * capacity, out_count), 'seq', spli...  19.5 us
    ppermute x2, starting transfers between devices, seq_halo(): lax.ppermute(cells[:width], 'seq', [(i + 1, i) for i in range(count - 1)])  18.4 us
    all_to_all x1, starting transfers between devices, per_device(): asked = lax.all_to_all(ask, 'seq', split_axis=0, concat_axis=0, tiled=True)  11.8 us
    all_to_all x1, waiting for transfers between devices, per_device(): asked = lax.all_to_all(ask, 'seq', split_axis=0, concat_axis=0, tiled=True)  9.02 us
    all_to_all x1, starting transfers between devices, per_device(): lax.all_to_all(term.reshape(shards, share, col_width), 'seq', split_axis=...  7.72 us
    all_to_all x1, starting transfers between devices, per_device(): lax.all_to_all(sent.reshape(shards, 2 * capacity, out_count), 'seq', spli...  6.68 us
    ppermute x2, waiting for transfers between devices, seq_halo(): lax.ppermute(cells[-width:], 'seq', [(i, i + 1) for i in range(count - 1)])  6.11 us
  transfers between devices with their start and end apart: 19, of which 8 were waited for; matrix products, arithmetic and copies ran while one was open for 16% of the time, Pallas kernels for 0%

profile of v1, /device:TPU:24, one launch (start us, length us, event | category | flops | bytes accessed | tf_op | source)
XLA Modules:
  0.0 175.8 jit_solution(392247983841428914)
XLA Ops:
  1.5 10.6 %collective-permute-start.1 = (bf16[16,768]{1,0:T(8,128)(2,1)S(1)}, bf16[16,768]{1,0:T(8,128)(2,1)S(1)}, u32[]{:S(2)}, u32[]{:S(2)}) collective-permute-start(bf16[16,768]{1,0:T(8,128)(2,1)S(1)} %get-tuple-element.22), channel_id=1, source_target_pairs={{1,0},{2,1},{3,2},{4,3},{5,4},{6,5},{7,6},{8,7},{9,8},{10,9},{11,1... | collective-permute-start | bytes 73736 | tf_op jit(solution)/shard_map/ppermute | solution.py:26
  12.1 1.9 %collective-permute-start = (bf16[16,768]{1,0:T(8,128)(2,1)S(1)}, bf16[16,768]{1,0:T(8,128)(2,1)S(1)}, u32[]{:S(2)}, u32[]{:S(2)}) collective-permute-start(bf16[16,768]{1,0:T(8,128)(2,1)S(1)} %get-tuple-element.21), channel_id=1, source_target_pairs={{0,1},{1,2},{2,3},{3,4},{4,5},{5,6},{6,7},{7,8},{8,9},{9,10},{10,1... | collective-permute-start | bytes 73736 | tf_op jit(solution)/shard_map/ppermute | solution.py:25
  18.0 11.8 %all-to-all-start = ((f32[64,1,8]{2,1,0:T(1,128)}), f32[64,1,8]{2,1,0:T(1,128)S(1)}, u32[]{:S(2)}, u32[]{:S(2)}) async-start(f32[64,1,8]{2,1,0:T(1,128)} %bitcast.9), calls=%async_computation | async-start | bytes 65536 | tf_op jit(solution)/shard_map/all_to_all | solution.py:99
  30.7 9.0 %all-to-all-done = f32[64,1,8]{2,1,0:T(1,128)S(1)} async-done(((f32[64,1,8]{2,1,0:T(1,128)}), f32[64,1,8]{2,1,0:T(1,128)S(1)}, u32[]{:S(2)}, u32[]{:S(2)}) %all-to-all-start) | async-done | bytes 2080 | tf_op jit(solution)/shard_map/all_to_all | solution.py:99
  42.6 4.0 %fusion.153 = f32[128,768]{1,0:T(8,128)S(1)} fusion(bf16[128,3840]{1,0:T(8,128)(2,1)S(1)} %slice_dynamic-update-slice_fusion.15, bf16[3840,768]{1,0:T(8,128)(2,1)} %param.10), kind=kOutput, calls=%fused_computation.236 | convolution fusion | flops 754974720 | bytes 7274496 | tf_op jit(solution)/shard_map/dot_general | solution.py:119
  46.6 2.1 %convolution_convert_fusion = bf16[512,768]{1,0:T(8,128)(2,1)} fusion(f32[128,768]{1,0:T(8,128)S(1)} %fusion.153, f32[512]{0:T(512)S(1)} %eq.48, f32[128]{0:T(128)S(1)} %iota_convert_fusion), kind=kOutput, calls=%fused_computation.22 | convolution fusion | flops 107511808 | bytes 1182208 | tf_op jit(solution)/shard_map/dot_general | solution.py:18
  48.7 6.7 %all-to-all-start.1 = ((bf16[64,8,768]{2,1,0:T(8,128)(2,1)}), bf16[64,8,768]{2,1,0:T(8,128)(2,1)S(1)}, u32[]{:S(2)}, u32[]{:S(2)}) async-start(bf16[64,8,768]{2,1,0:T(8,128)(2,1)} %bitcast.11), calls=%async_computation.1 | async-start | bytes 1572864 | tf_op jit(solution)/shard_map/all_to_all | solution.py:131
  59.1 19.5 %all-to-all-done.1 = bf16[64,8,768]{2,1,0:T(8,128)(2,1)S(1)} async-done(((bf16[64,8,768]{2,1,0:T(8,128)(2,1)}), bf16[64,8,768]{2,1,0:T(8,128)(2,1)S(1)}, u32[]{:S(2)}, u32[]{:S(2)}) %all-to-all-start.1) | async-done | bytes 786464 | tf_op jit(solution)/shard_map/all_to_all | solution.py:131
  78.8 1.6 fusion.109
  81.6 2.0 %collective-permute-start.11 = (bf16[128,768]{1,0:T(8,128)(2,1)}, bf16[128,768]{1,0:T(8,128)(2,1)}, u32[]{:S(2)}, u32[]{:S(2)}) collective-permute-start(bf16[128,768]{1,0:T(8,128)(2,1)} %convolution_convert_fusion.2), channel_id=1, source_target_pairs={{0,128},{64,192},{128,0},{192,64},{1,129},{65,193},{129,1},{193,65... | collective-permute-start | bytes 589832 | tf_op jit(solution)/shard_map/ppermute | solution.py:35
  83.7 2.6 %fusion.15 = bf16[512,768]{1,0:T(8,128)(2,1)S(1)} fusion(f32[768]{0:T(1024)S(1)} %convert_element_type.114, f32[512]{0:T(512)S(1)} %mul.205, bf16[768,768]{1,0:T(8,128)(2,1)S(1)} %copy-done, bf16[512,768]{1,0:T(8,128)(2,1)} %convolution_convert_fusion, bf16[64,4,768]{2,1,0:T(4,128)(2,1)S(1)} %get-tuple-element.10, bf16[64,4,768]{2,1,0:T(4,128)(2,1)S(1)} %get-tuple-element.9), kind=kOutput, calls=%fused_computation.21 | convolution fusion | flops 611450880 | bytes 3544064 | tf_op jit(solution)/shard_map/dot_general | solution.py:149
  87.5 1.3 slice.193
  89.6 2.0 %collective-permute-start.8 = (bf16[128,192]{1,0:T(8,128)(2,1)S(1)}, bf16[128,192]{1,0:T(8,128)(2,1)S(1)}, u32[]{:S(2)}, u32[]{:S(2)}) collective-permute-start(bf16[128,192]{1,0:T(8,128)(2,1)S(1)} %get-tuple-element.13), channel_id=1, source_target_pairs={{0,128},{64,192},{128,0},{192,64},{1,129},{65,193},{129,1},{193,65... | collective-permute-start | bytes 147464 | tf_op jit(solution)/shard_map/ppermute | solution.py:50
  91.8 1.4 collective-permute-done.9
  93.7 1.5 collective-permute-done.8
  96.5 2.5 %fusion = bf16[3840,192]{0,1:T(8,128)(2,1)S(1)} fusion(bf16[128,3840]{1,0:T(8,128)(2,1)} %copy-done.9, bf16[128,3840]{1,0:T(8,128)(2,1)S(1)} %copy-done.7, bf16[128,3840]{1,0:T(8,128)(2,1)} %copy-done.8, bf16[128,3840]{1,0:T(8,128)(2,1)S(1)} %copy-done.3, bf16[128,192]{1,0:T(8,128)(2,1)S(1)} %collective-permute-done.9, ...), kind=kOutput, calls=%fused_computation.1 | convolution fusion | flops 772964352 | bytes 5603328 | tf_op jit(solution)/shard_map/dot_general | solution.py:18
  99.6 1.5 fusion.17
  101.2 2.4 %copy.23 = bf16[4608,192]{1,0:T(8,128)(2,1)} copy(bf16[4608,192]{0,1:T(8,128)(2,1)S(1)} %pad_maximum_fusion) | data formatting | bytes 3538944 | tf_op jit(solution)/shard_map/concatenate | solution.py:175
  103.6 7.7 %all-to-all-start.2 = ((bf16[64,72,192]{2,1,0:T(8,128)(2,1)}), bf16[64,72,192]{2,1,0:T(8,128)(2,1)S(1)}, u32[]{:S(2)}, u32[]{:S(2)}) async-start(bf16[64,72,192]{2,1,0:T(8,128)(2,1)} %bitcast.51), calls=%async_computation.2 | async-start | bytes 4718592 | tf_op jit(solution)/shard_map/all_to_all | solution.py:177
  112.1 7.9 %collective-permute-start.3 = (bf16[16,768]{1,0:T(8,128)(2,1)S(1)}, bf16[16,768]{1,0:T(8,128)(2,1)S(1)}, u32[]{:S(2)}, u32[]{:S(2)}) collective-permute-start(bf16[16,768]{1,0:T(8,128)(2,1)S(1)} %get-tuple-element.20), channel_id=1, source_target_pairs={{1,0},{2,1},{3,2},{4,3},{5,4},{6,5},{7,6},{8,7},{9,8},{10,9},{11,1... | collective-permute-start | bytes 73736 | tf_op jit(solution)/shard_map/ppermute | solution.py:26
  120.0 1.9 %collective-permute-start.2 = (bf16[16,768]{1,0:T(8,128)(2,1)S(1)}, bf16[16,768]{1,0:T(8,128)(2,1)S(1)}, u32[]{:S(2)}, u32[]{:S(2)}) collective-permute-start(bf16[16,768]{1,0:T(8,128)(2,1)S(1)} %get-tuple-element.19), channel_id=1, source_target_pairs={{0,1},{1,2},{2,3},{3,4},{4,5},{5,6},{6,7},{7,8},{8,9},{9,10},{10,1... | collective-permute-start | bytes 73736 | tf_op jit(solution)/shard_map/ppermute | solution.py:25
  123.0 39.7 %collective-permute-done.3 = bf16[16,768]{1,0:T(8,128)(2,1)S(1)} collective-permute-done((bf16[16,768]{1,0:T(8,128)(2,1)S(1)}, bf16[16,768]{1,0:T(8,128)(2,1)S(1)}, u32[]{:S(2)}, u32[]{:S(2)}) %collective-permute-start.3) | collective-permute-done | bytes 24608 | tf_op jit(solution)/shard_map/ppermute | solution.py:26
  162.8 6.1 %collective-permute-done.2 = bf16[16,768]{1,0:T(8,128)(2,1)S(1)} collective-permute-done((bf16[16,768]{1,0:T(8,128)(2,1)S(1)}, bf16[16,768]{1,0:T(8,128)(2,1)S(1)}, u32[]{:S(2)}, u32[]{:S(2)}) %collective-permute-start.2) | collective-permute-done | bytes 24608 | tf_op jit(solution)/shard_map/ppermute | solution.py:25
  168.9 4.9 %fusion.64 = f32[160,3840]{1,0:T(8,128)S(1)} fusion(bf16[3840,768]{1,0:T(8,128)(2,1)} %param.10, bf16[16,768]{1,0:T(8,128)(2,1)S(1)} %collective-permute-done.3, bf16[128,768]{1,0:T(8,128)(2,1)} %copy-done.4, bf16[16,768]{1,0:T(8,128)(2,1)S(1)} %collective-permute-done.2), kind=kOutput, calls=%fused_computation.100 | convolution fusion | flops 944455680 | bytes 8601600 | tf_op jit(solution)/shard_map/dot_general | solution.py:183
  (113 shorter events, 21.8 us)
Async XLA Ops:
  0.6 83.0 %copy-start = (bf16[768,768]{1,0:T(8,128)(2,1)S(1)}, bf16[768,768]{1,0:T(8,128)(2,1)}, u32[]{:S(2)}) copy-start(bf16[768,768]{1,0:T(8,128)(2,1)} %param.11) | copy-start | bytes 3538948
  1.5 38.6 %collective-permute-start.1 = (bf16[16,768]{1,0:T(8,128)(2,1)S(1)}, bf16[16,768]{1,0:T(8,128)(2,1)S(1)}, u32[]{:S(2)}, u32[]{:S(2)}) collective-permute-start(bf16[16,768]{1,0:T(8,128)(2,1)S(1)} %get-tuple-element.22), channel_id=1, source_target_pairs={{1,0},{2,1},{3,2},{4,3},{5,4},{6,5},{7,6},{8,7},{9,8},{10,9},{11,1... | collective-permute-start | bytes 73736 | tf_op jit(solution)/shard_map/ppermute | solution.py:26
  12.1 28.1 %collective-permute-start = (bf16[16,768]{1,0:T(8,128)(2,1)S(1)}, bf16[16,768]{1,0:T(8,128)(2,1)S(1)}, u32[]{:S(2)}, u32[]{:S(2)}) collective-permute-start(bf16[16,768]{1,0:T(8,128)(2,1)S(1)} %get-tuple-element.21), channel_id=1, source_target_pairs={{0,1},{1,2},{2,3},{3,4},{4,5},{5,6},{6,7},{7,8},{8,9},{9,10},{10,1... | collective-permute-start | bytes 73736 | tf_op jit(solution)/shard_map/ppermute | solution.py:25
  18.0 21.7 %all-to-all-start = ((f32[64,1,8]{2,1,0:T(1,128)}), f32[64,1,8]{2,1,0:T(1,128)S(1)}, u32[]{:S(2)}, u32[]{:S(2)}) async-start(f32[64,1,8]{2,1,0:T(1,128)} %bitcast.9), calls=%async_computation | async-start | bytes 65536 | tf_op jit(solution)/shard_map/all_to_all | solution.py:99
  41.2 5.4 %copy-start.1 = (bf16[160,768]{1,0:T(8,128)(2,1)}, bf16[160,768]{1,0:T(8,128)(2,1)S(1)}, u32[]{:S(2)}) copy-start(bf16[160,768]{1,0:T(8,128)(2,1)S(1)} %get-tuple-element.8) | copy-start | bytes 737284
  41.2 14.1 %collective-permute-start.5 = (bf16[160,768]{1,0:T(8,128)(2,1)S(1)}, bf16[160,768]{1,0:T(8,128)(2,1)S(1)}, u32[]{:S(2)}, u32[]{:S(2)}) collective-permute-start(bf16[160,768]{1,0:T(8,128)(2,1)S(1)} %get-tuple-element.8), channel_id=1, source_target_pairs={{0,128},{64,192},{128,0},{192,64},{1,129},{65,193},{129,1},{193,65... | collective-permute-start | bytes 737288 | tf_op jit(solution)/shard_map/ppermute | solution.py:35
  42.3 13.4 %collective-permute-start.4 = (bf16[160,768]{1,0:T(8,128)(2,1)S(1)}, bf16[160,768]{1,0:T(8,128)(2,1)S(1)}, u32[]{:S(2)}, u32[]{:S(2)}) collective-permute-start(bf16[160,768]{1,0:T(8,128)(2,1)S(1)} %get-tuple-element.8), channel_id=1, source_target_pairs={{0,64},{64,0},{128,192},{192,128},{1,65},{65,1},{129,193},{193,129... | collective-permute-start | bytes 737288 | tf_op jit(solution)/shard_map/ppermute | solution.py:31
  48.7 29.9 %all-to-all-start.1 = ((bf16[64,8,768]{2,1,0:T(8,128)(2,1)}), bf16[64,8,768]{2,1,0:T(8,128)(2,1)S(1)}, u32[]{:S(2)}, u32[]{:S(2)}) async-start(bf16[64,8,768]{2,1,0:T(8,128)(2,1)} %bitcast.11), calls=%async_computation.1 | async-start | bytes 1572864 | tf_op jit(solution)/shard_map/all_to_all | solution.py:131
  56.1 1.6 collective-permute-start.6
  81.6 4.6 %copy-start.10 = (bf16[1,128,768]{2,1,0:T(8,128)(2,1)S(1)}, bf16[1,128,768]{2,1,0:T(8,128)(2,1)}, u32[]{:S(2)}) copy-start(bf16[1,128,768]{2,1,0:T(8,128)(2,1)} %param.13) | copy-start | bytes 589828
  81.6 14.4 %collective-permute-start.11 = (bf16[128,768]{1,0:T(8,128)(2,1)}, bf16[128,768]{1,0:T(8,128)(2,1)}, u32[]{:S(2)}, u32[]{:S(2)}) collective-permute-start(bf16[128,768]{1,0:T(8,128)(2,1)} %convolution_convert_fusion.2), channel_id=1, source_target_pairs={{0,128},{64,192},{128,0},{192,64},{1,129},{65,193},{129,1},{193,65... | collective-permute-start | bytes 589832 | tf_op jit(solution)/shard_map/ppermute | solution.py:35
  83.6 15.9 %collective-permute-start.10 = (bf16[128,768]{1,0:T(8,128)(2,1)}, bf16[128,768]{1,0:T(8,128)(2,1)}, u32[]{:S(2)}, u32[]{:S(2)}) collective-permute-start(bf16[128,768]{1,0:T(8,128)(2,1)} %convolution_convert_fusion.2), channel_id=1, source_target_pairs={{0,64},{64,0},{128,192},{192,128},{1,65},{65,1},{129,193},{193,129... | collective-permute-start | bytes 589832 | tf_op jit(solution)/shard_map/ppermute | solution.py:31
  87.5 9.0 %copy-start.3 = (bf16[128,3840]{1,0:T(8,128)(2,1)S(1)}, bf16[128,3840]{1,0:T(8,128)(2,1)}, u32[]{:S(2)}) copy-start(bf16[128,3840]{1,0:T(8,128)(2,1)} %copy-done.2) | copy-start | bytes 2949124
  88.9 7.6 %copy-start.7 = (bf16[128,3840]{1,0:T(8,128)(2,1)S(1)}, bf16[128,3840]{1,0:T(8,128)(2,1)}, u32[]{:S(2)}) copy-start(bf16[128,3840]{1,0:T(8,128)(2,1)} %copy-done.6) | copy-start | bytes 2949124
  89.4 3.8 %collective-permute-start.9 = (bf16[128,192]{1,0:T(8,128)(2,1)S(1)}, bf16[128,192]{1,0:T(8,128)(2,1)S(1)}, u32[]{:S(2)}, u32[]{:S(2)}) collective-permute-start(bf16[128,192]{1,0:T(8,128)(2,1)S(1)} %get-tuple-element.12), channel_id=1, source_target_pairs={{0,192},{64,128},{128,64},{192,0},{1,193},{65,129},{129,65},{193,1... | collective-permute-start | bytes 147464 | tf_op jit(solution)/shard_map/ppermute | solution.py:50
  89.6 5.7 %collective-permute-start.8 = (bf16[128,192]{1,0:T(8,128)(2,1)S(1)}, bf16[128,192]{1,0:T(8,128)(2,1)S(1)}, u32[]{:S(2)}, u32[]{:S(2)}) collective-permute-start(bf16[128,192]{1,0:T(8,128)(2,1)S(1)} %get-tuple-element.13), channel_id=1, source_target_pairs={{0,128},{64,192},{128,0},{192,64},{1,129},{65,193},{129,1},{193,65... | collective-permute-start | bytes 147464 | tf_op jit(solution)/shard_map/ppermute | solution.py:50
  91.6 4.4 %collective-permute-start.7 = (bf16[128,192]{1,0:T(8,128)(2,1)S(1)}, bf16[128,192]{1,0:T(8,128)(2,1)S(1)}, u32[]{:S(2)}, u32[]{:S(2)}) collective-permute-start(bf16[128,192]{1,0:T(8,128)(2,1)S(1)} %get-tuple-element.14), channel_id=1, source_target_pairs={{0,64},{64,0},{128,192},{192,128},{1,65},{65,1},{129,193},{193,129... | collective-permute-start | bytes 147464 | tf_op jit(solution)/shard_map/ppermute | solution.py:50
  93.2 5.8 %collective-permute-start.15 = (bf16[128,192]{1,0:T(8,128)(2,1)S(1)}, bf16[128,192]{1,0:T(8,128)(2,1)S(1)}, u32[]{:S(2)}, u32[]{:S(2)}) collective-permute-start(bf16[128,192]{1,0:T(8,128)(2,1)S(1)} %get-tuple-element.16), channel_id=1, source_target_pairs={{0,192},{64,128},{128,64},{192,0},{1,193},{65,129},{129,65},{193,1... | collective-permute-start | bytes 147464 | tf_op jit(solution)/shard_map/ppermute | solution.py:50
  95.3 4.3 %collective-permute-start.14 = (bf16[128,192]{1,0:T(8,128)(2,1)S(1)}, bf16[128,192]{1,0:T(8,128)(2,1)S(1)}, u32[]{:S(2)}, u32[]{:S(2)}) collective-permute-start(bf16[128,192]{1,0:T(8,128)(2,1)S(1)} %get-tuple-element.17), channel_id=1, source_target_pairs={{0,128},{64,192},{128,0},{192,64},{1,129},{65,193},{129,1},{193,65... | collective-permute-start | bytes 147464 | tf_op jit(solution)/shard_map/ppermute | solution.py:50
  96.0 3.5 %collective-permute-start.13 = (bf16[128,192]{1,0:T(8,128)(2,1)S(1)}, bf16[128,192]{1,0:T(8,128)(2,1)S(1)}, u32[]{:S(2)}, u32[]{:S(2)}) collective-permute-start(bf16[128,192]{1,0:T(8,128)(2,1)S(1)} %get-tuple-element.18), channel_id=1, source_target_pairs={{0,64},{64,0},{128,192},{192,128},{1,65},{65,1},{129,193},{193,129... | collective-permute-start | bytes 147464 | tf_op jit(solution)/shard_map/ppermute | solution.py:50
  96.0 3.5 %collective-permute-start.12 = (bf16[128,768]{1,0:T(8,128)(2,1)}, bf16[128,768]{1,0:T(8,128)(2,1)S(1)}, u32[]{:S(2)}, u32[]{:S(2)}) collective-permute-start(bf16[128,768]{1,0:T(8,128)(2,1)} %collective-permute-done.11), channel_id=1, source_target_pairs={{0,64},{64,0},{128,192},{192,128},{1,65},{65,1},{129,193},{193,129... | collective-permute-start | bytes 589832 | tf_op jit(solution)/shard_map/ppermute | solution.py:31
  103.6 71.2 %all-to-all-start.2 = ((bf16[64,72,192]{2,1,0:T(8,128)(2,1)}), bf16[64,72,192]{2,1,0:T(8,128)(2,1)S(1)}, u32[]{:S(2)}, u32[]{:S(2)}) async-start(bf16[64,72,192]{2,1,0:T(8,128)(2,1)} %bitcast.51), calls=%async_computation.2 | async-start | bytes 4718592 | tf_op jit(solution)/shard_map/all_to_all | solution.py:177
  112.1 50.7 %collective-permute-start.3 = (bf16[16,768]{1,0:T(8,128)(2,1)S(1)}, bf16[16,768]{1,0:T(8,128)(2,1)S(1)}, u32[]{:S(2)}, u32[]{:S(2)}) collective-permute-start(bf16[16,768]{1,0:T(8,128)(2,1)S(1)} %get-tuple-element.20), channel_id=1, source_target_pairs={{1,0},{2,1},{3,2},{4,3},{5,4},{6,5},{7,6},{8,7},{9,8},{10,9},{11,1... | collective-permute-start | bytes 73736 | tf_op jit(solution)/shard_map/ppermute | solution.py:26
  120.0 48.9 %collective-permute-start.2 = (bf16[16,768]{1,0:T(8,128)(2,1)S(1)}, bf16[16,768]{1,0:T(8,128)(2,1)S(1)}, u32[]{:S(2)}, u32[]{:S(2)}) collective-permute-start(bf16[16,768]{1,0:T(8,128)(2,1)S(1)} %get-tuple-element.19), channel_id=1, source_target_pairs={{0,1},{1,2},{2,3},{3,4},{4,5},{5,6},{6,7},{7,8},{8,9},{9,10},{10,1... | collective-permute-start | bytes 73736 | tf_op jit(solution)/shard_map/ppermute | solution.py:25
  (6 other events, 14.4 us)

commit v2 on v1

--- a/solution.py
+++ b/solution.py
@@ -1,9 +1,13 @@
+import functools
 import math
 
 import jax
 import jax.numpy as jnp
 from jax import lax
+from jax.experimental import pallas as pl
+from jax.experimental.pallas import tpu as pltpu
 from jax.sharding import PartitionSpec as P
+
 
 DILATION = 8
 
@@ -50,6 +54,31 @@
             piece = lax.ppermute(piece, "dp", [(i, i ^ flip) for i in range(4)])
         found.append(piece)
     return found
+
+
+def weight_kernel(scale, taps, *refs):
+    normed_ref, out_ref = refs[0], refs[-1]
+    grads, features, deltas = refs[1:5], refs[5:9], refs[9:13]
+    chan_count = normed_ref.shape[0]
+    width = grads[0].shape[1]
+    reach = (taps - 1) * DILATION
+    values = [ref[...].astype(jnp.float32) for ref in grads]
+    for k in range(taps):
+        pieces = []
+        for value in values:
+            if k:
+                pieces.append(jnp.zeros((k * DILATION, width), jnp.float32))
+            pieces.append(value)
+            if k < taps - 1:
+                pieces.append(jnp.zeros((reach - k * DILATION, width), jnp.float32))
+        shifted = jnp.concatenate(pieces, axis=0).astype(jnp.bfloat16)
+        term = jnp.dot(normed_ref[...], shifted, preferred_element_type=jnp.float32)
+        out_ref[k * chan_count : (k + 1) * chan_count, :] = (term * scale).astype(jnp.bfloat16)
+    term = contract_rows(
+        jnp.concatenate([ref[...] for ref in features], axis=0),
+        jnp.concatenate([ref[...] for ref in deltas], axis=0),
+    )
+    out_ref[taps * chan_count :, :] = (term * scale).astype(jnp.bfloat16)
 
 
 def per_device(
@@ -106,8 +135,7 @@
         inverse = lax.rsqrt(jnp.mean(values * values, axis=1, keepdims=True) + 1e-05)
         return values, inverse, (values * inverse).astype(jnp.bfloat16)
 
-    padded_values, padded_inverse, padded = normalise(padded_input)
-    input_values = padded_values[reach_rows : reach_rows + row_count]
+    _, padded_inverse, padded = normalise(padded_input)
     norm_inverse = padded_inverse[reach_rows : reach_rows + row_count]
 
     def tap_columns(field):
@@ -118,6 +146,8 @@
     columns = tap_columns(padded)
     preact = jnp.dot(columns, conv_weight, preferred_element_type=jnp.float32)
     hidden = jax.nn.gelu(preact, approximate=False).astype(jnp.bfloat16)
+    slope = gelu_slope(preact)
+    hidden, slope = lax.optimization_barrier((hidden, slope))
 
     row_ids = jnp.arange(row_count, dtype=jnp.int32).astype(jnp.float32)
     own_rows = jnp.concatenate(
@@ -158,25 +188,35 @@
     hidden_grad = hidden_cotangent[0].astype(jnp.float32) + jnp.dot(
         hits, row_grad, preferred_element_type=jnp.float32
     )
-    preact_grad = (hidden_grad * gelu_slope(preact)).astype(jnp.bfloat16)
+    preact_grad = (hidden_grad * slope).astype(jnp.bfloat16)
 
     grad_peers = dp_columns(preact_grad, col_width)
     grad_above, grad_below = seq_halo(preact_grad, reach_rows)
 
-    columns_all = jnp.concatenate(
-        [columns] + [tap_columns(normalise(peer)[2]) for peer in padded_peers[1:]], axis=0
-    )
-    conv_term = contract_rows(columns_all, jnp.concatenate(grad_peers, axis=0)) * (
-        1.0 / math.sqrt(dp_count * row_count * shards)
-    )
-    head_term = contract_rows(
-        jnp.concatenate(feature_peers, axis=0), jnp.concatenate(delta_peers, axis=0)
-    ) * (1.0 / math.sqrt(dp_count * pair_count * shards))
-    term = jnp.concatenate([conv_term.astype(jnp.bfloat16), head_term.astype(jnp.bfloat16)], axis=0)
+    normed_all = jnp.concatenate(
+        [padded] + [normalise(peer)[2] for peer in padded_peers[1:]], axis=0
+    ).T
+    term = pl.pallas_call(
+        functools.partial(
+            weight_kernel, 1.0 / math.sqrt(dp_count * row_count * shards), tap_count
+        ),
+        out_shape=jax.ShapeDtypeStruct(
+            (tap_count * chan_count + out_count, col_width), jnp.bfloat16
+        ),
+        in_specs=[pl.BlockSpec(memory_space=pltpu.VMEM)] * 13,
+        out_specs=pl.BlockSpec(memory_space=pltpu.VMEM),
+    )(normed_all, *grad_peers, *feature_peers, *delta_peers)
+    term, grad_above, grad_below, norm_inverse = lax.optimization_barrier(
+        (term, grad_above, grad_below, norm_inverse)
+    )
     share = term.shape[0] // shards
     terms = lax.all_to_all(
         term.reshape(shards, share, col_width), "seq", split_axis=0, concat_axis=0, tiled=True
     )
+    terms, grad_above, grad_below, late_input, norm_inverse = lax.optimization_barrier(
+        (terms, grad_above, grad_below, activations[0], norm_inverse)
+    )
+    input_values = late_input.astype(jnp.float32)
     weight_grads = jnp.sum(terms.astype(jnp.float32), axis=0)
 
     grad_padded = jnp.concatenate([grad_above, preact_grad, grad_below], axis=0)
@@ -211,6 +251,7 @@
         P("dp", "seq", None),
         P("dp", "seq"),
     )
+
     return jax.shard_map(
         per_device,
         mesh=mesh,

time: 177 us -> 198 us (1.12)
  the two profiles are of different devices: /device:TPU:24 before, /device:TPU:32 now
where the time goes in v2:
time: 198 us
  blocking collectives  69.8 us (35%)
  starting transfers between devices  51.1 us (26%)
  waiting for transfers between devices  26.1 us (13%)
  matrix products  19.6 us (10%)
  other arithmetic  14.3 us (7%)
  local copies, waits for them, and re-layouts  10.6 us (5%)
  Pallas kernels  4.93 us (2%)
    all_to_all x1, blocking collectives, per_device(): lax.all_to_all(term.reshape(shards, share, col_width), 'seq', split_axis=...  69.8 us
    all_to_all x1, waiting for transfers between devices, per_device(): lax.all_to_all(sent.reshape(shards, 2 * capacity, out_count), 'seq', spli...  21 us
    all_to_all x1, starting transfers between devices, per_device(): lax.all_to_all(sent.reshape(shards, 2 * capacity, out_count), 'seq', spli...  19.4 us
    all_to_all x1, starting transfers between devices, per_device(): asked = lax.all_to_all(ask, 'seq', split_axis=0, concat_axis=0, tiled=True)  13.7 us
    ppermute x2, starting transfers between devices, seq_halo(): lax.ppermute(cells[-width:], 'seq', [(i, i + 1) for i in range(count - 1)])  8.64 us
    dot_general x1, matrix products, per_device(): preact = jnp.dot(columns, conv_weight, preferred_element_type=jnp.float32)  5.38 us
    unnamed x28, local copies, waits for them, and re-layouts  5.29 us
    all_to_all x1, waiting for transfers between devices, per_device(): asked = lax.all_to_all(ask, 'seq', split_axis=0, concat_axis=0, tiled=True)  5.04 us
  transfers between devices with their start and end apart: 18, of which 3 were waited for; matrix products, arithmetic and copies ran while one was open for 13% of the time, Pallas kernels for 2%

profile of v2, /device:TPU:32, one launch (start us, length us, event | category | flops | bytes accessed | tf_op | source)
XLA Modules:
  0.0 197.6 jit_solution(10925688261223966008)
XLA Ops:
  4.7 13.7 %all-to-all-start = ((f32[64,1,8]{2,1,0:T(1,128)}), f32[64,1,8]{2,1,0:T(1,128)S(1)}, u32[]{:S(2)}, u32[]{:S(2)}) async-start(f32[64,1,8]{2,1,0:T(1,128)} %bitcast.10), calls=%async_computation | async-start | bytes 65536 | tf_op jit(solution)/shard_map/all_to_all | solution.py:128
  19.6 3.5 %collective-permute-start = (bf16[16,768]{0,1:T(8,128)(2,1)S(1)}, bf16[16,768]{0,1:T(8,128)(2,1)S(1)}, u32[]{:S(2)}, u32[]{:S(2)}) collective-permute-start(bf16[16,768]{0,1:T(8,128)(2,1)S(1)} %get-tuple-element.53), channel_id=1, source_target_pairs={{0,1},{1,2},{2,3},{3,4},{4,5},{5,6},{6,7},{7,8},{8,9},{9,10},{10,1... | collective-permute-start | bytes 73736 | tf_op jit(solution)/shard_map/ppermute | solution.py:29
  23.0 1.3 collective-permute-start.1
  25.2 5.0 %all-to-all-done = f32[64,1,8]{2,1,0:T(1,128)S(1)} async-done(((f32[64,1,8]{2,1,0:T(1,128)}), f32[64,1,8]{2,1,0:T(1,128)S(1)}, u32[]{:S(2)}, u32[]{:S(2)}) %all-to-all-start) | async-done | bytes 2080 | tf_op jit(solution)/shard_map/all_to_all | solution.py:128
  31.0 1.1 collective-permute-start.3
  32.9 5.4 %fusion.30 = (f32[128,768]{1,0:T(8,128)}, bf16[128,768]{1,0:T(8,128)(2,1)S(1)}) fusion(bf16[128,3840]{0,1:T(8,128)(2,1)S(1)} %slice_dynamic-update-slice_fusion, bf16[3840,768]{1,0:T(8,128)(2,1)} %param.10), kind=kOutput, calls=%fused_computation.51 | convolution fusion | flops 762150912 | bytes 7471104 | tf_op jit(solution)/shard_map/dot_general | solution.py:147
  38.3 1.4 convolution_convert_fusion
  39.7 19.4 %all-to-all-start.1 = ((bf16[64,8,768]{2,1,0:T(8,128)(2,1)}), bf16[64,8,768]{2,1,0:T(8,128)(2,1)S(1)}, u32[]{:S(2)}, u32[]{:S(2)}) async-start(bf16[64,8,768]{2,1,0:T(8,128)(2,1)} %bitcast.12), calls=%async_computation.1 | async-start | bytes 1572864 | tf_op jit(solution)/shard_map/all_to_all | solution.py:161
  59.5 1.1 fusion.16
  64.5 21.0 %all-to-all-done.1 = bf16[64,8,768]{2,1,0:T(8,128)(2,1)S(1)} async-done(((bf16[64,8,768]{2,1,0:T(8,128)(2,1)}), bf16[64,8,768]{2,1,0:T(8,128)(2,1)S(1)}, u32[]{:S(2)}, u32[]{:S(2)}) %all-to-all-start.1) | async-done | bytes 786464 | tf_op jit(solution)/shard_map/all_to_all | solution.py:161
  86.5 1.6 fusion.54
  89.1 1.9 convolution_convert_fusion.2.refs_5_
  91.0 1.2 collective-permute-start.9
  92.2 2.7 %fusion.7 = bf16[512,768]{1,0:T(8,128)(2,1)S(1)} fusion(f32[768]{0:T(1024)S(1)} %convert_element_type.118, f32[512]{0:T(512)S(1)} %mul.205, bf16[768,768]{1,0:T(8,128)(2,1)S(1)} %copy-done, bf16[512,768]{1,0:T(8,128)(2,1)} %convolution_convert_fusion, bf16[64,4,768]{2,1,0:T(4,128)(2,1)} %copy-done.4, bf16[64,4,768]{2,1,0:T(4,128)(2,1)S(1)} %copy-done.3), kind=kOutput, calls=%fused_computation.11 | convolution fusion | flops 611450880 | bytes 3544064 | tf_op jit(solution)/shard_map/dot_general | solution.py:179
  96.7 1.2 convolution_convert_fusion.1
  99.8 1.2 collective-permute-start.12
  101.0 2.6 %fusion.11 = bf16[128,768]{1,0:T(8,128)(2,1)S(1)} fusion(f32[128,768]{1,0:T(8,128)} %get-tuple-element.14, bf16[512,768]{1,0:T(8,128)(2,1)} %copy-done.7, bf16[768,768]{1,0:T(8,128)(2,1)S(1)} %copy-done, bf16[64,4,768]{2,1,0:T(4,128)(2,1)} %copy-done.4, bf16[64,4,768]{2,1,0:T(4,128)(2,1)S(1)} %copy-done.3, bf16[1,128,768]{2,1,0:T(8,128)(2,1)} %param.13, ...), kind=kOutput, calls=%fused_computation.16 | convolution fusion | flops 707854336 | bytes 3541504 | tf_op jit(solution)/shard_map/dot_general | solution.py:188
  105.2 1.2 collective-permute-start.6
  107.1 1.3 collective-permute-start.15
  108.4 5.2 %collective-permute-start.14 = (bf16[16,768]{1,0:T(8,128)(2,1)}, bf16[16,768]{1,0:T(8,128)(2,1)}, u32[]{:S(2)}, u32[]{:S(2)}) collective-permute-start(bf16[16,768]{1,0:T(8,128)(2,1)} %get-tuple-element.44), channel_id=1, source_target_pairs={{0,1},{1,2},{2,3},{3,4},{4,5},{5,6},{6,7},{7,8},{8,9},{9,10},{10,1... | collective-permute-start | bytes 73736 | tf_op jit(solution)/shard_map/ppermute | solution.py:29
  113.5 1.6 maximum_bitcast_fusion.refs_0_
  115.9 4.9 %shard_map.104 = bf16[4608,192]{1,0:T(8,128)(2,1)} custom-call(bf16[768,640]{1,0:T(8,128)(2,1)} %maximum_bitcast_fusion.refs_0_, bf16[128,192]{1,0:T(8,128)(2,1)} %get-tuple-element.52.refs_1_, bf16[128,192]{1,0:T(8,128)(2,1)} %copy-done.10, bf16[128,192]{1,0:T(8,128)(2,1)} %copy-done.9, bf16[128,192]{1,0:T(8,128)(2,1)} %copy-done.8, ...), custom_call_target="tpu_custom_call" | custom-call | tf_op jit(solution)/shard_map/pallas_call | solution.py:199
  120.9 69.8 %all_to_all.22 = bf16[64,72,192]{2,1,0:T(8,128)(2,1)S(1)} all-to-all(bf16[64,72,192]{2,1,0:T(8,128)(2,1)} %bitcast.55), channel_id=1, replica_groups=mesh['dp'=4,'seq'=64] {'seq'}, dimensions={0} | all-to-all | bytes 3538944 | tf_op jit(solution)/shard_map/all_to_all | solution.py:213
  191.7 4.4 %fusion.40 = f32[160,3840]{0,1:T(8,128)S(1)} fusion(bf16[3840,768]{1,0:T(8,128)(2,1)} %param.10, bf16[16,768]{1,0:T(8,128)(2,1)} %collective-permute-done.15, bf16[128,768]{1,0:T(8,128)(2,1)S(1)} %fusion.11, bf16[16,768]{1,0:T(8,128)(2,1)} %collective-permute-done.14), kind=kOutput, calls=%fused_computation.74 | convolution fusion | flops 944455680 | bytes 8601600 | tf_op jit(solution)/shard_map/dot_general | solution.py:223
  (96 shorter events, 22.8 us)
Async XLA Ops:
  0.6 91.6 %copy-start = (bf16[768,768]{1,0:T(8,128)(2,1)S(1)}, bf16[768,768]{1,0:T(8,128)(2,1)}, u32[]{:S(2)}) copy-start(bf16[768,768]{1,0:T(8,128)(2,1)} %param.11) | copy-start | bytes 3538948
  4.7 25.6 %all-to-all-start = ((f32[64,1,8]{2,1,0:T(1,128)}), f32[64,1,8]{2,1,0:T(1,128)S(1)}, u32[]{:S(2)}, u32[]{:S(2)}) async-start(f32[64,1,8]{2,1,0:T(1,128)} %bitcast.10), calls=%async_computation | async-start | bytes 65536 | tf_op jit(solution)/shard_map/all_to_all | solution.py:128
  19.6 11.1 %collective-permute-start = (bf16[16,768]{0,1:T(8,128)(2,1)S(1)}, bf16[16,768]{0,1:T(8,128)(2,1)S(1)}, u32[]{:S(2)}, u32[]{:S(2)}) collective-permute-start(bf16[16,768]{0,1:T(8,128)(2,1)S(1)} %get-tuple-element.53), channel_id=1, source_target_pairs={{0,1},{1,2},{2,3},{3,4},{4,5},{5,6},{6,7},{7,8},{8,9},{9,10},{10,1... | collective-permute-start | bytes 73736 | tf_op jit(solution)/shard_map/ppermute | solution.py:29
  23.0 7.7 %collective-permute-start.1 = (bf16[16,768]{0,1:T(8,128)(2,1)S(1)}, bf16[16,768]{0,1:T(8,128)(2,1)S(1)}, u32[]{:S(2)}, u32[]{:S(2)}) collective-permute-start(bf16[16,768]{0,1:T(8,128)(2,1)S(1)} %get-tuple-element.54), channel_id=1, source_target_pairs={{1,0},{2,1},{3,2},{4,3},{5,4},{6,5},{7,6},{8,7},{9,8},{10,9},{11,1... | collective-permute-start | bytes 73736 | tf_op jit(solution)/shard_map/ppermute | solution.py:30
  31.0 28.1 %collective-permute-start.3 = (bf16[160,768]{0,1:T(8,128)(2,1)S(1)}, bf16[160,768]{0,1:T(8,128)(2,1)}, u32[]{:S(2)}, u32[]{:S(2)}) collective-permute-start(bf16[160,768]{0,1:T(8,128)(2,1)S(1)} %get-tuple-element.38), channel_id=1, source_target_pairs={{0,128},{64,192},{128,0},{192,64},{1,129},{65,193},{129,1},{193,65... | collective-permute-start | bytes 737288 | tf_op jit(solution)/shard_map/ppermute | solution.py:39
  32.1 28.5 %collective-permute-start.2 = (bf16[160,768]{0,1:T(8,128)(2,1)S(1)}, bf16[160,768]{0,1:T(8,128)(2,1)S(1)}, u32[]{:S(2)}, u32[]{:S(2)}) collective-permute-start(bf16[160,768]{0,1:T(8,128)(2,1)S(1)} %get-tuple-element.38), channel_id=1, source_target_pairs={{0,64},{64,0},{128,192},{192,128},{1,65},{65,1},{129,193},{193,129... | collective-permute-start | bytes 737288 | tf_op jit(solution)/shard_map/ppermute | solution.py:35
  39.7 45.7 %all-to-all-start.1 = ((bf16[64,8,768]{2,1,0:T(8,128)(2,1)}), bf16[64,8,768]{2,1,0:T(8,128)(2,1)S(1)}, u32[]{:S(2)}, u32[]{:S(2)}) async-start(bf16[64,8,768]{2,1,0:T(8,128)(2,1)} %bitcast.12), calls=%async_computation.1 | async-start | bytes 1572864 | tf_op jit(solution)/shard_map/all_to_all | solution.py:161
  59.1 4.4 %collective-permute-start.4 = (bf16[160,768]{0,1:T(8,128)(2,1)}, bf16[160,768]{0,1:T(8,128)(2,1)S(1)}, u32[]{:S(2)}, u32[]{:S(2)}) collective-permute-start(bf16[160,768]{0,1:T(8,128)(2,1)} %collective-permute-done.3), channel_id=1, source_target_pairs={{0,64},{64,0},{128,192},{192,128},{1,65},{65,1},{129,193},{193,129... | collective-permute-start | bytes 737288 | tf_op jit(solution)/shard_map/ppermute | solution.py:35
  85.7 2.4 %copy-start.4 = (bf16[64,4,768]{2,1,0:T(4,128)(2,1)}, bf16[64,4,768]{2,1,0:T(4,128)(2,1)S(1)}, u32[]{:S(2)}) copy-start(bf16[64,4,768]{2,1,0:T(4,128)(2,1)S(1)} %get-tuple-element.40) | copy-start | bytes 1179652
  88.1 4.1 %copy-start.3 = (bf16[64,4,768]{2,1,0:T(4,128)(2,1)S(1)}, bf16[64,4,768]{2,1,0:T(4,128)(2,1)}, u32[]{:S(2)}) copy-start(bf16[64,4,768]{2,1,0:T(4,128)(2,1)} %copy-done.2) | copy-start | bytes 1179652
  91.0 15.5 %collective-permute-start.9 = (bf16[128,768]{1,0:T(8,128)(2,1)}, bf16[128,768]{1,0:T(8,128)(2,1)}, u32[]{:S(2)}, u32[]{:S(2)}) collective-permute-start(bf16[128,768]{1,0:T(8,128)(2,1)} %convolution_convert_fusion.2.refs_5_), channel_id=1, source_target_pairs={{0,128},{64,192},{128,0},{192,64},{1,129},{65,193},{129,1},{193,65... | collective-permute-start | bytes 589832 | tf_op jit(solution)/shard_map/ppermute | solution.py:39
  92.2 23.0 %collective-permute-start.8 = (bf16[128,768]{1,0:T(8,128)(2,1)}, bf16[128,768]{1,0:T(8,128)(2,1)}, u32[]{:S(2)}, u32[]{:S(2)}) collective-permute-start(bf16[128,768]{1,0:T(8,128)(2,1)} %convolution_convert_fusion.2.refs_5_), channel_id=1, source_target_pairs={{0,64},{64,0},{128,192},{192,128},{1,65},{65,1},{129,193},{193,129... | collective-permute-start | bytes 589832 | tf_op jit(solution)/shard_map/ppermute | solution.py:35
  98.8 5.5 %collective-permute-start.13 = (bf16[128,192]{1,0:T(8,128)(2,1)}, bf16[128,192]{1,0:T(8,128)(2,1)}, u32[]{:S(2)}, u32[]{:S(2)}) collective-permute-start(bf16[128,192]{1,0:T(8,128)(2,1)} %get-tuple-element.45), channel_id=1, source_target_pairs={{0,192},{64,128},{128,64},{192,0},{1,193},{65,129},{129,65},{193,1... | collective-permute-start | bytes 147464 | tf_op jit(solution)/shard_map/ppermute | solution.py:54
  99.8 5.5 %collective-permute-start.12 = (bf16[128,192]{1,0:T(8,128)(2,1)}, bf16[128,192]{1,0:T(8,128)(2,1)}, u32[]{:S(2)}, u32[]{:S(2)}) collective-permute-start(bf16[128,192]{1,0:T(8,128)(2,1)} %get-tuple-element.46), channel_id=1, source_target_pairs={{0,128},{64,192},{128,0},{192,64},{1,129},{65,193},{129,1},{193,65... | collective-permute-start | bytes 147464 | tf_op jit(solution)/shard_map/ppermute | solution.py:54
  101.0 12.6 %copy-start.1 = (bf16[160,768]{0,1:T(8,128)(2,1)S(1)}, bf16[160,768]{0,1:T(8,128)(2,1)}, u32[]{:S(2)}) copy-start(bf16[160,768]{0,1:T(8,128)(2,1)} %fusion.19) | copy-start | bytes 737284
  101.0 6.1 %collective-permute-start.11 = (bf16[128,192]{1,0:T(8,128)(2,1)}, bf16[128,192]{1,0:T(8,128)(2,1)}, u32[]{:S(2)}, u32[]{:S(2)}) collective-permute-start(bf16[128,192]{1,0:T(8,128)(2,1)} %get-tuple-element.47), channel_id=1, source_target_pairs={{0,64},{64,0},{128,192},{192,128},{1,65},{65,1},{129,193},{193,129... | collective-permute-start | bytes 147464 | tf_op jit(solution)/shard_map/ppermute | solution.py:54
  104.4 4.0 %collective-permute-start.7 = (bf16[128,192]{1,0:T(8,128)(2,1)S(1)}, bf16[128,192]{1,0:T(8,128)(2,1)S(1)}, u32[]{:S(2)}, u32[]{:S(2)}) collective-permute-start(bf16[128,192]{1,0:T(8,128)(2,1)S(1)} %get-tuple-element.49), channel_id=1, source_target_pairs={{0,192},{64,128},{128,64},{192,0},{1,193},{65,129},{129,65},{193,1... | collective-permute-start | bytes 147464 | tf_op jit(solution)/shard_map/ppermute | solution.py:54
  105.2 8.3 %collective-permute-start.6 = (bf16[128,192]{1,0:T(8,128)(2,1)S(1)}, bf16[128,192]{1,0:T(8,128)(2,1)S(1)}, u32[]{:S(2)}, u32[]{:S(2)}) collective-permute-start(bf16[128,192]{1,0:T(8,128)(2,1)S(1)} %get-tuple-element.50), channel_id=1, source_target_pairs={{0,128},{64,192},{128,0},{192,64},{1,129},{65,193},{129,1},{193,65... | collective-permute-start | bytes 147464 | tf_op jit(solution)/shard_map/ppermute | solution.py:54
  106.4 8.8 %collective-permute-start.10 = (bf16[128,768]{1,0:T(8,128)(2,1)}, bf16[128,768]{1,0:T(8,128)(2,1)S(1)}, u32[]{:S(2)}, u32[]{:S(2)}) collective-permute-start(bf16[128,768]{1,0:T(8,128)(2,1)} %collective-permute-done.9.refs_7_), channel_id=1, source_target_pairs={{0,64},{64,0},{128,192},{192,128},{1,65},{65,1},{129,193},{193,129... | collective-permute-start | bytes 589832 | tf_op jit(solution)/shard_map/ppermute | solution.py:35
  107.1 13.8 %collective-permute-start.15 = (bf16[16,768]{1,0:T(8,128)(2,1)}, bf16[16,768]{1,0:T(8,128)(2,1)}, u32[]{:S(2)}, u32[]{:S(2)}) collective-permute-start(bf16[16,768]{1,0:T(8,128)(2,1)} %get-tuple-element.43), channel_id=1, source_target_pairs={{1,0},{2,1},{3,2},{4,3},{5,4},{6,5},{7,6},{8,7},{9,8},{10,9},{11,1... | collective-permute-start | bytes 73736 | tf_op jit(solution)/shard_map/ppermute | solution.py:30
  108.4 6.9 %copy-start.8 = (bf16[128,192]{1,0:T(8,128)(2,1)}, bf16[128,192]{1,0:T(8,128)(2,1)S(1)}, u32[]{:S(2)}) copy-start(bf16[128,192]{1,0:T(8,128)(2,1)S(1)} %collective-permute-done.7.refs_4_) | copy-start | bytes 147460
  108.4 12.5 %collective-permute-start.14 = (bf16[16,768]{1,0:T(8,128)(2,1)}, bf16[16,768]{1,0:T(8,128)(2,1)}, u32[]{:S(2)}, u32[]{:S(2)}) collective-permute-start(bf16[16,768]{1,0:T(8,128)(2,1)} %get-tuple-element.44), channel_id=1, source_target_pairs={{0,1},{1,2},{2,3},{3,4},{4,5},{5,6},{6,7},{7,8},{8,9},{9,10},{10,1... | collective-permute-start | bytes 73736 | tf_op jit(solution)/shard_map/ppermute | solution.py:29
  113.5 1.7 copy-start.9
  113.5 1.7 collective-permute-start.5
  (5 other events, 3.7 us)

commit v3 on v2

--- a/solution.py
+++ b/solution.py
@@ -10,6 +10,8 @@
 
 
 DILATION = 8
+LANES = 128
+KERNEL_VMEM = 16 * 1024 * 1024
 
 
 def gelu_slope(values):
@@ -56,9 +58,40 @@
     return found
 
 
+def pair_kernel(got_ref, hidden_ref, first_ref, second_ref, cotangent_ref, *outs):
+    back_ref, part_ref, feature_ref, delta_ref = outs
+    chan_count = hidden_ref.shape[1]
+    slots = got_ref.shape[0]
+    note = got_ref[:, chan_count:].astype(jnp.float32)
+    score = note[:, 1:2] + note[:, 2:3] + note[:, 3:4]
+    row_ids = lax.broadcasted_iota(jnp.int32, (slots, hidden_ref.shape[0]), 1).astype(jnp.float32)
+    hits = (note[:, 0:1] == row_ids).astype(jnp.float32).astype(jnp.bfloat16)
+    accept = jnp.dot(hits, hidden_ref[...], preferred_element_type=jnp.float32)
+    donor = got_ref[:, :chan_count].astype(jnp.float32)
+    feature = (donor * accept).astype(jnp.bfloat16)
+    feature_ref[...] = feature
+    head_preact = jnp.dot(feature, first_ref[...], preferred_element_type=jnp.float32)
+    delta = (score * second_ref[...].astype(jnp.float32) * gelu_slope(head_preact)).astype(
+        jnp.bfloat16
+    )
+    delta_ref[...] = delta
+    feature_grad = lax.dot_general(
+        delta, first_ref[...], (((1,), (1,)), ((), ())), preferred_element_type=jnp.float32
+    )
+    back_ref[...] = (feature_grad * accept).astype(jnp.bfloat16)
+    accept_grad = (feature_grad * donor).astype(jnp.bfloat16)
+    part_ref[...] = cotangent_ref[...].astype(jnp.float32) + contract_rows(hits, accept_grad)
+
+
+def head_kernel(scale, *refs):
+    term = contract_rows(refs[0][...], refs[4][...])
+    for feature, delta in zip(refs[1:4], refs[5:8], strict=True):
+        term = term + contract_rows(feature[...], delta[...])
+    refs[8][...] = (term * scale).astype(jnp.bfloat16)
+
+
 def weight_kernel(scale, taps, *refs):
-    normed_ref, out_ref = refs[0], refs[-1]
-    grads, features, deltas = refs[1:5], refs[5:9], refs[9:13]
+    normed_ref, head_ref, grads, out_ref = refs[0], refs[1], refs[2:6], refs[6]
     chan_count = normed_ref.shape[0]
     width = grads[0].shape[1]
     reach = (taps - 1) * DILATION
@@ -74,11 +107,18 @@
         shifted = jnp.concatenate(pieces, axis=0).astype(jnp.bfloat16)
         term = jnp.dot(normed_ref[...], shifted, preferred_element_type=jnp.float32)
         out_ref[k * chan_count : (k + 1) * chan_count, :] = (term * scale).astype(jnp.bfloat16)
-    term = contract_rows(
-        jnp.concatenate([ref[...] for ref in features], axis=0),
-        jnp.concatenate([ref[...] for ref in deltas], axis=0),
-    )
-    out_ref[taps * chan_count :, :] = (term * scale).astype(jnp.bfloat16)
+    out_ref[taps * chan_count :, :] = head_ref[...]
+
+
+def in_vmem(kernel, shapes, count, limit):
+    spec = pl.BlockSpec(memory_space=pltpu.VMEM)
+    return pl.pallas_call(
+        kernel,
+        out_shape=shapes,
+        in_specs=[spec] * count,
+        out_specs=jax.tree.map(lambda _: spec, shapes),
+        compiler_params=pltpu.CompilerParams(vmem_limit_bytes=limit),
+    )
 
 
 def per_device(
@@ -114,18 +154,22 @@
         axis=1,
     )
     target = owner * capacity + rank
-    placed = target[:, None] == jnp.arange(slots, dtype=jnp.int32)[None, :]
-
-    def to_slots(values, empty):
-        return jnp.sum(jnp.where(placed, (values - empty)[:, None], 0.0), axis=0) + empty
-
-    score_slot = jnp.sum(jnp.where(placed, score_cotangent[0][:, None], 0.0), axis=0)
-    accept_slot = to_slots(acceptor_row[0].astype(jnp.float32), -1.0)
-    donor_slot = to_slots(donor_row[0].astype(jnp.float32), -1.0)
-    ask = jnp.concatenate(
-        [accept_slot.reshape(shards, capacity), score_slot.reshape(shards, capacity)], axis=1
-    )
-    asked = lax.all_to_all(ask, "seq", split_axis=0, concat_axis=0, tiled=True)
+    placed = target[None, :] == jnp.arange(slots, dtype=jnp.int32)[:, None]
+    score = score_cotangent[0]
+    high = lax.reduce_precision(score, 8, 7)
+    middle = lax.reduce_precision(score - high, 8, 7)
+    note = jnp.stack([acceptor_row[0].astype(jnp.float32) + 1.0, high, middle, score - high - middle])
+    note = jnp.pad(note, ((0, LANES - note.shape[0]), (0, 0))).astype(jnp.bfloat16)
+    notes = lax.dot_general(
+        placed.astype(jnp.bfloat16), note, (((1,), (1,)), ((), ())), preferred_element_type=jnp.float32
+    )
+    notes = (notes - (jnp.arange(LANES) == 0).astype(jnp.float32)[None, :]).astype(jnp.bfloat16)
+    donor_slot = (
+        jnp.sum(jnp.where(placed, donor_row[0][None, :] + 1, 0), axis=1, dtype=jnp.int32) - 1
+    )
+    row_ids = jnp.arange(row_count, dtype=jnp.int32)
+    hits = (donor_slot[:, None] == row_ids[None, :]).astype(jnp.bfloat16)
+    hits, notes = lax.optimization_barrier((hits, notes))
 
     padded_input = jnp.concatenate([above, activations[0], below], axis=0)
     padded_peers = dp_peers(padded_input)
@@ -149,45 +193,44 @@
     slope = gelu_slope(preact)
     hidden, slope = lax.optimization_barrier((hidden, slope))
 
-    row_ids = jnp.arange(row_count, dtype=jnp.int32).astype(jnp.float32)
-    own_rows = jnp.concatenate(
-        [donor_slot.reshape(shards, capacity), asked[:, :capacity]], axis=1
-    ).reshape(2 * slots)
-    own_scores = jnp.concatenate(
-        [score_slot.reshape(shards, capacity), asked[:, capacity:]], axis=1
-    ).reshape(2 * slots)
-    hits = (row_ids[:, None] == own_rows[None, :]).astype(jnp.bfloat16)
-    sent = contract_rows(hits, hidden).astype(jnp.bfloat16)
+    sent = jnp.concatenate(
+        [jnp.dot(hits, hidden, preferred_element_type=jnp.float32).astype(jnp.bfloat16), notes], axis=1
+    )
     got = lax.all_to_all(
-        sent.reshape(shards, 2 * capacity, out_count), "seq", split_axis=0, concat_axis=0, tiled=True
-    )
-    partner = jnp.concatenate([got[:, capacity:], got[:, :capacity]], axis=1).reshape(
-        2 * slots, out_count
-    )
-    partner_values = partner.astype(jnp.float32)
-    pair_feature = (sent.astype(jnp.float32) * partner_values).astype(jnp.bfloat16)
-
-    def own_pairs(field):
-        halves = field.reshape(shards, 2 * capacity, out_count)[:, :capacity].reshape(
-            slots, out_count
-        )
-        return jnp.dot(placed.astype(jnp.bfloat16), halves, preferred_element_type=jnp.float32).astype(
-            jnp.bfloat16
-        )
-
-    feature_peers = dp_peers(own_pairs(pair_feature))
-    head_preact = jnp.dot(pair_feature, head_first, preferred_element_type=jnp.float32)
-    head_delta = (
-        own_scores[:, None] * head_second.astype(jnp.float32)[None, :] * gelu_slope(head_preact)
-    ).astype(jnp.bfloat16)
-    delta_peers = dp_columns(own_pairs(head_delta), col_width)
-    feature_grad = lax.dot_general(
-        head_delta, head_first, (((1,), (1,)), ((), ())), preferred_element_type=jnp.float32
-    )
-    row_grad = (feature_grad * partner_values).astype(jnp.bfloat16)
-    hidden_grad = hidden_cotangent[0].astype(jnp.float32) + jnp.dot(
-        hits, row_grad, preferred_element_type=jnp.float32
-    )
+        sent.reshape(shards, capacity, out_count + LANES),
+        "seq",
+        split_axis=0,
+        concat_axis=0,
+        tiled=True,
+    ).reshape(slots, out_count + LANES)
+    slot_shape = jax.ShapeDtypeStruct((slots, out_count), jnp.bfloat16)
+    back, part, feature, delta = in_vmem(
+        pair_kernel,
+        (
+            slot_shape,
+            jax.ShapeDtypeStruct((row_count, out_count), jnp.float32),
+            slot_shape,
+            slot_shape,
+        ),
+        5,
+        KERNEL_VMEM,
+    )(got, hidden, head_first, head_second.reshape(1, out_count), hidden_cotangent[0])
+    donor_grad = lax.all_to_all(
+        back.reshape(shards, capacity, out_count),
+        "seq",
+        split_axis=0,
+        concat_axis=0,
+        tiled=True,
+    ).reshape(slots, out_count)
+    feature_peers = dp_peers(feature)
+    delta_peers = dp_columns(delta, col_width)
+    head_term = in_vmem(
+        functools.partial(head_kernel, 1.0 / math.sqrt(dp_count * pair_count * shards)),
+        jax.ShapeDtypeStruct((out_count, col_width), jnp.bfloat16),
+        8,
+        KERNEL_VMEM,
+    )(*feature_peers, *delta_peers)
+    hidden_grad = part + contract_rows(hits, donor_grad)
     preact_grad = (hidden_grad * slope).astype(jnp.bfloat16)
 
     grad_peers = dp_columns(preact_grad, col_width)
@@ -196,16 +239,14 @@
     normed_all = jnp.concatenate(
         [padded] + [normalise(peer)[2] for peer in padded_peers[1:]], axis=0
     ).T
-    term = pl.pallas_call(
+    term = in_vmem(
         functools.partial(
             weight_kernel, 1.0 / math.sqrt(dp_count * row_count * shards), tap_count
         ),
-        out_shape=jax.ShapeDtypeStruct(
-            (tap_count * chan_count + out_count, col_width), jnp.bfloat16
-        ),
-        in_specs=[pl.BlockSpec(memory_space=pltpu.VMEM)] * 13,
-        out_specs=pl.BlockSpec(memory_space=pltpu.VMEM),
-    )(normed_all, *grad_peers, *feature_peers, *delta_peers)
+        jax.ShapeDtypeStruct((tap_count * chan_count + out_count, col_width), jnp.bfloat16),
+        6,
+        KERNEL_VMEM,
+    )(normed_all, head_term, *grad_peers)
     term, grad_above, grad_below, norm_inverse = lax.optimization_barrier(
         (term, grad_above, grad_below, norm_inverse)
     )

time: 198 us -> 186 us (0.939)
  matrix products: 19.6 us -> 9.39 us
  starting transfers between devices: 51.1 us -> 42.3 us
  blocking collectives: 69.8 us -> 75.4 us
  waiting for transfers between devices: 26.1 us -> 29.4 us
    all_to_all x2, waiting for transfers between devices: 26 us -> 16.4 us  [the longest x1 16.4 us: per_device(): lax.all_to_all(sent.reshape(shards, capacity, out_count + LANES), 'seq',...]
    ppermute x2, waiting for transfers between devices: 0.01 us -> 8.85 us  [swap_z(): return lax.ppermute(field, 'dp', [(0, 2), (1, 3), (2, 0), (3, 1)])]
    dot_general x4 -> x2, matrix products: 8.44 us -> 1.02 us  [the longest x1 0.78 us: per_device(): lax.dot_general(placed.astype(jnp.bfloat16), note, (((1,), (1,)), ((), ()...]
    all_to_all x2, starting transfers between devices: 33.1 us -> 27.1 us  [the longest x1 21.6 us: per_device(): lax.all_to_all(sent.reshape(shards, capacity, out_count + LANES), 'seq',...]
    all_to_all x1, blocking collectives: 69.8 us -> 75.4 us  [per_device(): lax.all_to_all(term.reshape(shards, share, col_width), 'seq', split_axis=...]
    dot_general x1, matrix products: 4.42 us -> 1.7 us  [per_device(): lax.dot_general(grad_padded, conv_weight, (((1,), (1,)), ((), ())), prefe...]
    convert_element_type x4, other arithmetic: 3.06 us -> 5.54 us  [normalise(): return (values, inverse, (values * inverse).astype(jnp.bfloat16))]
    ppermute x2, waiting for transfers between devices: 0.07 us -> 2.29 us  [seq_halo(): lax.ppermute(cells[:width], 'seq', [(i + 1, i) for i in range(count - 1)])]
  transfers between devices with their start and end apart: 18 -> 18, of which waited for: 3 -> 5; matrix products, arithmetic and copies ran while one was open for 13% -> 14% of each run, Pallas kernels for 2% -> 2%
where the time goes in v3:
time: 186 us; the launch traced here: 185 us
  blocking collectives  75.4 us (41%)
  starting transfers between devices  42.3 us (23%)
  waiting for transfers between devices  29.4 us (16%)
  other arithmetic  15.2 us (8%)
  matrix products  9.39 us (5%)
  local copies, waits for them, and re-layouts  8.71 us (5%)
  Pallas kernels  3.68 us (2%)
    all_to_all x1, blocking collectives, per_device(): lax.all_to_all(term.reshape(shards, share, col_width), 'seq', split_axis=...  75.4 us
    all_to_all x1, starting transfers between devices, per_device(): lax.all_to_all(sent.reshape(shards, capacity, out_count + LANES), 'seq',...  21.6 us
    all_to_all x1, waiting for transfers between devices, per_device(): lax.all_to_all(sent.reshape(shards, capacity, out_count + LANES), 'seq',...  16.4 us
    ppermute x2, waiting for transfers between devices, swap_z(): return lax.ppermute(field, 'dp', [(0, 2), (1, 3), (2, 0), (3, 1)])  8.85 us
    ppermute x2, starting transfers between devices, seq_halo(): lax.ppermute(cells[-width:], 'seq', [(i, i + 1) for i in range(count - 1)])  7.3 us
    convert_element_type x4, other arithmetic, normalise(): return (values, inverse, (values * inverse).astype(jnp.bfloat16))  5.54 us
    all_to_all x1, starting transfers between devices, per_device(): lax.all_to_all(back.reshape(shards, capacity, out_count), 'seq', split_ax...  5.45 us
    dot_general x1, matrix products, per_device(): preact = jnp.dot(columns, conv_weight, preferred_element_type=jnp.float32)  5.4 us
  transfers between devices with their start and end apart: 18, of which 5 were waited for; matrix products, arithmetic and copies ran while one was open for 14% of the time, Pallas kernels for 2%

profile of v3, /device:TPU:32, one launch (start us, length us, event | category | flops | bytes accessed | tf_op | source)
XLA Modules:
  0.0 185.0 jit_solution(813868636238520171)
XLA Ops:
  1.9 3.4 %collective-permute-start = (bf16[16,768]{0,1:T(8,128)(2,1)S(1)}, bf16[16,768]{0,1:T(8,128)(2,1)S(1)}, u32[]{:S(2)}, u32[]{:S(2)}) collective-permute-start(bf16[16,768]{0,1:T(8,128)(2,1)S(1)} %get-tuple-element.56), channel_id=1, source_target_pairs={{0,1},{1,2},{2,3},{3,4},{4,5},{5,6},{6,7},{7,8},{8,9},{9,10},{10,1... | collective-permute-start | bytes 73736 | tf_op jit(solution)/shard_map/ppermute | solution.py:31
  5.3 1.3 collective-permute-start.1
  11.2 2.3 %collective-permute-done.1 = bf16[16,768]{0,1:T(8,128)(2,1)S(1)} collective-permute-done((bf16[16,768]{0,1:T(8,128)(2,1)S(1)}, bf16[16,768]{0,1:T(8,128)(2,1)S(1)}, u32[]{:S(2)}, u32[]{:S(2)}) %collective-permute-start.1) | collective-permute-done | bytes 24608 | tf_op jit(solution)/shard_map/ppermute | solution.py:32
  15.0 5.4 %fusion.21 = (f32[128,768]{1,0:T(8,128)}, bf16[128,768]{1,0:T(8,128)(2,1)S(1)}) fusion(bf16[128,3840]{0,1:T(8,128)(2,1)S(1)} %slice_dynamic-update-slice_fusion, bf16[3840,768]{1,0:T(8,128)(2,1)} %param.10), kind=kOutput, calls=%fused_computation.39 | convolution fusion | flops 762150912 | bytes 7471104 | tf_op jit(solution)/shard_map/dot_general | solution.py:191
  21.7 21.6 %all-to-all-start = ((bf16[64,4,896]{2,1,0:T(4,128)(2,1)}), bf16[64,4,896]{2,1,0:T(4,128)(2,1)S(1)}, u32[]{:S(2)}, u32[]{:S(2)}) async-start(bf16[64,4,896]{2,1,0:T(4,128)(2,1)} %reshape.92), calls=%async_computation | async-start | bytes 917504 | tf_op jit(solution)/shard_map/all_to_all | solution.py:199
  43.7 1.1 fusion.7
  44.9 1.8 fusion.8
  46.8 16.4 %all-to-all-done = bf16[64,4,896]{2,1,0:T(4,128)(2,1)S(1)} async-done(((bf16[64,4,896]{2,1,0:T(4,128)(2,1)}), bf16[64,4,896]{2,1,0:T(4,128)(2,1)S(1)}, u32[]{:S(2)}, u32[]{:S(2)}) %all-to-all-start) | async-done | bytes 458784 | tf_op jit(solution)/shard_map/all_to_all | solution.py:199
  64.2 1.4 shard_map.104
  66.4 5.5 %all-to-all-start.1 = ((bf16[64,4,768]{2,1,0:T(4,128)(2,1)}), bf16[64,4,768]{2,1,0:T(4,128)(2,1)}, u32[]{:S(2)}, u32[]{:S(2)}) async-start(bf16[64,4,768]{2,1,0:T(4,128)(2,1)} %reshape.95), calls=%async_computation.1 | async-start | bytes 786432 | tf_op jit(solution)/shard_map/all_to_all | solution.py:218
  71.9 1.8 fusion.6
  73.7 1.1 fusion.9
  75.5 1.8 fusion.10
  78.4 1.5 collective-permute-start.10
  80.5 8.8 %collective-permute-done.6.refs_2_ = bf16[256,768]{1,0:T(8,128)(2,1)S(1)} collective-permute-done((bf16[256,768]{1,0:T(8,128)(2,1)S(1)}, bf16[256,768]{1,0:T(8,128)(2,1)S(1)}, u32[]{:S(2)}, u32[]{:S(2)}) %collective-permute-start.6) | collective-permute-done | bytes 393248 | tf_op jit(solution)/shard_map/ppermute | solution.py:41
  89.4 1.1 reshape.96
  90.4 1.3 fusion.1
  91.9 1.3 collective-permute-start.15
  93.9 3.9 %collective-permute-start.14 = (bf16[16,768]{1,0:T(8,128)(2,1)S(1)}, bf16[16,768]{1,0:T(8,128)(2,1)S(1)}, u32[]{:S(2)}, u32[]{:S(2)}) collective-permute-start(bf16[16,768]{1,0:T(8,128)(2,1)S(1)} %get-tuple-element.51), channel_id=1, source_target_pairs={{0,1},{1,2},{2,3},{3,4},{4,5},{5,6},{6,7},{7,8},{8,9},{9,10},{10,1... | collective-permute-start | bytes 73736 | tf_op jit(solution)/shard_map/ppermute | solution.py:31
  99.8 2.1 %maximum_bitcast_fusion.refs_0_ = bf16[768,640]{1,0:T(8,128)(2,1)S(1)} fusion(bf16[160,768]{0,1:T(8,128)(2,1)} %fusion.10, bf16[160,768]{0,1:T(8,128)(2,1)} %fusion.8, bf16[160,768]{0,1:T(8,128)(2,1)} %fusion.6, bf16[160,768]{0,1:T(8,128)(2,1)S(1)} %copy-done.3), kind=kLoop, calls=%fused_computation.7 | loop fusion | flops 3932160 | bytes 1966080 | tf_op jit(solution)/shard_map/transpose | solution.py:241
  102.5 1.2 collective-permute-done.12.refs_4_
  103.7 1.7 shard_map.106
  105.4 75.4 %all_to_all.15 = bf16[64,72,192]{2,1,0:T(8,128)(2,1)S(1)} all-to-all(bf16[64,72,192]{2,1,0:T(8,128)(2,1)S(1)} %bitcast.27), channel_id=1, replica_groups=mesh['dp'=4,'seq'=64] {'seq'}, dimensions={0} | all-to-all | bytes 3538944 | tf_op jit(solution)/shard_map/all_to_all | solution.py:254
  181.9 1.7 fusion.29
  (88 shorter events, 19.1 us)
Async XLA Ops:
  1.7 18.7 %copy-start.4 = (bf16[1,128,768]{1,2,0:T(8,128)(2,1)}, bf16[1,128,768]{1,2,0:T(8,128)(2,1)S(1)}, u32[]{:S(2)}) copy-start(bf16[1,128,768]{1,2,0:T(8,128)(2,1)S(1)} %copy.20) | copy-start | bytes 589828
  1.9 9.4 %collective-permute-start = (bf16[16,768]{0,1:T(8,128)(2,1)S(1)}, bf16[16,768]{0,1:T(8,128)(2,1)S(1)}, u32[]{:S(2)}, u32[]{:S(2)}) collective-permute-start(bf16[16,768]{0,1:T(8,128)(2,1)S(1)} %get-tuple-element.56), channel_id=1, source_target_pairs={{0,1},{1,2},{2,3},{3,4},{4,5},{5,6},{6,7},{7,8},{8,9},{9,10},{10,1... | collective-permute-start | bytes 73736 | tf_op jit(solution)/shard_map/ppermute | solution.py:31
  5.3 8.3 %collective-permute-start.1 = (bf16[16,768]{0,1:T(8,128)(2,1)S(1)}, bf16[16,768]{0,1:T(8,128)(2,1)S(1)}, u32[]{:S(2)}, u32[]{:S(2)}) collective-permute-start(bf16[16,768]{0,1:T(8,128)(2,1)S(1)} %get-tuple-element.57), channel_id=1, source_target_pairs={{1,0},{2,1},{3,2},{4,3},{5,4},{6,5},{7,6},{8,7},{9,8},{10,9},{11,1... | collective-permute-start | bytes 73736 | tf_op jit(solution)/shard_map/ppermute | solution.py:32
  13.8 29.5 %collective-permute-start.3 = (bf16[160,768]{0,1:T(8,128)(2,1)S(1)}, bf16[160,768]{0,1:T(8,128)(2,1)}, u32[]{:S(2)}, u32[]{:S(2)}) collective-permute-start(bf16[160,768]{0,1:T(8,128)(2,1)S(1)} %get-tuple-element.43), channel_id=1, source_target_pairs={{0,128},{64,192},{128,0},{192,64},{1,129},{65,193},{129,1},{193,65... | collective-permute-start | bytes 737288 | tf_op jit(solution)/shard_map/ppermute | solution.py:41
  14.0 30.8 %collective-permute-start.2 = (bf16[160,768]{0,1:T(8,128)(2,1)S(1)}, bf16[160,768]{0,1:T(8,128)(2,1)S(1)}, u32[]{:S(2)}, u32[]{:S(2)}) collective-permute-start(bf16[160,768]{0,1:T(8,128)(2,1)S(1)} %get-tuple-element.43), channel_id=1, source_target_pairs={{0,64},{64,0},{128,192},{192,128},{1,65},{65,1},{129,193},{193,129... | collective-permute-start | bytes 737288 | tf_op jit(solution)/shard_map/ppermute | solution.py:37
  20.4 42.8 %copy-start = (bf16[768,768]{1,0:T(8,128)(2,1)S(1)}, bf16[768,768]{1,0:T(8,128)(2,1)}, u32[]{:S(2)}) copy-start(bf16[768,768]{1,0:T(8,128)(2,1)} %first_ref.1) | copy-start | bytes 3538948
  21.7 41.4 %all-to-all-start = ((bf16[64,4,896]{2,1,0:T(4,128)(2,1)}), bf16[64,4,896]{2,1,0:T(4,128)(2,1)S(1)}, u32[]{:S(2)}, u32[]{:S(2)}) async-start(bf16[64,4,896]{2,1,0:T(4,128)(2,1)} %reshape.92), calls=%async_computation | async-start | bytes 917504 | tf_op jit(solution)/shard_map/all_to_all | solution.py:199
  43.3 30.4 %collective-permute-start.4 = (bf16[160,768]{0,1:T(8,128)(2,1)}, bf16[160,768]{0,1:T(8,128)(2,1)}, u32[]{:S(2)}, u32[]{:S(2)}) collective-permute-start(bf16[160,768]{0,1:T(8,128)(2,1)} %collective-permute-done.3), channel_id=1, source_target_pairs={{0,64},{64,0},{128,192},{192,128},{1,65},{65,1},{129,193},{193,129... | collective-permute-start | bytes 737288 | tf_op jit(solution)/shard_map/ppermute | solution.py:37
  44.8 18.5 %copy-start.6 = (bf16[160,768]{0,1:T(8,128)(2,1)}, bf16[160,768]{0,1:T(8,128)(2,1)S(1)}, u32[]{:S(2)}) copy-start(bf16[160,768]{0,1:T(8,128)(2,1)S(1)} %collective-permute-done.2) | copy-start | bytes 737284
  65.6 34.2 %copy-start.3 = (bf16[160,768]{0,1:T(8,128)(2,1)S(1)}, bf16[160,768]{0,1:T(8,128)(2,1)}, u32[]{:S(2)}) copy-start(bf16[160,768]{0,1:T(8,128)(2,1)} %copy-done.2) | copy-start | bytes 737284
  66.4 22.9 %all-to-all-start.1 = ((bf16[64,4,768]{2,1,0:T(4,128)(2,1)}), bf16[64,4,768]{2,1,0:T(4,128)(2,1)}, u32[]{:S(2)}, u32[]{:S(2)}) async-start(bf16[64,4,768]{2,1,0:T(4,128)(2,1)} %reshape.95), calls=%async_computation.1 | async-start | bytes 786432 | tf_op jit(solution)/shard_map/all_to_all | solution.py:218
  74.8 14.5 %collective-permute-start.6 = (bf16[256,768]{1,0:T(8,128)(2,1)S(1)}, bf16[256,768]{1,0:T(8,128)(2,1)S(1)}, u32[]{:S(2)}, u32[]{:S(2)}) collective-permute-start(bf16[256,768]{1,0:T(8,128)(2,1)S(1)} %get-tuple-element.22.refs_0_), channel_id=1, source_target_pairs={{0,128},{64,192},{128,0},{192,64},{1,129},{65,193},{129,1},{193,65... | collective-permute-start | bytes 1179656 | tf_op jit(solution)/shard_map/ppermute | solution.py:41
  77.4 21.4 %collective-permute-start.5 = (bf16[256,768]{1,0:T(8,128)(2,1)S(1)}, bf16[256,768]{1,0:T(8,128)(2,1)S(1)}, u32[]{:S(2)}, u32[]{:S(2)}) collective-permute-start(bf16[256,768]{1,0:T(8,128)(2,1)S(1)} %get-tuple-element.22.refs_0_), channel_id=1, source_target_pairs={{0,64},{64,0},{128,192},{192,128},{1,65},{65,1},{129,193},{193,129... | collective-permute-start | bytes 1179656 | tf_op jit(solution)/shard_map/ppermute | solution.py:37
  78.4 13.6 %collective-permute-start.10 = (bf16[256,192]{1,0:T(8,128)(2,1)}, bf16[256,192]{1,0:T(8,128)(2,1)S(1)}, u32[]{:S(2)}, u32[]{:S(2)}) collective-permute-start(bf16[256,192]{1,0:T(8,128)(2,1)} %get-tuple-element.44), channel_id=1, source_target_pairs={{0,192},{64,128},{128,64},{192,0},{1,193},{65,129},{129,65},{193,1... | collective-permute-start | bytes 294920 | tf_op jit(solution)/shard_map/ppermute | solution.py:56
  79.9 14.0 %collective-permute-start.9 = (bf16[256,192]{1,0:T(8,128)(2,1)}, bf16[256,192]{1,0:T(8,128)(2,1)S(1)}, u32[]{:S(2)}, u32[]{:S(2)}) collective-permute-start(bf16[256,192]{1,0:T(8,128)(2,1)} %get-tuple-element.45), channel_id=1, source_target_pairs={{0,128},{64,192},{128,0},{192,64},{1,129},{65,193},{129,1},{193,65... | collective-permute-start | bytes 294920 | tf_op jit(solution)/shard_map/ppermute | solution.py:56
  80.5 17.3 %collective-permute-start.8 = (bf16[256,192]{1,0:T(8,128)(2,1)}, bf16[256,192]{1,0:T(8,128)(2,1)S(1)}, u32[]{:S(2)}, u32[]{:S(2)}) collective-permute-start(bf16[256,192]{1,0:T(8,128)(2,1)} %get-tuple-element.46), channel_id=1, source_target_pairs={{0,64},{64,0},{128,192},{192,128},{1,65},{65,1},{129,193},{193,129... | collective-permute-start | bytes 294920 | tf_op jit(solution)/shard_map/ppermute | solution.py:56
  89.3 10.1 %collective-permute-start.7 = (bf16[256,768]{1,0:T(8,128)(2,1)S(1)}, bf16[256,768]{1,0:T(8,128)(2,1)S(1)}, u32[]{:S(2)}, u32[]{:S(2)}) collective-permute-start(bf16[256,768]{1,0:T(8,128)(2,1)S(1)} %collective-permute-done.6.refs_2_), channel_id=1, source_target_pairs={{0,64},{64,0},{128,192},{192,128},{1,65},{65,1},{129,193},{193,129... | collective-permute-start | bytes 1179656 | tf_op jit(solution)/shard_map/ppermute | solution.py:37
  91.9 13.5 %collective-permute-start.15 = (bf16[16,768]{1,0:T(8,128)(2,1)S(1)}, bf16[16,768]{1,0:T(8,128)(2,1)S(1)}, u32[]{:S(2)}, u32[]{:S(2)}) collective-permute-start(bf16[16,768]{1,0:T(8,128)(2,1)S(1)} %get-tuple-element.50), channel_id=1, source_target_pairs={{1,0},{2,1},{3,2},{4,3},{5,4},{6,5},{7,6},{8,7},{9,8},{10,9},{11,1... | collective-permute-start | bytes 73736 | tf_op jit(solution)/shard_map/ppermute | solution.py:32
  93.9 11.5 %collective-permute-start.14 = (bf16[16,768]{1,0:T(8,128)(2,1)S(1)}, bf16[16,768]{1,0:T(8,128)(2,1)S(1)}, u32[]{:S(2)}, u32[]{:S(2)}) collective-permute-start(bf16[16,768]{1,0:T(8,128)(2,1)S(1)} %get-tuple-element.51), channel_id=1, source_target_pairs={{0,1},{1,2},{2,3},{3,4},{4,5},{5,6},{6,7},{7,8},{8,9},{9,10},{10,1... | collective-permute-start | bytes 73736 | tf_op jit(solution)/shard_map/ppermute | solution.py:31
  97.8 4.6 %collective-permute-start.13 = (bf16[128,192]{1,0:T(8,128)(2,1)S(1)}, bf16[128,192]{1,0:T(8,128)(2,1)S(1)}, u32[]{:S(2)}, u32[]{:S(2)}) collective-permute-start(bf16[128,192]{1,0:T(8,128)(2,1)S(1)} %get-tuple-element.52), channel_id=1, source_target_pairs={{0,192},{64,128},{128,64},{192,0},{1,193},{65,129},{129,65},{193,1... | collective-permute-start | bytes 147464 | tf_op jit(solution)/shard_map/ppermute | solution.py:56
  98.8 4.9 %collective-permute-start.12 = (bf16[128,192]{1,0:T(8,128)(2,1)S(1)}, bf16[128,192]{1,0:T(8,128)(2,1)S(1)}, u32[]{:S(2)}, u32[]{:S(2)}) collective-permute-start(bf16[128,192]{1,0:T(8,128)(2,1)S(1)} %get-tuple-element.53), channel_id=1, source_target_pairs={{0,128},{64,192},{128,0},{192,64},{1,129},{65,193},{129,1},{193,65... | collective-permute-start | bytes 147464 | tf_op jit(solution)/shard_map/ppermute | solution.py:56
  99.5 4.2 %collective-permute-start.11 = (bf16[128,192]{1,0:T(8,128)(2,1)S(1)}, bf16[128,192]{1,0:T(8,128)(2,1)S(1)}, u32[]{:S(2)}, u32[]{:S(2)}) collective-permute-start(bf16[128,192]{1,0:T(8,128)(2,1)S(1)} %get-tuple-element.54), channel_id=1, source_target_pairs={{0,64},{64,0},{128,192},{192,128},{1,65},{65,1},{129,193},{193,129... | collective-permute-start | bytes 147464 | tf_op jit(solution)/shard_map/ppermute | solution.py:56
  99.8 82.1 %slice-start = ((s8[5898240]{0:T(1024)(128)(4,1)}), s8[4194304]{0:T(1024)(128)(4,1)S(1)}, s32[]{:S(2)}) async-start(s8[5898240]{0:T(1024)(128)(4,1)} %bitcast.32), calls=%async_computation.3 | async-start | bytes 8388608
  103.7 78.2 %slice-start.1 = ((s8[5898240]{0:T(1024)(128)(4,1)}), s8[1703936]{0:T(1024)(128)(4,1)S(1)}, s32[]{:S(2)}) async-start(s8[5898240]{0:T(1024)(128)(4,1)} %bitcast.32), calls=%async_computation.4 | async-start | bytes 3407872
  (5 other events, 20.5 us)

commit v4 on v3

--- a/solution.py
+++ b/solution.py
@@ -84,18 +84,29 @@
 
 
 def head_kernel(scale, *refs):
-    term = contract_rows(refs[0][...], refs[4][...])
+    term = contract_rows(refs[4][...], refs[0][...])
     for feature, delta in zip(refs[1:4], refs[5:8], strict=True):
-        term = term + contract_rows(feature[...], delta[...])
+        term = term + contract_rows(delta[...], feature[...])
     refs[8][...] = (term * scale).astype(jnp.bfloat16)
 
 
 def weight_kernel(scale, taps, *refs):
-    normed_ref, head_ref, grads, out_ref = refs[0], refs[1], refs[2:6], refs[6]
-    chan_count = normed_ref.shape[0]
+    normed, head_ref, grads, out_ref = refs[0:4], refs[4], refs[5:9], refs[9]
+    chan_count = normed[0].shape[1]
     width = grads[0].shape[1]
     reach = (taps - 1) * DILATION
+    piece = out_ref.shape[2]
+    inputs = jnp.concatenate([ref[...] for ref in normed], axis=0)
     values = [ref[...].astype(jnp.float32) for ref in grads]
+
+    def put(first, block):
+        done = 0
+        while done < block.shape[1]:
+            part, inside = divmod(first + done, piece)
+            step = min(piece - inside, block.shape[1] - done)
+            out_ref[part, :, inside : inside + step] = block[:, done : done + step]
+            done += step
+
     for k in range(taps):
         pieces = []
         for value in values:
@@ -105,9 +116,16 @@
             if k < taps - 1:
                 pieces.append(jnp.zeros((reach - k * DILATION, width), jnp.float32))
         shifted = jnp.concatenate(pieces, axis=0).astype(jnp.bfloat16)
-        term = jnp.dot(normed_ref[...], shifted, preferred_element_type=jnp.float32)
-        out_ref[k * chan_count : (k + 1) * chan_count, :] = (term * scale).astype(jnp.bfloat16)
-    out_ref[taps * chan_count :, :] = head_ref[...]
+        term = contract_rows(shifted, inputs)
+        put(k * chan_count, (term * scale).astype(jnp.bfloat16))
+    put(taps * chan_count, head_ref[...])
+
+
+def fold_kernel(terms_ref, out_ref):
+    total = terms_ref[0].astype(jnp.float32)
+    for index in range(1, terms_ref.shape[0]):
+        total = total + terms_ref[index].astype(jnp.float32)
+    out_ref[...] = total.T.astype(jnp.bfloat16)
 
 
 def in_vmem(kernel, shapes, count, limit):
@@ -226,7 +244,7 @@
     delta_peers = dp_columns(delta, col_width)
     head_term = in_vmem(
         functools.partial(head_kernel, 1.0 / math.sqrt(dp_count * pair_count * shards)),
-        jax.ShapeDtypeStruct((out_count, col_width), jnp.bfloat16),
+        jax.ShapeDtypeStruct((col_width, out_count), jnp.bfloat16),
         8,
         KERNEL_VMEM,
     )(*feature_peers, *delta_peers)
@@ -234,32 +252,54 @@
     preact_grad = (hidden_grad * slope).astype(jnp.bfloat16)
 
     grad_peers = dp_columns(preact_grad, col_width)
-    grad_above, grad_below = seq_halo(preact_grad, reach_rows)
-
-    normed_all = jnp.concatenate(
-        [padded] + [normalise(peer)[2] for peer in padded_peers[1:]], axis=0
-    ).T
+
+    normed_peers = [padded] + [normalise(peer)[2] for peer in padded_peers[1:]]
+    row_total = tap_count * chan_count + out_count
+    outer = 4
+    inner = shards // outer
     term = in_vmem(
         functools.partial(
             weight_kernel, 1.0 / math.sqrt(dp_count * row_count * shards), tap_count
         ),
-        jax.ShapeDtypeStruct((tap_count * chan_count + out_count, col_width), jnp.bfloat16),
-        6,
+        jax.ShapeDtypeStruct((outer, col_width, row_total // outer), jnp.bfloat16),
+        9,
         KERNEL_VMEM,
-    )(normed_all, head_term, *grad_peers)
-    term, grad_above, grad_below, norm_inverse = lax.optimization_barrier(
-        (term, grad_above, grad_below, norm_inverse)
-    )
-    share = term.shape[0] // shards
+    )(*normed_peers, head_term, *grad_peers)
     terms = lax.all_to_all(
-        term.reshape(shards, share, col_width), "seq", split_axis=0, concat_axis=0, tiled=True
-    )
-    terms, grad_above, grad_below, late_input, norm_inverse = lax.optimization_barrier(
-        (terms, grad_above, grad_below, activations[0], norm_inverse)
-    )
-    input_values = late_input.astype(jnp.float32)
-    weight_grads = jnp.sum(terms.astype(jnp.float32), axis=0)
-
+        term,
+        "seq",
+        split_axis=0,
+        concat_axis=0,
+        tiled=True,
+        axis_index_groups=[[i + j * inner for j in range(outer)] for i in range(inner)],
+    )
+    terms, halo_source = lax.optimization_barrier((terms, preact_grad))
+    folded = in_vmem(
+        fold_kernel,
+        jax.ShapeDtypeStruct((row_total // outer, col_width), jnp.bfloat16),
+        1,
+        KERNEL_VMEM,
+    )(terms)
+    shares = lax.all_to_all(
+        folded.reshape(inner, row_total // shards, col_width),
+        "seq",
+        split_axis=0,
+        concat_axis=0,
+        tiled=True,
+        axis_index_groups=[[j * inner + i for i in range(inner)] for j in range(outer)],
+    )
+    weight_grads = jnp.sum(shares.astype(jnp.float32), axis=0)
+
+    input_grad = data_grad(
+        activations[0], norm_inverse, halo_source, conv_weight, reach_rows, tap_count
+    )
+    return (input_grad.astype(jnp.bfloat16)[None], weight_grads)
+
+
+def data_grad(inputs, norm_inverse, preact_grad, conv_weight, reach_rows, tap_count):
+    row_count, chan_count = inputs.shape
+    input_values = inputs.astype(jnp.float32)
+    grad_above, grad_below = seq_halo(preact_grad, reach_rows)
     grad_padded = jnp.concatenate([grad_above, preact_grad, grad_below], axis=0)
     spread = lax.dot_general(
         grad_padded, conv_weight, (((1,), (1,)), ((), ())), preferred_element_type=jnp.float32
@@ -274,10 +314,9 @@
                 tap_index * chan_count : (tap_index + 1) * chan_count,
             ]
         )
-    input_grad = norm_inverse * normed_grad - input_values * norm_inverse**3 * jnp.mean(
+    return norm_inverse * normed_grad - input_values * norm_inverse**3 * jnp.mean(
         normed_grad * input_values, axis=1, keepdims=True
     )
-    return (input_grad.astype(jnp.bfloat16)[None], weight_grads)
 
 
 def solution(mesh):

time: 186 us -> 152 us (0.82)
  the two profiles are of different devices: /device:TPU:32 before, /device:TPU:24 now
where the time goes in v4:
time: 152 us; the launch traced here: 151 us
  starting transfers between devices  54 us (36%)
  waiting for transfers between devices  36.9 us (24%)
  blocking collectives  24.3 us (16%)
  matrix products  11.9 us (8%)
  other arithmetic  11.7 us (8%)
  local copies, waits for them, and re-layouts  6.45 us (4%)
  Pallas kernels  4.37 us (3%)
    all_to_all x1, blocking collectives, per_device(): lax.all_to_all(term, 'seq', split_axis=0, concat_axis=0, tiled=True, axis...  24.3 us
    ppermute x2, starting transfers between devices, seq_halo(): lax.ppermute(cells[:width], 'seq', [(i + 1, i) for i in range(count - 1)])  16.7 us
    all_to_all x1, waiting for transfers between devices, per_device(): lax.all_to_all(sent.reshape(shards, capacity, out_count + LANES), 'seq',...  12.3 us
    all_to_all x1, waiting for transfers between devices, per_device(): lax.all_to_all(folded.reshape(inner, row_total // shards, col_width), 'se...  11.3 us
    ppermute x2, waiting for transfers between devices, swap_z(): return lax.ppermute(field, 'dp', [(0, 2), (1, 3), (2, 0), (3, 1)])  10.9 us
    all_to_all x1, starting transfers between devices, per_device(): lax.all_to_all(sent.reshape(shards, capacity, out_count + LANES), 'seq',...  10.7 us
    all_to_all x1, starting transfers between devices, per_device(): lax.all_to_all(back.reshape(shards, capacity, out_count), 'seq', split_ax...  7.38 us
    ppermute x2, starting transfers between devices, seq_halo(): lax.ppermute(cells[-width:], 'seq', [(i, i + 1) for i in range(count - 1)])  6.75 us
  transfers between devices with their start and end apart: 19, of which 5 were waited for; matrix products, arithmetic and copies ran while one was open for 17% of the time, Pallas kernels for 2%

profile of v4, /device:TPU:24, one launch (start us, length us, event | category | flops | bytes accessed | tf_op | source)
XLA Modules:
  0.0 150.7 jit_solution(781634926636376231)
XLA Ops:
  1.4 3.4 %collective-permute-start = (bf16[16,768]{1,0:T(8,128)(2,1)S(1)}, bf16[16,768]{1,0:T(8,128)(2,1)S(1)}, u32[]{:S(2)}, u32[]{:S(2)}) collective-permute-start(bf16[16,768]{1,0:T(8,128)(2,1)S(1)} %get-tuple-element.38), channel_id=1, source_target_pairs={{0,1},{1,2},{2,3},{3,4},{4,5},{5,6},{6,7},{7,8},{8,9},{9,10},{10,1... | collective-permute-start | bytes 73736 | tf_op jit(solution)/shard_map/ppermute | solution.py:31
  4.8 9.1 %collective-permute-start.1 = (bf16[16,768]{1,0:T(8,128)(2,1)S(1)}, bf16[16,768]{1,0:T(8,128)(2,1)S(1)}, u32[]{:S(2)}, u32[]{:S(2)}) collective-permute-start(bf16[16,768]{1,0:T(8,128)(2,1)S(1)} %get-tuple-element.39), channel_id=1, source_target_pairs={{1,0},{2,1},{3,2},{4,3},{5,4},{6,5},{7,6},{8,7},{9,8},{10,9},{11,1... | collective-permute-start | bytes 73736 | tf_op jit(solution)/shard_map/ppermute | solution.py:32
  17.3 1.1 fusion.3
  18.3 1.1 collective-permute-start.3
  19.7 5.2 %fusion.21 = (f32[128,768]{1,0:T(8,128)}, bf16[128,768]{1,0:T(8,128)(2,1)S(1)}) fusion(bf16[128,3840]{1,0:T(8,128)(2,1)S(1)} %slice_dynamic-update-slice_fusion, bf16[3840,768]{1,0:T(8,128)(2,1)} %param.10), kind=kOutput, calls=%fused_computation.38 | convolution fusion | flops 762150912 | bytes 7471104 | tf_op jit(solution)/shard_map/dot_general | solution.py:209
  26.1 10.7 %all-to-all-start = ((bf16[64,4,896]{2,1,0:T(4,128)(2,1)}), bf16[64,4,896]{2,1,0:T(4,128)(2,1)S(1)}, u32[]{:S(2)}, u32[]{:S(2)}) async-start(bf16[64,4,896]{2,1,0:T(4,128)(2,1)} %reshape.93), calls=%async_computation | async-start | bytes 917504 | tf_op jit(solution)/shard_map/all_to_all | solution.py:217
  37.5 1.1 fusion.7
  39.8 12.3 %all-to-all-done = bf16[64,4,896]{2,1,0:T(4,128)(2,1)S(1)} async-done(((bf16[64,4,896]{2,1,0:T(4,128)(2,1)}), bf16[64,4,896]{2,1,0:T(4,128)(2,1)S(1)}, u32[]{:S(2)}, u32[]{:S(2)}) %all-to-all-start) | async-done | bytes 458784 | tf_op jit(solution)/shard_map/all_to_all | solution.py:217
  53.1 1.4 shard_map.104
  56.1 7.4 %all-to-all-start.1 = ((bf16[64,4,768]{2,1,0:T(4,128)(2,1)}), bf16[64,4,768]{2,1,0:T(4,128)(2,1)S(1)}, u32[]{:S(2)}, u32[]{:S(2)}) async-start(bf16[64,4,768]{2,1,0:T(4,128)(2,1)} %reshape.96), calls=%async_computation.1 | async-start | bytes 786432 | tf_op jit(solution)/shard_map/all_to_all | solution.py:236
  65.0 1.1 fusion.9
  67.2 1.7 %collective-permute-start.10 = (bf16[256,192]{1,0:T(8,128)(2,1)}, bf16[256,192]{1,0:T(8,128)(2,1)S(1)}, u32[]{:S(2)}, u32[]{:S(2)}) collective-permute-start(bf16[256,192]{1,0:T(8,128)(2,1)} %get-tuple-element.26), channel_id=1, source_target_pairs={{0,192},{64,128},{128,64},{192,0},{1,193},{65,129},{129,65},{193,1... | collective-permute-start | bytes 294920 | tf_op jit(solution)/shard_map/ppermute | solution.py:56
  69.3 10.9 %collective-permute-done.6.refs_2_ = bf16[256,768]{1,0:T(8,128)(2,1)S(1)} collective-permute-done((bf16[256,768]{1,0:T(8,128)(2,1)S(1)}, bf16[256,768]{1,0:T(8,128)(2,1)S(1)}, u32[]{:S(2)}, u32[]{:S(2)}) %collective-permute-start.6) | collective-permute-done | bytes 393248 | tf_op jit(solution)/shard_map/ppermute | solution.py:41
  81.1 1.5 fusion.1
  82.8 2.4 %collective-permute-start.13 = (bf16[128,192]{1,0:T(8,128)(2,1)S(1)}, bf16[128,192]{1,0:T(8,128)(2,1)S(1)}, u32[]{:S(2)}, u32[]{:S(2)}) collective-permute-start(bf16[128,192]{1,0:T(8,128)(2,1)S(1)} %get-tuple-element.34), channel_id=1, source_target_pairs={{0,192},{64,128},{128,64},{192,0},{1,193},{65,129},{129,65},{193,1... | collective-permute-start | bytes 147464 | tf_op jit(solution)/shard_map/ppermute | solution.py:56
  87.7 1.8 %collective-permute-done.12.refs_7_ = bf16[128,192]{1,0:T(8,128)(2,1)S(1)} collective-permute-done((bf16[128,192]{1,0:T(8,128)(2,1)S(1)}, bf16[128,192]{1,0:T(8,128)(2,1)S(1)}, u32[]{:S(2)}, u32[]{:S(2)}) %collective-permute-start.12) | collective-permute-done | bytes 49184 | tf_op jit(solution)/shard_map/ppermute | solution.py:56
  89.5 1.3 shard_map.106
  90.8 24.3 %all_to_all.20.terms_ref = bf16[4,192,1152]{2,1,0:T(8,128)(2,1)S(1)} all-to-all(bf16[4,192,1152]{2,1,0:T(8,128)(2,1)S(1)} %shard_map.106), channel_id=1, replica_groups={{0,16,32,48},{1,17,33,49},{2,18,34,50},{3,19,35,51},{4,20,36,52},{5,21,..., dimensions={0} | all-to-all | bytes 3538944 | tf_op jit(solution)/shard_map/all_to_all | solution.py:268
  115.1 3.4 %collective-permute-start.14 = (bf16[16,768]{1,0:T(8,128)(2,1)S(1)}, bf16[16,768]{1,0:T(8,128)(2,1)S(1)}, u32[]{:S(2)}, u32[]{:S(2)}) collective-permute-start(bf16[16,768]{1,0:T(8,128)(2,1)S(1)} %get-tuple-element.32), channel_id=1, source_target_pairs={{0,1},{1,2},{2,3},{3,4},{4,5},{5,6},{6,7},{7,8},{8,9},{9,10},{10,1... | collective-permute-start | bytes 73736 | tf_op jit(solution)/shard_map/ppermute | solution.py:31
  118.5 7.6 %collective-permute-start.15 = (bf16[16,768]{1,0:T(8,128)(2,1)S(1)}, bf16[16,768]{1,0:T(8,128)(2,1)S(1)}, u32[]{:S(2)}, u32[]{:S(2)}) collective-permute-start(bf16[16,768]{1,0:T(8,128)(2,1)S(1)} %get-tuple-element.33), channel_id=1, source_target_pairs={{1,0},{2,1},{3,2},{4,3},{5,4},{6,5},{7,6},{8,7},{9,8},{10,9},{11,1... | collective-permute-start | bytes 73736 | tf_op jit(solution)/shard_map/ppermute | solution.py:32
  126.3 1.2 shard_map.107
  127.4 5.4 %all-to-all-start.3 = ((bf16[16,72,192]{2,1,0:T(8,128)(2,1)}), bf16[16,72,192]{2,1,0:T(8,128)(2,1)S(1)}, u32[]{:S(2)}, u32[]{:S(2)}) async-start(bf16[16,72,192]{2,1,0:T(8,128)(2,1)} %bitcast.9), calls=%async_computation.3 | async-start | bytes 1179648 | tf_op jit(solution)/shard_map/all_to_all | solution.py:283
  132.8 4.8 %fusion.29 = f32[160,3840]{1,0:T(8,128)S(1)} fusion(bf16[3840,768]{1,0:T(8,128)(2,1)} %param.10, bf16[16,768]{1,0:T(8,128)(2,1)S(1)} %collective-permute-done.15, bf16[128,768]{1,0:T(8,128)(2,1)S(1)} %fusion.1, bf16[16,768]{1,0:T(8,128)(2,1)S(1)} %collective-permute-done.14), kind=kOutput, calls=%fused_computation.59 | convolution fusion | flops 944455680 | bytes 8601600 | tf_op jit(solution)/shard_map/dot_general | solution.py:304
  138.6 11.3 %all-to-all-done.3 = bf16[16,72,192]{2,1,0:T(8,128)(2,1)S(1)} async-done(((bf16[16,72,192]{2,1,0:T(8,128)(2,1)}), bf16[16,72,192]{2,1,0:T(8,128)(2,1)S(1)}, u32[]{:S(2)}, u32[]{:S(2)}) %all-to-all-start.3) | async-done | bytes 442400 | tf_op jit(solution)/shard_map/all_to_all | solution.py:283
  (79 shorter events, 18.3 us)
Async XLA Ops:
  1.4 15.9 %collective-permute-start = (bf16[16,768]{1,0:T(8,128)(2,1)S(1)}, bf16[16,768]{1,0:T(8,128)(2,1)S(1)}, u32[]{:S(2)}, u32[]{:S(2)}) collective-permute-start(bf16[16,768]{1,0:T(8,128)(2,1)S(1)} %get-tuple-element.38), channel_id=1, source_target_pairs={{0,1},{1,2},{2,3},{3,4},{4,5},{5,6},{6,7},{7,8},{8,9},{9,10},{10,1... | collective-permute-start | bytes 73736 | tf_op jit(solution)/shard_map/ppermute | solution.py:31
  4.8 12.5 %collective-permute-start.1 = (bf16[16,768]{1,0:T(8,128)(2,1)S(1)}, bf16[16,768]{1,0:T(8,128)(2,1)S(1)}, u32[]{:S(2)}, u32[]{:S(2)}) collective-permute-start(bf16[16,768]{1,0:T(8,128)(2,1)S(1)} %get-tuple-element.39), channel_id=1, source_target_pairs={{1,0},{2,1},{3,2},{4,3},{5,4},{6,5},{7,6},{8,7},{9,8},{10,9},{11,1... | collective-permute-start | bytes 73736 | tf_op jit(solution)/shard_map/ppermute | solution.py:32
  16.4 8.5 %copy-start.5 = (bf16[256,128]{1,0:T(8,128)(2,1)}, bf16[256,128]{1,0:T(8,128)(2,1)S(1)}, u32[]{:S(2)}) copy-start(bf16[256,128]{1,0:T(8,128)(2,1)S(1)} %fusion.36) | copy-start | bytes 196612
  18.3 18.7 %collective-permute-start.3 = (bf16[160,768]{1,0:T(8,128)(2,1)S(1)}, bf16[160,768]{1,0:T(8,128)(2,1)}, u32[]{:S(2)}, u32[]{:S(2)}) collective-permute-start(bf16[160,768]{1,0:T(8,128)(2,1)S(1)} %get-tuple-element.25), channel_id=1, source_target_pairs={{0,128},{64,192},{128,0},{192,64},{1,129},{65,193},{129,1},{193,65... | collective-permute-start | bytes 737288 | tf_op jit(solution)/shard_map/ppermute | solution.py:41
  19.7 17.3 %copy-start.6 = (bf16[768]{0:T(1024)(128)(2,1)S(1)}, bf16[768]{0:T(1024)(128)(2,1)}, u32[]{:S(2)}) copy-start(bf16[768]{0:T(1024)(128)(2,1)} %param.12) | copy-start | bytes 4612
  24.9 27.3 %copy-start = (bf16[768,768]{1,0:T(8,128)(2,1)S(1)}, bf16[768,768]{1,0:T(8,128)(2,1)}, u32[]{:S(2)}) copy-start(bf16[768,768]{1,0:T(8,128)(2,1)} %first_ref.1) | copy-start | bytes 3538948
  26.1 26.0 %all-to-all-start = ((bf16[64,4,896]{2,1,0:T(4,128)(2,1)}), bf16[64,4,896]{2,1,0:T(4,128)(2,1)S(1)}, u32[]{:S(2)}, u32[]{:S(2)}) async-start(bf16[64,4,896]{2,1,0:T(4,128)(2,1)} %reshape.93), calls=%async_computation | async-start | bytes 917504 | tf_op jit(solution)/shard_map/all_to_all | solution.py:217
  36.8 1.8 %collective-permute-start.2 = (bf16[160,768]{1,0:T(8,128)(2,1)S(1)}, bf16[160,768]{1,0:T(8,128)(2,1)S(1)}, u32[]{:S(2)}, u32[]{:S(2)}) collective-permute-start(bf16[160,768]{1,0:T(8,128)(2,1)S(1)} %get-tuple-element.25), channel_id=1, source_target_pairs={{0,64},{64,0},{128,192},{192,128},{1,65},{65,1},{129,193},{193,129... | collective-permute-start | bytes 737288 | tf_op jit(solution)/shard_map/ppermute | solution.py:37
  37.0 28.0 %collective-permute-start.4 = (bf16[160,768]{1,0:T(8,128)(2,1)}, bf16[160,768]{1,0:T(8,128)(2,1)}, u32[]{:S(2)}, u32[]{:S(2)}) collective-permute-start(bf16[160,768]{1,0:T(8,128)(2,1)} %collective-permute-done.3), channel_id=1, source_target_pairs={{0,64},{64,0},{128,192},{192,128},{1,65},{65,1},{129,193},{193,129... | collective-permute-start | bytes 737288 | tf_op jit(solution)/shard_map/ppermute | solution.py:37
  38.6 13.6 %copy-start.4 = (bf16[160,768]{1,0:T(8,128)(2,1)}, bf16[160,768]{1,0:T(8,128)(2,1)S(1)}, u32[]{:S(2)}) copy-start(bf16[160,768]{1,0:T(8,128)(2,1)S(1)} %collective-permute-done.2) | copy-start | bytes 737284
  56.1 24.1 %all-to-all-start.1 = ((bf16[64,4,768]{2,1,0:T(4,128)(2,1)}), bf16[64,4,768]{2,1,0:T(4,128)(2,1)S(1)}, u32[]{:S(2)}, u32[]{:S(2)}) async-start(bf16[64,4,768]{2,1,0:T(4,128)(2,1)} %reshape.96), calls=%async_computation.1 | async-start | bytes 786432 | tf_op jit(solution)/shard_map/all_to_all | solution.py:236
  64.6 15.7 %collective-permute-start.6 = (bf16[256,768]{1,0:T(8,128)(2,1)S(1)}, bf16[256,768]{1,0:T(8,128)(2,1)S(1)}, u32[]{:S(2)}, u32[]{:S(2)}) collective-permute-start(bf16[256,768]{1,0:T(8,128)(2,1)S(1)} %get-tuple-element.15.refs_0_), channel_id=1, source_target_pairs={{0,128},{64,192},{128,0},{192,64},{1,129},{65,193},{129,1},{193,65... | collective-permute-start | bytes 1179656 | tf_op jit(solution)/shard_map/ppermute | solution.py:41
  66.1 20.4 %collective-permute-start.5 = (bf16[256,768]{1,0:T(8,128)(2,1)S(1)}, bf16[256,768]{1,0:T(8,128)(2,1)S(1)}, u32[]{:S(2)}, u32[]{:S(2)}) collective-permute-start(bf16[256,768]{1,0:T(8,128)(2,1)S(1)} %get-tuple-element.15.refs_0_), channel_id=1, source_target_pairs={{0,64},{64,0},{128,192},{192,128},{1,65},{65,1},{129,193},{193,129... | collective-permute-start | bytes 1179656 | tf_op jit(solution)/shard_map/ppermute | solution.py:37
  67.2 15.6 %collective-permute-start.10 = (bf16[256,192]{1,0:T(8,128)(2,1)}, bf16[256,192]{1,0:T(8,128)(2,1)S(1)}, u32[]{:S(2)}, u32[]{:S(2)}) collective-permute-start(bf16[256,192]{1,0:T(8,128)(2,1)} %get-tuple-element.26), channel_id=1, source_target_pairs={{0,192},{64,128},{128,64},{192,0},{1,193},{65,129},{129,65},{193,1... | collective-permute-start | bytes 294920 | tf_op jit(solution)/shard_map/ppermute | solution.py:56
  68.9 16.3 %collective-permute-start.9 = (bf16[256,192]{1,0:T(8,128)(2,1)}, bf16[256,192]{1,0:T(8,128)(2,1)S(1)}, u32[]{:S(2)}, u32[]{:S(2)}) collective-permute-start(bf16[256,192]{1,0:T(8,128)(2,1)} %get-tuple-element.27), channel_id=1, source_target_pairs={{0,128},{64,192},{128,0},{192,64},{1,129},{65,193},{129,1},{193,65... | collective-permute-start | bytes 294920 | tf_op jit(solution)/shard_map/ppermute | solution.py:56
  69.3 15.9 %collective-permute-start.8 = (bf16[256,192]{1,0:T(8,128)(2,1)}, bf16[256,192]{1,0:T(8,128)(2,1)S(1)}, u32[]{:S(2)}, u32[]{:S(2)}) collective-permute-start(bf16[256,192]{1,0:T(8,128)(2,1)} %get-tuple-element.28), channel_id=1, source_target_pairs={{0,64},{64,0},{128,192},{192,128},{1,65},{65,1},{129,193},{193,129... | collective-permute-start | bytes 294920 | tf_op jit(solution)/shard_map/ppermute | solution.py:56
  80.2 6.3 %collective-permute-start.7 = (bf16[256,768]{1,0:T(8,128)(2,1)S(1)}, bf16[256,768]{1,0:T(8,128)(2,1)S(1)}, u32[]{:S(2)}, u32[]{:S(2)}) collective-permute-start(bf16[256,768]{1,0:T(8,128)(2,1)S(1)} %collective-permute-done.6.refs_2_), channel_id=1, source_target_pairs={{0,64},{64,0},{128,192},{192,128},{1,65},{65,1},{129,193},{193,129... | collective-permute-start | bytes 1179656 | tf_op jit(solution)/shard_map/ppermute | solution.py:37
  82.8 4.9 %collective-permute-start.13 = (bf16[128,192]{1,0:T(8,128)(2,1)S(1)}, bf16[128,192]{1,0:T(8,128)(2,1)S(1)}, u32[]{:S(2)}, u32[]{:S(2)}) collective-permute-start(bf16[128,192]{1,0:T(8,128)(2,1)S(1)} %get-tuple-element.34), channel_id=1, source_target_pairs={{0,192},{64,128},{128,64},{192,0},{1,193},{65,129},{129,65},{193,1... | collective-permute-start | bytes 147464 | tf_op jit(solution)/shard_map/ppermute | solution.py:56
  85.2 4.3 %collective-permute-start.12 = (bf16[128,192]{1,0:T(8,128)(2,1)S(1)}, bf16[128,192]{1,0:T(8,128)(2,1)S(1)}, u32[]{:S(2)}, u32[]{:S(2)}) collective-permute-start(bf16[128,192]{1,0:T(8,128)(2,1)S(1)} %get-tuple-element.35), channel_id=1, source_target_pairs={{0,128},{64,192},{128,0},{192,64},{1,129},{65,193},{129,1},{193,65... | collective-permute-start | bytes 147464 | tf_op jit(solution)/shard_map/ppermute | solution.py:56
  85.3 4.2 %collective-permute-start.11 = (bf16[128,192]{1,0:T(8,128)(2,1)S(1)}, bf16[128,192]{1,0:T(8,128)(2,1)S(1)}, u32[]{:S(2)}, u32[]{:S(2)}) collective-permute-start(bf16[128,192]{1,0:T(8,128)(2,1)S(1)} %get-tuple-element.36), channel_id=1, source_target_pairs={{0,64},{64,0},{128,192},{192,128},{1,65},{65,1},{129,193},{193,129... | collective-permute-start | bytes 147464 | tf_op jit(solution)/shard_map/ppermute | solution.py:56
  115.1 17.7 %collective-permute-start.14 = (bf16[16,768]{1,0:T(8,128)(2,1)S(1)}, bf16[16,768]{1,0:T(8,128)(2,1)S(1)}, u32[]{:S(2)}, u32[]{:S(2)}) collective-permute-start(bf16[16,768]{1,0:T(8,128)(2,1)S(1)} %get-tuple-element.32), channel_id=1, source_target_pairs={{0,1},{1,2},{2,3},{3,4},{4,5},{5,6},{6,7},{7,8},{8,9},{9,10},{10,1... | collective-permute-start | bytes 73736 | tf_op jit(solution)/shard_map/ppermute | solution.py:31
  118.5 14.3 %collective-permute-start.15 = (bf16[16,768]{1,0:T(8,128)(2,1)S(1)}, bf16[16,768]{1,0:T(8,128)(2,1)S(1)}, u32[]{:S(2)}, u32[]{:S(2)}) collective-permute-start(bf16[16,768]{1,0:T(8,128)(2,1)S(1)} %get-tuple-element.33), channel_id=1, source_target_pairs={{1,0},{2,1},{3,2},{4,3},{5,4},{6,5},{7,6},{8,7},{9,8},{10,9},{11,1... | collective-permute-start | bytes 73736 | tf_op jit(solution)/shard_map/ppermute | solution.py:32
  126.3 11.3 %copy-start.3 = (bf16[1,128,768]{2,1,0:T(8,128)(2,1)S(1)}, bf16[1,128,768]{2,1,0:T(8,128)(2,1)}, u32[]{:S(2)}) copy-start(bf16[1,128,768]{2,1,0:T(8,128)(2,1)} %param.9) | copy-start | bytes 589828
  127.4 22.5 %all-to-all-start.3 = ((bf16[16,72,192]{2,1,0:T(8,128)(2,1)}), bf16[16,72,192]{2,1,0:T(8,128)(2,1)S(1)}, u32[]{:S(2)}, u32[]{:S(2)}) async-start(bf16[16,72,192]{2,1,0:T(8,128)(2,1)} %bitcast.9), calls=%async_computation.3 | async-start | bytes 1179648 | tf_op jit(solution)/shard_map/all_to_all | solution.py:283
  (2 other events, 1.7 us)

commit v5 on v4

--- a/solution.py
+++ b/solution.py
@@ -11,6 +11,7 @@
 
 DILATION = 8
 LANES = 128
+SEQ_GRID = (4, 4, 4)
 KERNEL_VMEM = 16 * 1024 * 1024
 
 
@@ -47,19 +48,40 @@
     return field, core, z_side, swap_core(z_side)
 
 
-def dp_columns(field, width):
-    index = lax.axis_index("dp")
-    found = []
-    for flip in range(4):
-        piece = lax.dynamic_slice_in_dim(field, (index ^ flip) * width, width, axis=1)
-        if flip:
-            piece = lax.ppermute(piece, "dp", [(i, i ^ flip) for i in range(4)])
-        found.append(piece)
-    return found
-
-
-def pair_kernel(got_ref, hidden_ref, first_ref, second_ref, cotangent_ref, *outs):
-    back_ref, part_ref, feature_ref, delta_ref = outs
+def dp_exchange(pieces):
+    return [pieces[0]] + [
+        lax.ppermute(pieces[flip], "dp", [(i, i ^ flip) for i in range(4)]) for flip in range(1, 4)
+    ]
+
+
+def split_columns(values, place, blocks_ref, outs):
+    tiles = [values[:, i * LANES : (i + 1) * LANES] for i in range(values.shape[1] // LANES)]
+    turned = [pltpu.roll(tile, LANES // 2, axis=1) for tile in tiles]
+    low = lax.broadcasted_iota(jnp.int32, tiles[0].shape, 1) < LANES // 2
+    for pair in range(2):
+        first, middle, last = range(3 * pair, 3 * pair + 3)
+        blocks = (
+            (tiles[first], jnp.where(low, tiles[middle], turned[middle])),
+            (
+                jnp.where(low, turned[middle], turned[last]),
+                jnp.where(low, turned[last], tiles[last]),
+            ),
+        )
+        for side, halves in enumerate(blocks):
+            blocks_ref[2 * pair + side] = jnp.concatenate(halves, axis=1).astype(jnp.bfloat16)
+    for flip, out in enumerate(outs):
+        out[...] = blocks_ref[place ^ flip]
+
+
+def grad_kernel(place_ref, hits_ref, back_ref, part_ref, slope_ref, grad_ref, *rest):
+    hidden_grad = part_ref[...] + contract_rows(hits_ref[...], back_ref[...])
+    grad = hidden_grad * slope_ref[...]
+    grad_ref[...] = grad.astype(jnp.bfloat16)
+    split_columns(grad, place_ref[0], rest[-1], rest[:-1])
+
+
+def pair_kernel(place_ref, got_ref, hidden_ref, first_ref, second_ref, cotangent_ref, *outs):
+    back_ref, part_ref, feature_ref = outs[:3]
     chan_count = hidden_ref.shape[1]
     slots = got_ref.shape[0]
     note = got_ref[:, chan_count:].astype(jnp.float32)
@@ -71,10 +93,9 @@
     feature = (donor * accept).astype(jnp.bfloat16)
     feature_ref[...] = feature
     head_preact = jnp.dot(feature, first_ref[...], preferred_element_type=jnp.float32)
-    delta = (score * second_ref[...].astype(jnp.float32) * gelu_slope(head_preact)).astype(
-        jnp.bfloat16
-    )
-    delta_ref[...] = delta
+    delta = score * second_ref[...].astype(jnp.float32) * gelu_slope(head_preact)
+    split_columns(delta, place_ref[0], outs[-1], outs[3:-1])
+    delta = delta.astype(jnp.bfloat16)
     feature_grad = lax.dot_general(
         delta, first_ref[...], (((1,), (1,)), ((), ())), preferred_element_type=jnp.float32
     )
@@ -84,27 +105,31 @@
 
 
 def head_kernel(scale, *refs):
-    term = contract_rows(refs[4][...], refs[0][...])
+    term = contract_rows(refs[0][...], refs[4][...])
     for feature, delta in zip(refs[1:4], refs[5:8], strict=True):
-        term = term + contract_rows(delta[...], feature[...])
+        term = term + contract_rows(feature[...], delta[...])
     refs[8][...] = (term * scale).astype(jnp.bfloat16)
 
 
-def weight_kernel(scale, taps, *refs):
-    normed, head_ref, grads, out_ref = refs[0:4], refs[4], refs[5:9], refs[9]
-    chan_count = normed[0].shape[1]
+def weight_kernel(scale, taps, grid, *refs):
+    normed_ref, head_ref, grads, out_ref, tail_ref = refs[0], refs[1], refs[2:6], refs[6], refs[7]
+    ys, zs, xs = grid
+    chan_count = normed_ref.shape[0]
     width = grads[0].shape[1]
     reach = (taps - 1) * DILATION
-    piece = out_ref.shape[2]
-    inputs = jnp.concatenate([ref[...] for ref in normed], axis=0)
+    share = tail_ref.shape[0] // (ys * zs * xs)
+    chunk = share * zs + share * zs // 2
     values = [ref[...].astype(jnp.float32) for ref in grads]
 
     def put(first, block):
+        tail_ref[first : first + block.shape[0], :] = block[:, LANES:]
         done = 0
-        while done < block.shape[1]:
-            part, inside = divmod(first + done, piece)
-            step = min(piece - inside, block.shape[1] - done)
-            out_ref[part, :, inside : inside + step] = block[:, done : done + step]
+        while done < block.shape[0]:
+            owner, inside = divmod(first + done, share)
+            step = min(share - inside, block.shape[0] - done)
+            y, z, x = owner // (zs * xs), owner // xs % zs, owner % xs
+            start = (y * xs + x) * chunk + z * share + inside
+            out_ref[start : start + step, :] = block[done : done + step, :LANES].astype(jnp.bfloat16)
             done += step
 
     for k in range(taps):
@@ -116,25 +141,41 @@
             if k < taps - 1:
                 pieces.append(jnp.zeros((reach - k * DILATION, width), jnp.float32))
         shifted = jnp.concatenate(pieces, axis=0).astype(jnp.bfloat16)
-        term = contract_rows(shifted, inputs)
-        put(k * chan_count, (term * scale).astype(jnp.bfloat16))
-    put(taps * chan_count, head_ref[...])
-
-
-def fold_kernel(terms_ref, out_ref):
+        put(
+            k * chan_count,
+            jnp.dot(normed_ref[...], shifted, preferred_element_type=jnp.float32) * scale,
+        )
+    put(taps * chan_count, head_ref[...].astype(jnp.float32))
+    low = lax.broadcasted_iota(jnp.int32, (share, LANES), 1) < LANES // 2
+    for y in range(ys):
+        for x in range(xs):
+            for z in range(zs // 2):
+                rows = [((y * zs + half) * xs + x) * share for half in (z, z + zs // 2)]
+                start = (y * xs + x) * chunk + (zs + z) * share
+                out_ref[start : start + share, :] = jnp.where(
+                    low, tail_ref[rows[0] : rows[0] + share, :], tail_ref[rows[1] : rows[1] + share, :]
+                ).astype(jnp.bfloat16)
+
+
+def fold_kernel(share, zs, terms_ref, out_ref):
     total = terms_ref[0].astype(jnp.float32)
     for index in range(1, terms_ref.shape[0]):
         total = total + terms_ref[index].astype(jnp.float32)
-    out_ref[...] = total.T.astype(jnp.bfloat16)
-
-
-def in_vmem(kernel, shapes, count, limit):
+    for z in range(zs):
+        out_ref[z, :share, :] = total[z * share : (z + 1) * share].astype(jnp.bfloat16)
+        first = (zs + z % (zs // 2)) * share
+        out_ref[z, share:, :] = total[first : first + share].astype(jnp.bfloat16)
+
+
+def in_vmem(kernel, shapes, count, limit, scratch=(), scalars=0):
     spec = pl.BlockSpec(memory_space=pltpu.VMEM)
+    scalar = pl.BlockSpec(memory_space=pltpu.SMEM)
     return pl.pallas_call(
         kernel,
         out_shape=shapes,
-        in_specs=[spec] * count,
+        in_specs=[scalar] * scalars + [spec] * count,
         out_specs=jax.tree.map(lambda _: spec, shapes),
+        scratch_shapes=scratch,
         compiler_params=pltpu.CompilerParams(vmem_limit_bytes=limit),
     )
 
@@ -160,7 +201,6 @@
     pair_count = donor_row.shape[1]
     capacity = max(2, 2 * pair_count // shards)
     slots = shards * capacity
-    col_width = out_count // dp_count
 
     above, below = seq_halo(activations[0], reach_rows)
     owner = acceptor_owner[0, :, 0]
@@ -222,17 +262,16 @@
         tiled=True,
     ).reshape(slots, out_count + LANES)
     slot_shape = jax.ShapeDtypeStruct((slots, out_count), jnp.bfloat16)
-    back, part, feature, delta = in_vmem(
+    place = lax.axis_index("dp").astype(jnp.int32).reshape(1)
+    back, part, feature, *delta = in_vmem(
         pair_kernel,
-        (
-            slot_shape,
-            jax.ShapeDtypeStruct((row_count, out_count), jnp.float32),
-            slot_shape,
-            slot_shape,
-        ),
+        (slot_shape, jax.ShapeDtypeStruct((row_count, out_count), jnp.float32), slot_shape)
+        + (jax.ShapeDtypeStruct((slots, 2 * LANES), jnp.bfloat16),) * dp_count,
         5,
         KERNEL_VMEM,
-    )(got, hidden, head_first, head_second.reshape(1, out_count), hidden_cotangent[0])
+        [pltpu.VMEM((dp_count, slots, 2 * LANES), jnp.bfloat16)],
+        1,
+    )(place, got, hidden, head_first, head_second.reshape(1, out_count), hidden_cotangent[0])
     donor_grad = lax.all_to_all(
         back.reshape(shards, capacity, out_count),
         "seq",
@@ -241,54 +280,71 @@
         tiled=True,
     ).reshape(slots, out_count)
     feature_peers = dp_peers(feature)
-    delta_peers = dp_columns(delta, col_width)
+    delta_peers = dp_exchange(delta)
     head_term = in_vmem(
         functools.partial(head_kernel, 1.0 / math.sqrt(dp_count * pair_count * shards)),
-        jax.ShapeDtypeStruct((col_width, out_count), jnp.bfloat16),
+        jax.ShapeDtypeStruct((out_count, 2 * LANES), jnp.bfloat16),
         8,
         KERNEL_VMEM,
     )(*feature_peers, *delta_peers)
-    hidden_grad = part + contract_rows(hits, donor_grad)
-    preact_grad = (hidden_grad * slope).astype(jnp.bfloat16)
-
-    grad_peers = dp_columns(preact_grad, col_width)
-
-    normed_peers = [padded] + [normalise(peer)[2] for peer in padded_peers[1:]]
+    preact_grad, *grads = in_vmem(
+        grad_kernel,
+        (jax.ShapeDtypeStruct((row_count, out_count), jnp.bfloat16),)
+        + (jax.ShapeDtypeStruct((row_count, 2 * LANES), jnp.bfloat16),) * dp_count,
+        4,
+        KERNEL_VMEM,
+        [pltpu.VMEM((dp_count, row_count, 2 * LANES), jnp.bfloat16)],
+        1,
+    )(place, hits, donor_grad, part, slope)
+    grad_peers = dp_exchange(grads)
+
+    normed_all = jnp.concatenate(
+        [padded] + [normalise(peer)[2] for peer in padded_peers[1:]], axis=0
+    ).T
+    ys, zs, xs = SEQ_GRID
     row_total = tap_count * chan_count + out_count
-    outer = 4
-    inner = shards // outer
+    share = row_total // shards
+    chunk = share * zs + share * zs // 2
     term = in_vmem(
         functools.partial(
-            weight_kernel, 1.0 / math.sqrt(dp_count * row_count * shards), tap_count
+            weight_kernel, 1.0 / math.sqrt(dp_count * row_count * shards), tap_count, SEQ_GRID
         ),
-        jax.ShapeDtypeStruct((outer, col_width, row_total // outer), jnp.bfloat16),
-        9,
-        KERNEL_VMEM,
-    )(*normed_peers, head_term, *grad_peers)
+        jax.ShapeDtypeStruct((ys * xs * chunk, LANES), jnp.bfloat16),
+        6,
+        KERNEL_VMEM,
+        [pltpu.VMEM((row_total, LANES), jnp.float32)],
+    )(normed_all, head_term, *grad_peers)
     terms = lax.all_to_all(
-        term,
+        term.reshape(ys * xs, chunk, LANES),
         "seq",
         split_axis=0,
         concat_axis=0,
         tiled=True,
-        axis_index_groups=[[i + j * inner for j in range(outer)] for i in range(inner)],
+        axis_index_groups=[
+            [(y * zs + z) * xs + x for y in range(ys) for x in range(xs)] for z in range(zs)
+        ],
     )
     terms, halo_source = lax.optimization_barrier((terms, preact_grad))
     folded = in_vmem(
-        fold_kernel,
-        jax.ShapeDtypeStruct((row_total // outer, col_width), jnp.bfloat16),
+        functools.partial(fold_kernel, share, zs),
+        jax.ShapeDtypeStruct((zs, 2 * share, LANES), jnp.bfloat16),
         1,
         KERNEL_VMEM,
     )(terms)
     shares = lax.all_to_all(
-        folded.reshape(inner, row_total // shards, col_width),
+        folded,
         "seq",
         split_axis=0,
         concat_axis=0,
         tiled=True,
-        axis_index_groups=[[j * inner + i for i in range(inner)] for j in range(outer)],
-    )
-    weight_grads = jnp.sum(shares.astype(jnp.float32), axis=0)
+        axis_index_groups=[
+            [(y * zs + z) * xs + x for z in range(zs)] for y in range(ys) for x in range(xs)
+        ],
+    )
+    total = jnp.sum(shares.astype(jnp.float32), axis=0)
+    upper = lax.axis_index("seq") // xs % zs >= zs // 2
+    others = jnp.where(upper, total[share:, LANES // 2 :], total[share:, : LANES // 2])
+    weight_grads = jnp.concatenate([total[:share], others], axis=1)
 
     input_grad = data_grad(
         activations[0], norm_inverse, halo_source, conv_weight, reach_rows, tap_count

time: 152 us -> 160 us (1.053)
  blocking collectives: 24.3 us -> 0 us
  waiting for transfers between devices: 36.9 us -> 55.6 us
  starting transfers between devices: 54 us -> 59.6 us
  other arithmetic: 11.7 us -> 16.6 us
  local copies, waits for them, and re-layouts: 6.45 us -> 9.48 us
  Pallas kernels: 4.37 us -> 7.09 us
  matrix products: 11.9 us -> 9.45 us
    all_to_all x1 -> x0, blocking collectives: 24.3 us -> none  [per_device(): lax.all_to_all(term, 'seq', split_axis=0, concat_axis=0, tiled=True, axis...]
    all_to_all x1 -> x2, waiting for transfers between devices: 11.3 us -> 31 us  [the longest x1 28.1 us: per_device(): lax.all_to_all(term.reshape(ys * xs, chunk, LANES), 'seq', split_axis=0,...]
    ppermute x2, waiting for transfers between devices: 10.9 us -> 0.01 us  [swap_z(): return lax.ppermute(field, 'dp', [(0, 2), (1, 3), (2, 0), (3, 1)])]
    all_to_all x1, waiting for transfers between devices: 0.01 us -> 7.37 us  [per_device(): lax.all_to_all(back.reshape(shards, capacity, out_count), 'seq', split_ax...]
    unnamed x18 -> x30, local copies, waits for them, and re-layouts: 1.74 us -> 6.19 us
    ppermute x2, waiting for transfers between devices: 0.01 us -> 3.87 us  [seq_halo(): lax.ppermute(cells[:width], 'seq', [(i + 1, i) for i in range(count - 1)])]
    all_to_all x1 -> x2, starting transfers between devices: 5.4 us -> 9.13 us  [the longest x1 5.8 us: per_device(): lax.all_to_all(term.reshape(ys * xs, chunk, LANES), 'seq', split_axis=0,...]
    convert_element_type x4, other arithmetic: 3.26 us -> 6.58 us  [normalise(): return (values, inverse, (values * inverse).astype(jnp.bfloat16))]
  transfers between devices with their start and end apart: 19 -> 20, of which waited for: 5 -> 7; matrix products, arithmetic and copies ran while one was open for 17% -> 18% of each run, Pallas kernels for 2% -> 3%
where the time goes in v5:
time: 160 us; the launch traced here: 159 us
  starting transfers between devices  59.6 us (37%)
  waiting for transfers between devices  55.6 us (35%)
  other arithmetic  16.6 us (10%)
  local copies, waits for them, and re-layouts  9.48 us (6%)
  matrix products  9.45 us (6%)
  Pallas kernels  7.09 us (4%)
    all_to_all x1, waiting for transfers between devices, per_device(): lax.all_to_all(term.reshape(ys * xs, chunk, LANES), 'seq', split_axis=0,...  28.1 us
    ppermute x2, starting transfers between devices, seq_halo(): lax.ppermute(cells[:width], 'seq', [(i + 1, i) for i in range(count - 1)])  18.1 us
    all_to_all x1, starting transfers between devices, per_device(): lax.all_to_all(sent.reshape(shards, capacity, out_count + LANES), 'seq',...  13 us
    all_to_all x1, waiting for transfers between devices, per_device(): lax.all_to_all(sent.reshape(shards, capacity, out_count + LANES), 'seq',...  11.9 us
    all_to_all x1, starting transfers between devices, per_device(): lax.all_to_all(back.reshape(shards, capacity, out_count), 'seq', split_ax...  7.61 us
    all_to_all x1, waiting for transfers between devices, per_device(): lax.all_to_all(back.reshape(shards, capacity, out_count), 'seq', split_ax...  7.37 us
    convert_element_type x4, other arithmetic, normalise(): return (values, inverse, (values * inverse).astype(jnp.bfloat16))  6.58 us
    unnamed x30, local copies, waits for them, and re-layouts  6.19 us
  transfers between devices with their start and end apart: 20, of which 7 were waited for; matrix products, arithmetic and copies ran while one was open for 18% of the time, Pallas kernels for 3%

profile of v5, /device:TPU:24, one launch (start us, length us, event | category | flops | bytes accessed | tf_op | source)
XLA Modules:
  0.0 158.9 jit_solution(12285379872525666326)
XLA Ops:
  1.9 3.4 %collective-permute-start = (bf16[16,768]{0,1:T(8,128)(2,1)S(1)}, bf16[16,768]{0,1:T(8,128)(2,1)S(1)}, u32[]{:S(2)}, u32[]{:S(2)}) collective-permute-start(bf16[16,768]{0,1:T(8,128)(2,1)S(1)} %get-tuple-element.50), channel_id=1, source_target_pairs={{0,1},{1,2},{2,3},{3,4},{4,5},{5,6},{6,7},{7,8},{8,9},{9,10},{10,1... | collective-permute-start | bytes 73736 | tf_op jit(solution)/shard_map/ppermute | solution.py:32
  5.3 9.1 %collective-permute-start.1 = (bf16[16,768]{0,1:T(8,128)(2,1)S(1)}, bf16[16,768]{0,1:T(8,128)(2,1)S(1)}, u32[]{:S(2)}, u32[]{:S(2)}) collective-permute-start(bf16[16,768]{0,1:T(8,128)(2,1)S(1)} %get-tuple-element.51), channel_id=1, source_target_pairs={{1,0},{2,1},{3,2},{4,3},{5,4},{6,5},{7,6},{8,7},{9,8},{10,9},{11,1... | collective-permute-start | bytes 73736 | tf_op jit(solution)/shard_map/ppermute | solution.py:33
  18.9 3.9 %collective-permute-done.1 = bf16[16,768]{0,1:T(8,128)(2,1)S(1)} collective-permute-done((bf16[16,768]{0,1:T(8,128)(2,1)S(1)}, bf16[16,768]{0,1:T(8,128)(2,1)S(1)}, u32[]{:S(2)}, u32[]{:S(2)}) %collective-permute-start.1) | collective-permute-done | bytes 24608 | tf_op jit(solution)/shard_map/ppermute | solution.py:33
  25.8 4.6 %fusion.19 = (f32[128,768]{1,0:T(8,128)S(1)}, bf16[128,768]{1,0:T(8,128)(2,1)S(1)}) fusion(bf16[128,3840]{0,1:T(8,128)(2,1)S(1)} %slice_dynamic-update-slice_fusion, bf16[3840,768]{1,0:T(8,128)(2,1)} %param.10), kind=kOutput, calls=%fused_computation.35 | convolution fusion | flops 762150912 | bytes 7471104 | tf_op jit(solution)/shard_map/dot_general | solution.py:249
  31.7 13.0 %all-to-all-start = ((bf16[64,4,896]{2,1,0:T(4,128)(2,1)}), bf16[64,4,896]{2,1,0:T(4,128)(2,1)S(1)}, u32[]{:S(2)}, u32[]{:S(2)}) async-start(bf16[64,4,896]{2,1,0:T(4,128)(2,1)} %reshape.97), calls=%async_computation | async-start | bytes 917504 | tf_op jit(solution)/shard_map/all_to_all | solution.py:257
  46.9 1.8 %fusion.6 = bf16[160,768]{0,1:T(8,128)(2,1)} fusion(bf16[160,768]{0,1:T(8,128)(2,1)} %collective-permute-done.3, f32[160]{0:T(256)S(1)} %add_rsqrt_fusion.1), kind=kLoop, calls=%fused_computation.17 | loop fusion | flops 368640 | bytes 492160 | tf_op jit(solution)/shard_map/convert_element_type | solution.py:238
  48.7 11.9 %all-to-all-done = bf16[64,4,896]{2,1,0:T(4,128)(2,1)S(1)} async-done(((bf16[64,4,896]{2,1,0:T(4,128)(2,1)}), bf16[64,4,896]{2,1,0:T(4,128)(2,1)S(1)}, u32[]{:S(2)}, u32[]{:S(2)}) %all-to-all-start) | async-done | bytes 458784 | tf_op jit(solution)/shard_map/all_to_all | solution.py:257
  61.7 1.4 shard_map.104
  65.7 1.4 collective-permute-start.6
  67.9 7.6 %all-to-all-start.1 = ((bf16[64,4,768]{2,1,0:T(4,128)(2,1)}), bf16[64,4,768]{2,1,0:T(4,128)(2,1)}, u32[]{:S(2)}, u32[]{:S(2)}) async-start(bf16[64,4,768]{2,1,0:T(4,128)(2,1)} %reshape.100), calls=%async_computation.1 | async-start | bytes 786432 | tf_op jit(solution)/shard_map/all_to_all | solution.py:275
  75.5 1.8 %fusion.4 = bf16[160,768]{0,1:T(8,128)(2,1)} fusion(bf16[160,768]{0,1:T(8,128)(2,1)} %copy-done.10, f32[160]{0:T(256)S(1)} %add_rsqrt_fusion.2), kind=kLoop, calls=%fused_computation.15 | loop fusion | flops 368640 | bytes 492160 | tf_op jit(solution)/shard_map/convert_element_type | solution.py:238
  80.9 1.8 %fusion.8 = bf16[160,768]{0,1:T(8,128)(2,1)} fusion(bf16[160,768]{0,1:T(8,128)(2,1)} %collective-permute-done.4, f32[160]{0:T(256)S(1)} %add_rsqrt_fusion), kind=kLoop, calls=%fused_computation.19 | loop fusion | flops 368640 | bytes 492160 | tf_op jit(solution)/shard_map/convert_element_type | solution.py:238
  82.8 7.4 %all-to-all-done.1 = bf16[64,4,768]{2,1,0:T(4,128)(2,1)} async-done(((bf16[64,4,768]{2,1,0:T(4,128)(2,1)}), bf16[64,4,768]{2,1,0:T(4,128)(2,1)}, u32[]{:S(2)}, u32[]{:S(2)}) %all-to-all-start.1) | async-done | bytes 393248 | tf_op jit(solution)/shard_map/all_to_all | solution.py:275
  91.8 1.7 %collective-permute-start.13 = (bf16[128,256]{1,0:T(8,128)(2,1)S(1)}, bf16[128,256]{1,0:T(8,128)(2,1)S(1)}, u32[]{:S(2)}, u32[]{:S(2)}) collective-permute-start(bf16[128,256]{1,0:T(8,128)(2,1)S(1)} %get-tuple-element.34), channel_id=1, source_target_pairs={{0,192},{64,128},{128,64},{192,0},{1,193},{65,129},{129,65},{193,1... | collective-permute-start | bytes 196616 | tf_op jit(solution)/shard_map/ppermute | solution.py:53
  93.5 2.0 %maximum_bitcast_fusion.refs_0_ = bf16[768,640]{1,0:T(8,128)(2,1)S(1)} fusion(bf16[160,768]{0,1:T(8,128)(2,1)} %fusion.8, bf16[160,768]{0,1:T(8,128)(2,1)} %fusion.6, bf16[160,768]{0,1:T(8,128)(2,1)} %fusion.4, bf16[160,768]{0,1:T(8,128)(2,1)} %copy-done.7), kind=kLoop, calls=%fused_computation.3 | loop fusion | flops 3932160 | bytes 1966080 | tf_op jit(solution)/shard_map/transpose | solution.py:303
  95.6 1.5 shard_map.105.refs_1_
  97.1 3.0 %shard_map.107 = bf16[6912,128]{1,0:T(8,128)(2,1)} custom-call(bf16[768,640]{1,0:T(8,128)(2,1)S(1)} %maximum_bitcast_fusion.refs_0_, bf16[768,256]{1,0:T(8,128)(2,1)S(1)} %shard_map.105.refs_1_, bf16[128,256]{1,0:T(8,128)(2,1)S(1)} %get-tuple-element.31.refs_2_, bf16[128,256]{1,0:T(8,128)(2,1)S(1)} %collective-permute-done.11.refs_3_, ...), custom_call_target="tpu_custom_call" | custom-call | tf_op jit(solution)/shard_map/pallas_call | solution.py:308
  100.1 5.8 %all-to-all-start.2 = ((bf16[16,432,128]{2,1,0:T(8,128)(2,1)}), bf16[16,432,128]{2,1,0:T(8,128)(2,1)S(1)}, u32[]{:S(2)}, u32[]{:S(2)}) async-start(bf16[16,432,128]{2,1,0:T(8,128)(2,1)} %bitcast.8), calls=%async_computation.2 | async-start | bytes 3538944 | tf_op jit(solution)/shard_map/all_to_all | solution.py:317
  105.9 28.1 %all-to-all-done.2.terms_ref = bf16[16,432,128]{2,1,0:T(8,128)(2,1)S(1)} async-done(((bf16[16,432,128]{2,1,0:T(8,128)(2,1)}), bf16[16,432,128]{2,1,0:T(8,128)(2,1)S(1)}, u32[]{:S(2)}, u32[]{:S(2)}) %all-to-all-start.2) | async-done | bytes 1769504 | tf_op jit(solution)/shard_map/all_to_all | solution.py:317
  134.0 1.9 %collective-permute-start.14 = (bf16[16,768]{1,0:T(8,128)(2,1)S(1)}, bf16[16,768]{1,0:T(8,128)(2,1)S(1)}, u32[]{:S(2)}, u32[]{:S(2)}) collective-permute-start(bf16[16,768]{1,0:T(8,128)(2,1)S(1)} %get-tuple-element.48), channel_id=1, source_target_pairs={{0,1},{1,2},{2,3},{3,4},{4,5},{5,6},{6,7},{7,8},{8,9},{9,10},{10,1... | collective-permute-start | bytes 73736 | tf_op jit(solution)/shard_map/ppermute | solution.py:32
  135.9 9.0 %collective-permute-start.15 = (bf16[16,768]{1,0:T(8,128)(2,1)S(1)}, bf16[16,768]{1,0:T(8,128)(2,1)S(1)}, u32[]{:S(2)}, u32[]{:S(2)}) collective-permute-start(bf16[16,768]{1,0:T(8,128)(2,1)S(1)} %get-tuple-element.49), channel_id=1, source_target_pairs={{1,0},{2,1},{3,2},{4,3},{5,4},{6,5},{7,6},{8,7},{9,8},{10,9},{11,1... | collective-permute-start | bytes 73736 | tf_op jit(solution)/shard_map/ppermute | solution.py:33
  146.0 3.3 %all-to-all-start.3 = ((bf16[4,144,128]{2,1,0:T(8,128)(2,1)}), bf16[4,144,128]{2,1,0:T(8,128)(2,1)S(1)}, u32[]{:S(2)}, u32[]{:S(2)}) async-start(bf16[4,144,128]{2,1,0:T(8,128)(2,1)} %shard_map.108), calls=%async_computation.3 | async-start | bytes 294912 | tf_op jit(solution)/shard_map/all_to_all | solution.py:334
  149.4 4.4 %fusion.27 = f32[160,3840]{0,1:T(8,128)S(1)} fusion(bf16[3840,768]{1,0:T(8,128)(2,1)} %param.10, bf16[16,768]{1,0:T(8,128)(2,1)S(1)} %collective-permute-done.15, bf16[128,768]{1,0:T(8,128)(2,1)S(1)} %get-tuple-element.36, bf16[16,768]{1,0:T(8,128)(2,1)S(1)} %collective-permute-done.14), kind=kOutput, calls=%fused_computation.57 | convolution fusion | flops 944455680 | bytes 8601600 | tf_op jit(solution)/shard_map/dot_general | solution.py:360
  155.3 2.9 %all-to-all-done.3 = bf16[4,144,128]{2,1,0:T(8,128)(2,1)S(1)} async-done(((bf16[4,144,128]{2,1,0:T(8,128)(2,1)}), bf16[4,144,128]{2,1,0:T(8,128)(2,1)S(1)}, u32[]{:S(2)}, u32[]{:S(2)}) %all-to-all-start.3) | async-done | bytes 147488 | tf_op jit(solution)/shard_map/all_to_all | solution.py:334
  (94 shorter events, 24.9 us)
Async XLA Ops:
  1.7 28.7 %copy-start.8 = (bf16[1,128,768]{1,2,0:T(8,128)(2,1)}, bf16[1,128,768]{1,2,0:T(8,128)(2,1)S(1)}, u32[]{:S(2)}) copy-start(bf16[1,128,768]{1,2,0:T(8,128)(2,1)S(1)} %copy.20) | copy-start | bytes 589828
  1.9 17.0 %collective-permute-start = (bf16[16,768]{0,1:T(8,128)(2,1)S(1)}, bf16[16,768]{0,1:T(8,128)(2,1)S(1)}, u32[]{:S(2)}, u32[]{:S(2)}) collective-permute-start(bf16[16,768]{0,1:T(8,128)(2,1)S(1)} %get-tuple-element.50), channel_id=1, source_target_pairs={{0,1},{1,2},{2,3},{3,4},{4,5},{5,6},{6,7},{7,8},{8,9},{9,10},{10,1... | collective-permute-start | bytes 73736 | tf_op jit(solution)/shard_map/ppermute | solution.py:32
  5.3 17.5 %collective-permute-start.1 = (bf16[16,768]{0,1:T(8,128)(2,1)S(1)}, bf16[16,768]{0,1:T(8,128)(2,1)S(1)}, u32[]{:S(2)}, u32[]{:S(2)}) collective-permute-start(bf16[16,768]{0,1:T(8,128)(2,1)S(1)} %get-tuple-element.51), channel_id=1, source_target_pairs={{1,0},{2,1},{3,2},{4,3},{5,4},{6,5},{7,6},{8,7},{9,8},{10,9},{11,1... | collective-permute-start | bytes 73736 | tf_op jit(solution)/shard_map/ppermute | solution.py:33
  23.8 21.0 %collective-permute-start.3 = (bf16[160,768]{0,1:T(8,128)(2,1)}, bf16[160,768]{0,1:T(8,128)(2,1)}, u32[]{:S(2)}, u32[]{:S(2)}) collective-permute-start(bf16[160,768]{0,1:T(8,128)(2,1)} %get-tuple-element.45), channel_id=1, source_target_pairs={{0,128},{64,192},{128,0},{192,64},{1,129},{65,193},{129,1},{193,65... | collective-permute-start | bytes 737288 | tf_op jit(solution)/shard_map/ppermute | solution.py:42
  25.8 19.0 %copy-start.11 = (bf16[768]{0:T(1024)(128)(2,1)S(1)}, bf16[768]{0:T(1024)(128)(2,1)}, u32[]{:S(2)}) copy-start(bf16[768]{0:T(1024)(128)(2,1)} %param.12) | copy-start | bytes 4612
  30.5 30.3 %copy-start = (bf16[768,768]{1,0:T(8,128)(2,1)S(1)}, bf16[768,768]{1,0:T(8,128)(2,1)}, u32[]{:S(2)}) copy-start(bf16[768,768]{1,0:T(8,128)(2,1)} %first_ref.1) | copy-start | bytes 3538948
  31.7 28.9 %all-to-all-start = ((bf16[64,4,896]{2,1,0:T(4,128)(2,1)}), bf16[64,4,896]{2,1,0:T(4,128)(2,1)S(1)}, u32[]{:S(2)}, u32[]{:S(2)}) async-start(bf16[64,4,896]{2,1,0:T(4,128)(2,1)} %reshape.97), calls=%async_computation | async-start | bytes 917504 | tf_op jit(solution)/shard_map/all_to_all | solution.py:257
  44.7 2.0 %collective-permute-start.2 = (bf16[160,768]{0,1:T(8,128)(2,1)}, bf16[160,768]{0,1:T(8,128)(2,1)S(1)}, u32[]{:S(2)}, u32[]{:S(2)}) collective-permute-start(bf16[160,768]{0,1:T(8,128)(2,1)} %get-tuple-element.45), channel_id=1, source_target_pairs={{0,64},{64,0},{128,192},{192,128},{1,65},{65,1},{129,193},{193,129... | collective-permute-start | bytes 737288 | tf_op jit(solution)/shard_map/ppermute | solution.py:38
  44.8 32.5 %collective-permute-start.4 = (bf16[160,768]{0,1:T(8,128)(2,1)}, bf16[160,768]{0,1:T(8,128)(2,1)}, u32[]{:S(2)}, u32[]{:S(2)}) collective-permute-start(bf16[160,768]{0,1:T(8,128)(2,1)} %collective-permute-done.3), channel_id=1, source_target_pairs={{0,64},{64,0},{128,192},{192,128},{1,65},{65,1},{129,193},{193,129... | collective-permute-start | bytes 737288 | tf_op jit(solution)/shard_map/ppermute | solution.py:38
  65.7 12.9 %collective-permute-start.6 = (bf16[256,768]{1,0:T(8,128)(2,1)S(1)}, bf16[256,768]{1,0:T(8,128)(2,1)S(1)}, u32[]{:S(2)}, u32[]{:S(2)}) collective-permute-start(bf16[256,768]{1,0:T(8,128)(2,1)S(1)} %get-tuple-element.23.refs_0_), channel_id=1, source_target_pairs={{0,128},{64,192},{128,0},{192,64},{1,129},{65,193},{129,1},{193,65... | collective-permute-start | bytes 1179656 | tf_op jit(solution)/shard_map/ppermute | solution.py:42
  67.1 28.5 %copy-start.3 = (bf16[256,256]{1,0:T(8,128)(2,1)S(1)}, bf16[256,256]{1,0:T(8,128)(2,1)}, u32[]{:S(2)}) copy-start(bf16[256,256]{1,0:T(8,128)(2,1)} %copy-done.2) | copy-start | bytes 393220
  67.9 22.2 %all-to-all-start.1 = ((bf16[64,4,768]{2,1,0:T(4,128)(2,1)}), bf16[64,4,768]{2,1,0:T(4,128)(2,1)}, u32[]{:S(2)}, u32[]{:S(2)}) async-start(bf16[64,4,768]{2,1,0:T(4,128)(2,1)} %reshape.100), calls=%async_computation.1 | async-start | bytes 786432 | tf_op jit(solution)/shard_map/all_to_all | solution.py:275
  78.5 17.1 %collective-permute-start.5 = (bf16[256,768]{1,0:T(8,128)(2,1)S(1)}, bf16[256,768]{1,0:T(8,128)(2,1)S(1)}, u32[]{:S(2)}, u32[]{:S(2)}) collective-permute-start(bf16[256,768]{1,0:T(8,128)(2,1)S(1)} %get-tuple-element.23.refs_0_), channel_id=1, source_target_pairs={{0,64},{64,0},{128,192},{192,128},{1,65},{65,1},{129,193},{193,129... | collective-permute-start | bytes 1179656 | tf_op jit(solution)/shard_map/ppermute | solution.py:38
  78.6 17.0 %collective-permute-start.7 = (bf16[256,768]{1,0:T(8,128)(2,1)S(1)}, bf16[256,768]{1,0:T(8,128)(2,1)S(1)}, u32[]{:S(2)}, u32[]{:S(2)}) collective-permute-start(bf16[256,768]{1,0:T(8,128)(2,1)S(1)} %collective-permute-done.6.refs_2_), channel_id=1, source_target_pairs={{0,64},{64,0},{128,192},{192,128},{1,65},{65,1},{129,193},{193,129... | collective-permute-start | bytes 1179656 | tf_op jit(solution)/shard_map/ppermute | solution.py:38
  79.1 12.5 %collective-permute-start.8 = (bf16[256,256]{1,0:T(8,128)(2,1)}, bf16[256,256]{1,0:T(8,128)(2,1)S(1)}, u32[]{:S(2)}, u32[]{:S(2)}) collective-permute-start(bf16[256,256]{1,0:T(8,128)(2,1)} %copy-done.6), channel_id=1, source_target_pairs={{0,64},{64,0},{128,192},{192,128},{1,65},{65,1},{129,193},{193,129... | collective-permute-start | bytes 393224 | tf_op jit(solution)/shard_map/ppermute | solution.py:53
  79.2 12.5 %collective-permute-start.9 = (bf16[256,256]{1,0:T(8,128)(2,1)}, bf16[256,256]{1,0:T(8,128)(2,1)S(1)}, u32[]{:S(2)}, u32[]{:S(2)}) collective-permute-start(bf16[256,256]{1,0:T(8,128)(2,1)} %copy-done.5), channel_id=1, source_target_pairs={{0,128},{64,192},{128,0},{192,64},{1,129},{65,193},{129,1},{193,65... | collective-permute-start | bytes 393224 | tf_op jit(solution)/shard_map/ppermute | solution.py:53
  79.9 11.9 %collective-permute-start.10 = (bf16[256,256]{1,0:T(8,128)(2,1)}, bf16[256,256]{1,0:T(8,128)(2,1)}, u32[]{:S(2)}, u32[]{:S(2)}) collective-permute-start(bf16[256,256]{1,0:T(8,128)(2,1)} %copy-done.4), channel_id=1, source_target_pairs={{0,192},{64,128},{128,64},{192,0},{1,193},{65,129},{129,65},{193,1... | collective-permute-start | bytes 393224 | tf_op jit(solution)/shard_map/ppermute | solution.py:53
  91.6 5.5 %collective-permute-start.11 = (bf16[128,256]{1,0:T(8,128)(2,1)S(1)}, bf16[128,256]{1,0:T(8,128)(2,1)S(1)}, u32[]{:S(2)}, u32[]{:S(2)}) collective-permute-start(bf16[128,256]{1,0:T(8,128)(2,1)S(1)} %get-tuple-element.32), channel_id=1, source_target_pairs={{0,64},{64,0},{128,192},{192,128},{1,65},{65,1},{129,193},{193,129... | collective-permute-start | bytes 196616 | tf_op jit(solution)/shard_map/ppermute | solution.py:53
  91.7 5.4 %collective-permute-start.12 = (bf16[128,256]{1,0:T(8,128)(2,1)S(1)}, bf16[128,256]{1,0:T(8,128)(2,1)S(1)}, u32[]{:S(2)}, u32[]{:S(2)}) collective-permute-start(bf16[128,256]{1,0:T(8,128)(2,1)S(1)} %get-tuple-element.33), channel_id=1, source_target_pairs={{0,128},{64,192},{128,0},{192,64},{1,129},{65,193},{129,1},{193,65... | collective-permute-start | bytes 196616 | tf_op jit(solution)/shard_map/ppermute | solution.py:53
  91.8 5.3 %collective-permute-start.13 = (bf16[128,256]{1,0:T(8,128)(2,1)S(1)}, bf16[128,256]{1,0:T(8,128)(2,1)S(1)}, u32[]{:S(2)}, u32[]{:S(2)}) collective-permute-start(bf16[128,256]{1,0:T(8,128)(2,1)S(1)} %get-tuple-element.34), channel_id=1, source_target_pairs={{0,192},{64,128},{128,64},{192,0},{1,193},{65,129},{129,65},{193,1... | collective-permute-start | bytes 196616 | tf_op jit(solution)/shard_map/ppermute | solution.py:53
  100.1 33.9 %all-to-all-start.2 = ((bf16[16,432,128]{2,1,0:T(8,128)(2,1)}), bf16[16,432,128]{2,1,0:T(8,128)(2,1)S(1)}, u32[]{:S(2)}, u32[]{:S(2)}) async-start(bf16[16,432,128]{2,1,0:T(8,128)(2,1)} %bitcast.8), calls=%async_computation.2 | async-start | bytes 3538944 | tf_op jit(solution)/shard_map/all_to_all | solution.py:317
  134.0 15.4 %collective-permute-start.14 = (bf16[16,768]{1,0:T(8,128)(2,1)S(1)}, bf16[16,768]{1,0:T(8,128)(2,1)S(1)}, u32[]{:S(2)}, u32[]{:S(2)}) collective-permute-start(bf16[16,768]{1,0:T(8,128)(2,1)S(1)} %get-tuple-element.48), channel_id=1, source_target_pairs={{0,1},{1,2},{2,3},{3,4},{4,5},{5,6},{6,7},{7,8},{8,9},{9,10},{10,1... | collective-permute-start | bytes 73736 | tf_op jit(solution)/shard_map/ppermute | solution.py:32
  135.9 13.4 %collective-permute-start.15 = (bf16[16,768]{1,0:T(8,128)(2,1)S(1)}, bf16[16,768]{1,0:T(8,128)(2,1)S(1)}, u32[]{:S(2)}, u32[]{:S(2)}) collective-permute-start(bf16[16,768]{1,0:T(8,128)(2,1)S(1)} %get-tuple-element.49), channel_id=1, source_target_pairs={{1,0},{2,1},{3,2},{4,3},{5,4},{6,5},{7,6},{8,7},{9,8},{10,9},{11,1... | collective-permute-start | bytes 73736 | tf_op jit(solution)/shard_map/ppermute | solution.py:33
  146.0 12.2 %all-to-all-start.3 = ((bf16[4,144,128]{2,1,0:T(8,128)(2,1)}), bf16[4,144,128]{2,1,0:T(8,128)(2,1)S(1)}, u32[]{:S(2)}, u32[]{:S(2)}) async-start(bf16[4,144,128]{2,1,0:T(8,128)(2,1)} %shard_map.108), calls=%async_computation.3 | async-start | bytes 294912 | tf_op jit(solution)/shard_map/all_to_all | solution.py:334
  (8 other events, 22.8 us)

commit v6 on v5

--- a/solution.py
+++ b/solution.py
@@ -48,40 +48,23 @@
     return field, core, z_side, swap_core(z_side)
 
 
-def dp_exchange(pieces):
-    return [pieces[0]] + [
-        lax.ppermute(pieces[flip], "dp", [(i, i ^ flip) for i in range(4)]) for flip in range(1, 4)
-    ]
-
-
-def split_columns(values, place, blocks_ref, outs):
-    tiles = [values[:, i * LANES : (i + 1) * LANES] for i in range(values.shape[1] // LANES)]
-    turned = [pltpu.roll(tile, LANES // 2, axis=1) for tile in tiles]
-    low = lax.broadcasted_iota(jnp.int32, tiles[0].shape, 1) < LANES // 2
-    for pair in range(2):
-        first, middle, last = range(3 * pair, 3 * pair + 3)
-        blocks = (
-            (tiles[first], jnp.where(low, tiles[middle], turned[middle])),
-            (
-                jnp.where(low, turned[middle], turned[last]),
-                jnp.where(low, turned[last], tiles[last]),
-            ),
-        )
-        for side, halves in enumerate(blocks):
-            blocks_ref[2 * pair + side] = jnp.concatenate(halves, axis=1).astype(jnp.bfloat16)
-    for flip, out in enumerate(outs):
-        out[...] = blocks_ref[place ^ flip]
-
-
-def grad_kernel(place_ref, hits_ref, back_ref, part_ref, slope_ref, grad_ref, *rest):
-    hidden_grad = part_ref[...] + contract_rows(hits_ref[...], back_ref[...])
-    grad = hidden_grad * slope_ref[...]
-    grad_ref[...] = grad.astype(jnp.bfloat16)
-    split_columns(grad, place_ref[0], rest[-1], rest[:-1])
-
-
-def pair_kernel(place_ref, got_ref, hidden_ref, first_ref, second_ref, cotangent_ref, *outs):
-    back_ref, part_ref, feature_ref = outs[:3]
+def dp_columns(field, width):
+    index = lax.axis_index("dp")
+    found = []
+    for flip in range(4):
+        piece = lax.dynamic_slice_in_dim(field, (index ^ flip) * width, width, axis=1)
+        if flip:
+            piece = lax.ppermute(piece, "dp", [(i, i ^ flip) for i in range(4)])
+        found.append(piece)
+    return found
+
+
+def tail_twice(values):
+    return jnp.concatenate([values, values[:, LANES:]], axis=1)
+
+
+def pair_kernel(got_ref, hidden_ref, first_ref, second_ref, cotangent_ref, *outs):
+    back_ref, part_ref, feature_ref, delta_ref = outs
     chan_count = hidden_ref.shape[1]
     slots = got_ref.shape[0]
     note = got_ref[:, chan_count:].astype(jnp.float32)
@@ -93,9 +76,10 @@
     feature = (donor * accept).astype(jnp.bfloat16)
     feature_ref[...] = feature
     head_preact = jnp.dot(feature, first_ref[...], preferred_element_type=jnp.float32)
-    delta = score * second_ref[...].astype(jnp.float32) * gelu_slope(head_preact)
-    split_columns(delta, place_ref[0], outs[-1], outs[3:-1])
-    delta = delta.astype(jnp.bfloat16)
+    delta = (score * second_ref[...].astype(jnp.float32) * gelu_slope(head_preact)).astype(
+        jnp.bfloat16
+    )
+    delta_ref[...] = delta
     feature_grad = lax.dot_general(
         delta, first_ref[...], (((1,), (1,)), ((), ())), preferred_element_type=jnp.float32
     )
@@ -105,21 +89,21 @@
 
 
 def head_kernel(scale, *refs):
-    term = contract_rows(refs[0][...], refs[4][...])
+    term = contract_rows(refs[4][...], refs[0][...])
     for feature, delta in zip(refs[1:4], refs[5:8], strict=True):
-        term = term + contract_rows(feature[...], delta[...])
-    refs[8][...] = (term * scale).astype(jnp.bfloat16)
+        term = term + contract_rows(delta[...], feature[...])
+    refs[8][...] = (term.T * scale).astype(jnp.bfloat16)
 
 
 def weight_kernel(scale, taps, grid, *refs):
     normed_ref, head_ref, grads, out_ref, tail_ref = refs[0], refs[1], refs[2:6], refs[6], refs[7]
     ys, zs, xs = grid
     chan_count = normed_ref.shape[0]
-    width = grads[0].shape[1]
+    width = 2 * LANES
     reach = (taps - 1) * DILATION
     share = tail_ref.shape[0] // (ys * zs * xs)
     chunk = share * zs + share * zs // 2
-    values = [ref[...].astype(jnp.float32) for ref in grads]
+    values = [tail_twice(ref[...].astype(jnp.float32)) for ref in grads]
 
     def put(first, block):
         tail_ref[first : first + block.shape[0], :] = block[:, LANES:]
@@ -145,7 +129,7 @@
             k * chan_count,
             jnp.dot(normed_ref[...], shifted, preferred_element_type=jnp.float32) * scale,
         )
-    put(taps * chan_count, head_ref[...].astype(jnp.float32))
+    put(taps * chan_count, tail_twice(head_ref[...].astype(jnp.float32)))
     low = lax.broadcasted_iota(jnp.int32, (share, LANES), 1) < LANES // 2
     for y in range(ys):
         for x in range(xs):
@@ -167,13 +151,12 @@
         out_ref[z, share:, :] = total[first : first + share].astype(jnp.bfloat16)
 
 
-def in_vmem(kernel, shapes, count, limit, scratch=(), scalars=0):
+def in_vmem(kernel, shapes, count, limit, scratch=()):
     spec = pl.BlockSpec(memory_space=pltpu.VMEM)
-    scalar = pl.BlockSpec(memory_space=pltpu.SMEM)
     return pl.pallas_call(
         kernel,
         out_shape=shapes,
-        in_specs=[scalar] * scalars + [spec] * count,
+        in_specs=[spec] * count,
         out_specs=jax.tree.map(lambda _: spec, shapes),
         scratch_shapes=scratch,
         compiler_params=pltpu.CompilerParams(vmem_limit_bytes=limit),
@@ -201,6 +184,7 @@
     pair_count = donor_row.shape[1]
     capacity = max(2, 2 * pair_count // shards)
     slots = shards * capacity
+    col_width = out_count // dp_count
 
     above, below = seq_halo(activations[0], reach_rows)
     owner = acceptor_owner[0, :, 0]
@@ -230,7 +214,8 @@
     hits, notes = lax.optimization_barrier((hits, notes))
 
     padded_input = jnp.concatenate([above, activations[0], below], axis=0)
-    padded_peers = dp_peers(padded_input)
+    core_input, z_input = swap_core(padded_input), swap_z(padded_input)
+    padded_peers = padded_input, core_input, z_input, swap_core(z_input)
 
     def normalise(field):
         values = field.astype(jnp.float32)
@@ -262,16 +247,17 @@
         tiled=True,
     ).reshape(slots, out_count + LANES)
     slot_shape = jax.ShapeDtypeStruct((slots, out_count), jnp.bfloat16)
-    place = lax.axis_index("dp").astype(jnp.int32).reshape(1)
-    back, part, feature, *delta = in_vmem(
+    back, part, feature, delta = in_vmem(
         pair_kernel,
-        (slot_shape, jax.ShapeDtypeStruct((row_count, out_count), jnp.float32), slot_shape)
-        + (jax.ShapeDtypeStruct((slots, 2 * LANES), jnp.bfloat16),) * dp_count,
+        (
+            slot_shape,
+            jax.ShapeDtypeStruct((row_count, out_count), jnp.float32),
+            slot_shape,
+            slot_shape,
+        ),
         5,
         KERNEL_VMEM,
-        [pltpu.VMEM((dp_count, slots, 2 * LANES), jnp.bfloat16)],
-        1,
-    )(place, got, hidden, head_first, head_second.reshape(1, out_count), hidden_cotangent[0])
+    )(got, hidden, head_first, head_second.reshape(1, out_count), hidden_cotangent[0])
     donor_grad = lax.all_to_all(
         back.reshape(shards, capacity, out_count),
         "seq",
@@ -280,23 +266,16 @@
         tiled=True,
     ).reshape(slots, out_count)
     feature_peers = dp_peers(feature)
-    delta_peers = dp_exchange(delta)
+    delta_peers = dp_columns(delta, col_width)
     head_term = in_vmem(
         functools.partial(head_kernel, 1.0 / math.sqrt(dp_count * pair_count * shards)),
-        jax.ShapeDtypeStruct((out_count, 2 * LANES), jnp.bfloat16),
+        jax.ShapeDtypeStruct((out_count, col_width), jnp.bfloat16),
         8,
         KERNEL_VMEM,
     )(*feature_peers, *delta_peers)
-    preact_grad, *grads = in_vmem(
-        grad_kernel,
-        (jax.ShapeDtypeStruct((row_count, out_count), jnp.bfloat16),)
-        + (jax.ShapeDtypeStruct((row_count, 2 * LANES), jnp.bfloat16),) * dp_count,
-        4,
-        KERNEL_VMEM,
-        [pltpu.VMEM((dp_count, row_count, 2 * LANES), jnp.bfloat16)],
-        1,
-    )(place, hits, donor_grad, part, slope)
-    grad_peers = dp_exchange(grads)
+    hidden_grad = part + contract_rows(hits, donor_grad)
+    preact_grad = (hidden_grad * slope).astype(jnp.bfloat16)
+    grad_peers = dp_columns(preact_grad, col_width)
 
     normed_all = jnp.concatenate(
         [padded] + [normalise(peer)[2] for peer in padded_peers[1:]], axis=0
@@ -314,6 +293,7 @@
         KERNEL_VMEM,
         [pltpu.VMEM((row_total, LANES), jnp.float32)],
     )(normed_all, head_term, *grad_peers)
+    term, halo_source = lax.optimization_barrier((term, preact_grad))
     terms = lax.all_to_all(
         term.reshape(ys * xs, chunk, LANES),
         "seq",
@@ -324,7 +304,6 @@
             [(y * zs + z) * xs + x for y in range(ys) for x in range(xs)] for z in range(zs)
         ],
     )
-    terms, halo_source = lax.optimization_barrier((terms, preact_grad))
     folded = in_vmem(
         functools.partial(fold_kernel, share, zs),
         jax.ShapeDtypeStruct((zs, 2 * share, LANES), jnp.bfloat16),

time: 160 us -> 157 us (0.981)
  the two profiles are of different devices: /device:TPU:24 before, /device:TPU:6 now
where the time goes in v6:
time: 157 us
  waiting for transfers between devices  57.6 us (37%)
  starting transfers between devices  57.1 us (36%)
  other arithmetic  14 us (9%)
  matrix products  12.1 us (8%)
  local copies, waits for them, and re-layouts  8.73 us (6%)
  Pallas kernels  5.96 us (4%)
    ppermute x2, waiting for transfers between devices, seq_halo(): lax.ppermute(cells[-width:], 'seq', [(i, i + 1) for i in range(count - 1)])  16.4 us
    all_to_all x1, starting transfers between devices, per_device(): lax.all_to_all(sent.reshape(shards, capacity, out_count + LANES), 'seq',...  13.3 us
    all_to_all x1, waiting for transfers between devices, per_device(): lax.all_to_all(sent.reshape(shards, capacity, out_count + LANES), 'seq',...  12.8 us
    ppermute x2, waiting for transfers between devices, swap_z(): return lax.ppermute(field, 'dp', [(0, 2), (1, 3), (2, 0), (3, 1)])  9.56 us
    ppermute x2, starting transfers between devices, seq_halo(): lax.ppermute(cells[-width:], 'seq', [(i, i + 1) for i in range(count - 1)])  9.49 us
    all_to_all x1, starting transfers between devices, per_device(): lax.all_to_all(back.reshape(shards, capacity, out_count), 'seq', split_ax...  9.12 us
    ppermute x2, waiting for transfers between devices, seq_halo(): lax.ppermute(cells[:width], 'seq', [(i + 1, i) for i in range(count - 1)])  8.88 us
    all_to_all x1, starting transfers between devices, per_device(): lax.all_to_all(folded, 'seq', split_axis=0, concat_axis=0, tiled=True, ax...  8.3 us
  transfers between devices with their start and end apart: 20, of which 7 were waited for; matrix products, arithmetic and copies ran while one was open for 20% of the time, Pallas kernels for 1%

profile of v6, /device:TPU:6, one launch (start us, length us, event | category | flops | bytes accessed | tf_op | source)
XLA Modules:
  0.0 156.5 jit_solution(2858413354983524774)
XLA Ops:
  1.9 5.1 %collective-permute-start = (bf16[16,768]{0,1:T(8,128)(2,1)S(1)}, bf16[16,768]{0,1:T(8,128)(2,1)S(1)}, u32[]{:S(2)}, u32[]{:S(2)}) collective-permute-start(bf16[16,768]{0,1:T(8,128)(2,1)S(1)} %get-tuple-element.42), channel_id=1, source_target_pairs={{0,1},{1,2},{2,3},{3,4},{4,5},{5,6},{6,7},{7,8},{8,9},{9,10},{10,1... | collective-permute-start | bytes 73736 | tf_op jit(solution)/shard_map/ppermute | solution.py:32
  7.0 1.9 %collective-permute-start.1 = (bf16[16,768]{0,1:T(8,128)(2,1)S(1)}, bf16[16,768]{0,1:T(8,128)(2,1)S(1)}, u32[]{:S(2)}, u32[]{:S(2)}) collective-permute-start(bf16[16,768]{0,1:T(8,128)(2,1)S(1)} %get-tuple-element.43), channel_id=1, source_target_pairs={{1,0},{2,1},{3,2},{4,3},{5,4},{6,5},{7,6},{8,7},{9,8},{10,9},{11,1... | collective-permute-start | bytes 73736 | tf_op jit(solution)/shard_map/ppermute | solution.py:33
  13.6 8.9 %collective-permute-done.1 = bf16[16,768]{0,1:T(8,128)(2,1)S(1)} collective-permute-done((bf16[16,768]{0,1:T(8,128)(2,1)S(1)}, bf16[16,768]{0,1:T(8,128)(2,1)S(1)}, u32[]{:S(2)}, u32[]{:S(2)}) %collective-permute-start.1) | collective-permute-done | bytes 24608 | tf_op jit(solution)/shard_map/ppermute | solution.py:33
  24.0 5.4 %fusion.21 = (f32[128,768]{1,0:T(8,128)}, bf16[128,768]{1,0:T(8,128)(2,1)S(1)}) fusion(bf16[128,3840]{0,1:T(8,128)(2,1)S(1)} %slice_dynamic-update-slice_fusion, bf16[3840,768]{1,0:T(8,128)(2,1)} %param.10), kind=kOutput, calls=%fused_computation.38 | convolution fusion | flops 762150912 | bytes 7471104 | tf_op jit(solution)/shard_map/dot_general | solution.py:234
  30.6 13.3 %all-to-all-start = ((bf16[64,4,896]{2,1,0:T(4,128)(2,1)}), bf16[64,4,896]{2,1,0:T(4,128)(2,1)S(1)}, u32[]{:S(2)}, u32[]{:S(2)}) async-start(bf16[64,4,896]{2,1,0:T(4,128)(2,1)} %reshape.93), calls=%async_computation | async-start | bytes 917504 | tf_op jit(solution)/shard_map/all_to_all | solution.py:242
  45.3 1.8 %fusion.8 = bf16[160,768]{0,1:T(8,128)(2,1)} fusion(bf16[160,768]{0,1:T(8,128)(2,1)} %collective-permute-done.3, f32[160]{0:T(256)S(1)} %add_rsqrt_fusion.1), kind=kLoop, calls=%fused_computation.20 | loop fusion | flops 368640 | bytes 492160 | tf_op jit(solution)/shard_map/convert_element_type | solution.py:223
  47.1 12.8 %all-to-all-done = bf16[64,4,896]{2,1,0:T(4,128)(2,1)S(1)} async-done(((bf16[64,4,896]{2,1,0:T(4,128)(2,1)}), bf16[64,4,896]{2,1,0:T(4,128)(2,1)S(1)}, u32[]{:S(2)}, u32[]{:S(2)}) %all-to-all-start) | async-done | bytes 458784 | tf_op jit(solution)/shard_map/all_to_all | solution.py:242
  60.9 1.4 shard_map.104
  63.1 9.1 %all-to-all-start.1 = ((bf16[64,4,768]{2,1,0:T(4,128)(2,1)}), bf16[64,4,768]{2,1,0:T(4,128)(2,1)}, u32[]{:S(2)}, u32[]{:S(2)}) async-start(bf16[64,4,768]{2,1,0:T(4,128)(2,1)} %reshape.96), calls=%async_computation.1 | async-start | bytes 786432 | tf_op jit(solution)/shard_map/all_to_all | solution.py:261
  73.3 1.1 fusion.9
  74.5 1.5 collective-permute-start.6
  75.9 1.8 %fusion.10 = bf16[160,768]{0,1:T(8,128)(2,1)} fusion(bf16[160,768]{0,1:T(8,128)(2,1)} %collective-permute-done.4, f32[160]{0:T(256)S(1)} %add_rsqrt_fusion), kind=kLoop, calls=%fused_computation.22 | loop fusion | flops 368640 | bytes 492160 | tf_op jit(solution)/shard_map/convert_element_type | solution.py:223
  79.5 1.4 collective-permute-start.9
  80.9 9.6 %collective-permute-done.6.refs_2_ = bf16[256,768]{1,0:T(8,128)(2,1)S(1)} collective-permute-done((bf16[256,768]{1,0:T(8,128)(2,1)S(1)}, bf16[256,768]{1,0:T(8,128)(2,1)S(1)}, u32[]{:S(2)}, u32[]{:S(2)}) %collective-permute-start.6) | collective-permute-done | bytes 393248 | tf_op jit(solution)/shard_map/ppermute | solution.py:42
  91.5 1.3 fusion.1
  95.8 1.9 %maximum_bitcast_fusion.refs_0_ = bf16[768,640]{1,0:T(8,128)(2,1)S(1)} fusion(bf16[160,768]{0,1:T(8,128)(2,1)} %fusion.10, bf16[160,768]{0,1:T(8,128)(2,1)} %fusion.8, bf16[160,768]{0,1:T(8,128)(2,1)S(1)} %fusion.6, bf16[160,768]{0,1:T(8,128)(2,1)} %copy-done.2), kind=kLoop, calls=%fused_computation.6 | loop fusion | flops 3932160 | bytes 1966080 | tf_op jit(solution)/shard_map/transpose | solution.py:282
  99.4 3.0 %shard_map.106 = bf16[6912,128]{1,0:T(8,128)(2,1)} custom-call(bf16[768,640]{1,0:T(8,128)(2,1)S(1)} %maximum_bitcast_fusion.refs_0_, bf16[768,192]{1,0:T(8,128)(2,1)S(1)} %shard_map.105.refs_1_, bf16[128,192]{1,0:T(8,128)(2,1)S(1)} %get-tuple-element.41.refs_2_, bf16[128,192]{1,0:T(8,128)(2,1)S(1)} %collective-permute-done.11.refs_3_, ...), custom_call_target="tpu_custom_call" | custom-call | tf_op jit(solution)/shard_map/pallas_call | solution.py:287
  102.4 7.5 %all-to-all-start.2 = ((bf16[16,432,128]{2,1,0:T(8,128)(2,1)}), bf16[16,432,128]{2,1,0:T(8,128)(2,1)S(1)}, u32[]{:S(2)}, u32[]{:S(2)}) async-start(bf16[16,432,128]{2,1,0:T(8,128)(2,1)} %bitcast.10), calls=%async_computation.2 | async-start | bytes 3538944 | tf_op jit(solution)/shard_map/all_to_all | solution.py:297
  109.9 4.4 %collective-permute-start.14 = (bf16[16,768]{1,0:T(8,128)(2,1)S(1)}, bf16[16,768]{1,0:T(8,128)(2,1)S(1)}, u32[]{:S(2)}, u32[]{:S(2)}) collective-permute-start(bf16[16,768]{1,0:T(8,128)(2,1)S(1)} %get-tuple-element.36), channel_id=1, source_target_pairs={{0,1},{1,2},{2,3},{3,4},{4,5},{5,6},{6,7},{7,8},{8,9},{9,10},{10,1... | collective-permute-start | bytes 73736 | tf_op jit(solution)/shard_map/ppermute | solution.py:32
  114.3 1.9 %collective-permute-start.15 = (bf16[16,768]{1,0:T(8,128)(2,1)S(1)}, bf16[16,768]{1,0:T(8,128)(2,1)S(1)}, u32[]{:S(2)}, u32[]{:S(2)}) collective-permute-start(bf16[16,768]{1,0:T(8,128)(2,1)S(1)} %get-tuple-element.37), channel_id=1, source_target_pairs={{1,0},{2,1},{3,2},{4,3},{5,4},{6,5},{7,6},{8,7},{9,8},{10,9},{11,1... | collective-permute-start | bytes 73736 | tf_op jit(solution)/shard_map/ppermute | solution.py:33
  116.4 16.4 %collective-permute-done.14 = bf16[16,768]{1,0:T(8,128)(2,1)S(1)} collective-permute-done((bf16[16,768]{1,0:T(8,128)(2,1)S(1)}, bf16[16,768]{1,0:T(8,128)(2,1)S(1)}, u32[]{:S(2)}, u32[]{:S(2)}) %collective-permute-start.14) | collective-permute-done | bytes 24608 | tf_op jit(solution)/shard_map/ppermute | solution.py:32
  132.8 4.4 %fusion.29 = f32[160,3840]{0,1:T(8,128)S(1)} fusion(bf16[3840,768]{1,0:T(8,128)(2,1)} %param.10, bf16[16,768]{1,0:T(8,128)(2,1)S(1)} %collective-permute-done.15, bf16[128,768]{1,0:T(8,128)(2,1)S(1)} %fusion.1, bf16[16,768]{1,0:T(8,128)(2,1)S(1)} %collective-permute-done.14), kind=kOutput, calls=%fused_computation.60 | convolution fusion | flops 944455680 | bytes 8601600 | tf_op jit(solution)/shard_map/dot_general | solution.py:339
  138.6 8.3 %all-to-all-start.3 = ((bf16[4,144,128]{2,1,0:T(8,128)(2,1)}), bf16[4,144,128]{2,1,0:T(8,128)(2,1)S(1)}, u32[]{:S(2)}, u32[]{:S(2)}) async-start(bf16[4,144,128]{2,1,0:T(8,128)(2,1)} %shard_map.107), calls=%async_computation.3 | async-start | bytes 294912 | tf_op jit(solution)/shard_map/all_to_all | solution.py:313
  147.8 8.0 %all-to-all-done.3 = bf16[4,144,128]{2,1,0:T(8,128)(2,1)S(1)} async-done(((bf16[4,144,128]{2,1,0:T(8,128)(2,1)}), bf16[4,144,128]{2,1,0:T(8,128)(2,1)S(1)}, u32[]{:S(2)}, u32[]{:S(2)}) %all-to-all-start.3) | async-done | bytes 147488 | tf_op jit(solution)/shard_map/all_to_all | solution.py:313
  (88 shorter events, 23.6 us)
Async XLA Ops:
  1.7 27.6 %copy-start.3 = (bf16[1,128,768]{1,2,0:T(8,128)(2,1)}, bf16[1,128,768]{1,2,0:T(8,128)(2,1)S(1)}, u32[]{:S(2)}) copy-start(bf16[1,128,768]{1,2,0:T(8,128)(2,1)S(1)} %copy.20) | copy-start | bytes 589828
  1.9 11.7 %collective-permute-start = (bf16[16,768]{0,1:T(8,128)(2,1)S(1)}, bf16[16,768]{0,1:T(8,128)(2,1)S(1)}, u32[]{:S(2)}, u32[]{:S(2)}) collective-permute-start(bf16[16,768]{0,1:T(8,128)(2,1)S(1)} %get-tuple-element.42), channel_id=1, source_target_pairs={{0,1},{1,2},{2,3},{3,4},{4,5},{5,6},{6,7},{7,8},{8,9},{9,10},{10,1... | collective-permute-start | bytes 73736 | tf_op jit(solution)/shard_map/ppermute | solution.py:32
  7.0 15.5 %collective-permute-start.1 = (bf16[16,768]{0,1:T(8,128)(2,1)S(1)}, bf16[16,768]{0,1:T(8,128)(2,1)S(1)}, u32[]{:S(2)}, u32[]{:S(2)}) collective-permute-start(bf16[16,768]{0,1:T(8,128)(2,1)S(1)} %get-tuple-element.43), channel_id=1, source_target_pairs={{1,0},{2,1},{3,2},{4,3},{5,4},{6,5},{7,6},{8,7},{9,8},{10,9},{11,1... | collective-permute-start | bytes 73736 | tf_op jit(solution)/shard_map/ppermute | solution.py:33
  11.4 18.0 %copy-start.6 = (bf16[256,128]{1,0:T(8,128)(2,1)}, bf16[256,128]{1,0:T(8,128)(2,1)S(1)}, u32[]{:S(2)}) copy-start(bf16[256,128]{1,0:T(8,128)(2,1)S(1)} %fusion.36) | copy-start | bytes 196612
  22.7 21.1 %collective-permute-start.3 = (bf16[160,768]{0,1:T(8,128)(2,1)S(1)}, bf16[160,768]{0,1:T(8,128)(2,1)}, u32[]{:S(2)}, u32[]{:S(2)}) collective-permute-start(bf16[160,768]{0,1:T(8,128)(2,1)S(1)} %get-tuple-element.29), channel_id=1, source_target_pairs={{0,128},{64,192},{128,0},{192,64},{1,129},{65,193},{129,1},{193,65... | collective-permute-start | bytes 737288 | tf_op jit(solution)/shard_map/ppermute | solution.py:42
  22.8 22.3 %collective-permute-start.2 = (bf16[160,768]{0,1:T(8,128)(2,1)S(1)}, bf16[160,768]{0,1:T(8,128)(2,1)S(1)}, u32[]{:S(2)}, u32[]{:S(2)}) collective-permute-start(bf16[160,768]{0,1:T(8,128)(2,1)S(1)} %get-tuple-element.29), channel_id=1, source_target_pairs={{0,64},{64,0},{128,192},{192,128},{1,65},{65,1},{129,193},{193,129... | collective-permute-start | bytes 737288 | tf_op jit(solution)/shard_map/ppermute | solution.py:38
  29.4 30.6 %copy-start = (bf16[768,768]{1,0:T(8,128)(2,1)S(1)}, bf16[768,768]{1,0:T(8,128)(2,1)}, u32[]{:S(2)}) copy-start(bf16[768,768]{1,0:T(8,128)(2,1)} %first_ref.1) | copy-start | bytes 3538948
  30.6 29.3 %all-to-all-start = ((bf16[64,4,896]{2,1,0:T(4,128)(2,1)}), bf16[64,4,896]{2,1,0:T(4,128)(2,1)S(1)}, u32[]{:S(2)}, u32[]{:S(2)}) async-start(bf16[64,4,896]{2,1,0:T(4,128)(2,1)} %reshape.93), calls=%async_computation | async-start | bytes 917504 | tf_op jit(solution)/shard_map/all_to_all | solution.py:242
  43.9 29.4 %collective-permute-start.4 = (bf16[160,768]{0,1:T(8,128)(2,1)}, bf16[160,768]{0,1:T(8,128)(2,1)}, u32[]{:S(2)}, u32[]{:S(2)}) collective-permute-start(bf16[160,768]{0,1:T(8,128)(2,1)} %collective-permute-done.3), channel_id=1, source_target_pairs={{0,64},{64,0},{128,192},{192,128},{1,65},{65,1},{129,193},{193,129... | collective-permute-start | bytes 737288 | tf_op jit(solution)/shard_map/ppermute | solution.py:38
  63.1 27.3 %all-to-all-start.1 = ((bf16[64,4,768]{2,1,0:T(4,128)(2,1)}), bf16[64,4,768]{2,1,0:T(4,128)(2,1)}, u32[]{:S(2)}, u32[]{:S(2)}) async-start(bf16[64,4,768]{2,1,0:T(4,128)(2,1)} %reshape.96), calls=%async_computation.1 | async-start | bytes 786432 | tf_op jit(solution)/shard_map/all_to_all | solution.py:261
  74.5 16.0 %collective-permute-start.6 = (bf16[256,768]{1,0:T(8,128)(2,1)S(1)}, bf16[256,768]{1,0:T(8,128)(2,1)S(1)}, u32[]{:S(2)}, u32[]{:S(2)}) collective-permute-start(bf16[256,768]{1,0:T(8,128)(2,1)S(1)} %get-tuple-element.15.refs_0_), channel_id=1, source_target_pairs={{0,128},{64,192},{128,0},{192,64},{1,129},{65,193},{129,1},{193,65... | collective-permute-start | bytes 1179656 | tf_op jit(solution)/shard_map/ppermute | solution.py:42
  77.7 20.0 %collective-permute-start.5 = (bf16[256,768]{1,0:T(8,128)(2,1)S(1)}, bf16[256,768]{1,0:T(8,128)(2,1)S(1)}, u32[]{:S(2)}, u32[]{:S(2)}) collective-permute-start(bf16[256,768]{1,0:T(8,128)(2,1)S(1)} %get-tuple-element.15.refs_0_), channel_id=1, source_target_pairs={{0,64},{64,0},{128,192},{192,128},{1,65},{65,1},{129,193},{193,129... | collective-permute-start | bytes 1179656 | tf_op jit(solution)/shard_map/ppermute | solution.py:38
  78.7 14.3 %collective-permute-start.10 = (bf16[256,192]{1,0:T(8,128)(2,1)}, bf16[256,192]{1,0:T(8,128)(2,1)S(1)}, u32[]{:S(2)}, u32[]{:S(2)}) collective-permute-start(bf16[256,192]{1,0:T(8,128)(2,1)} %get-tuple-element.30), channel_id=1, source_target_pairs={{0,192},{64,128},{128,64},{192,0},{1,193},{65,129},{129,65},{193,1... | collective-permute-start | bytes 294920 | tf_op jit(solution)/shard_map/ppermute | solution.py:57
  79.5 15.7 %collective-permute-start.9 = (bf16[256,192]{1,0:T(8,128)(2,1)}, bf16[256,192]{1,0:T(8,128)(2,1)S(1)}, u32[]{:S(2)}, u32[]{:S(2)}) collective-permute-start(bf16[256,192]{1,0:T(8,128)(2,1)} %get-tuple-element.31), channel_id=1, source_target_pairs={{0,128},{64,192},{128,0},{192,64},{1,129},{65,193},{129,1},{193,65... | collective-permute-start | bytes 294920 | tf_op jit(solution)/shard_map/ppermute | solution.py:57
  80.9 15.0 %collective-permute-start.8 = (bf16[256,192]{1,0:T(8,128)(2,1)}, bf16[256,192]{1,0:T(8,128)(2,1)S(1)}, u32[]{:S(2)}, u32[]{:S(2)}) collective-permute-start(bf16[256,192]{1,0:T(8,128)(2,1)} %get-tuple-element.32), channel_id=1, source_target_pairs={{0,64},{64,0},{128,192},{192,128},{1,65},{65,1},{129,193},{193,129... | collective-permute-start | bytes 294920 | tf_op jit(solution)/shard_map/ppermute | solution.py:57
  90.4 7.3 %collective-permute-start.7 = (bf16[256,768]{1,0:T(8,128)(2,1)S(1)}, bf16[256,768]{1,0:T(8,128)(2,1)S(1)}, u32[]{:S(2)}, u32[]{:S(2)}) collective-permute-start(bf16[256,768]{1,0:T(8,128)(2,1)S(1)} %collective-permute-done.6.refs_2_), channel_id=1, source_target_pairs={{0,64},{64,0},{128,192},{192,128},{1,65},{65,1},{129,193},{193,129... | collective-permute-start | bytes 1179656 | tf_op jit(solution)/shard_map/ppermute | solution.py:38
  93.0 5.5 %collective-permute-start.13 = (bf16[128,192]{1,0:T(8,128)(2,1)S(1)}, bf16[128,192]{1,0:T(8,128)(2,1)S(1)}, u32[]{:S(2)}, u32[]{:S(2)}) collective-permute-start(bf16[128,192]{1,0:T(8,128)(2,1)S(1)} %get-tuple-element.38), channel_id=1, source_target_pairs={{0,192},{64,128},{128,64},{192,0},{1,193},{65,129},{129,65},{193,1... | collective-permute-start | bytes 147464 | tf_op jit(solution)/shard_map/ppermute | solution.py:57
  95.2 4.3 %collective-permute-start.12 = (bf16[128,192]{1,0:T(8,128)(2,1)S(1)}, bf16[128,192]{1,0:T(8,128)(2,1)S(1)}, u32[]{:S(2)}, u32[]{:S(2)}) collective-permute-start(bf16[128,192]{1,0:T(8,128)(2,1)S(1)} %get-tuple-element.39), channel_id=1, source_target_pairs={{0,128},{64,192},{128,0},{192,64},{1,129},{65,193},{129,1},{193,65... | collective-permute-start | bytes 147464 | tf_op jit(solution)/shard_map/ppermute | solution.py:57
  95.8 3.6 %collective-permute-start.11 = (bf16[128,192]{1,0:T(8,128)(2,1)S(1)}, bf16[128,192]{1,0:T(8,128)(2,1)S(1)}, u32[]{:S(2)}, u32[]{:S(2)}) collective-permute-start(bf16[128,192]{1,0:T(8,128)(2,1)S(1)} %get-tuple-element.40), channel_id=1, source_target_pairs={{0,64},{64,0},{128,192},{192,128},{1,65},{65,1},{129,193},{193,129... | collective-permute-start | bytes 147464 | tf_op jit(solution)/shard_map/ppermute | solution.py:57
  102.4 35.2 %all-to-all-start.2 = ((bf16[16,432,128]{2,1,0:T(8,128)(2,1)}), bf16[16,432,128]{2,1,0:T(8,128)(2,1)S(1)}, u32[]{:S(2)}, u32[]{:S(2)}) async-start(bf16[16,432,128]{2,1,0:T(8,128)(2,1)} %bitcast.10), calls=%async_computation.2 | async-start | bytes 3538944 | tf_op jit(solution)/shard_map/all_to_all | solution.py:297
  109.9 22.8 %collective-permute-start.14 = (bf16[16,768]{1,0:T(8,128)(2,1)S(1)}, bf16[16,768]{1,0:T(8,128)(2,1)S(1)}, u32[]{:S(2)}, u32[]{:S(2)}) collective-permute-start(bf16[16,768]{1,0:T(8,128)(2,1)S(1)} %get-tuple-element.36), channel_id=1, source_target_pairs={{0,1},{1,2},{2,3},{3,4},{4,5},{5,6},{6,7},{7,8},{8,9},{9,10},{10,1... | collective-permute-start | bytes 73736 | tf_op jit(solution)/shard_map/ppermute | solution.py:32
  114.3 18.4 %collective-permute-start.15 = (bf16[16,768]{1,0:T(8,128)(2,1)S(1)}, bf16[16,768]{1,0:T(8,128)(2,1)S(1)}, u32[]{:S(2)}, u32[]{:S(2)}) collective-permute-start(bf16[16,768]{1,0:T(8,128)(2,1)S(1)} %get-tuple-element.37), channel_id=1, source_target_pairs={{1,0},{2,1},{3,2},{4,3},{5,4},{6,5},{7,6},{8,7},{9,8},{10,9},{11,1... | collective-permute-start | bytes 73736 | tf_op jit(solution)/shard_map/ppermute | solution.py:33
  116.4 20.8 %copy-start.4 = (bf16[1,128,768]{1,2,0:T(8,128)(2,1)S(1)}, bf16[1,128,768]{1,2,0:T(8,128)(2,1)}, u32[]{:S(2)}) copy-start(bf16[1,128,768]{1,2,0:T(8,128)(2,1)} %copy-done.3) | copy-start | bytes 589828
  138.6 17.2 %all-to-all-start.3 = ((bf16[4,144,128]{2,1,0:T(8,128)(2,1)}), bf16[4,144,128]{2,1,0:T(8,128)(2,1)S(1)}, u32[]{:S(2)}, u32[]{:S(2)}) async-start(bf16[4,144,128]{2,1,0:T(8,128)(2,1)} %shard_map.107), calls=%async_computation.3 | async-start | bytes 294912 | tf_op jit(solution)/shard_map/all_to_all | solution.py:313
  (4 other events, 22.2 us)

commit v7 on v6

--- a/solution.py
+++ b/solution.py
@@ -61,6 +61,41 @@
 
 def tail_twice(values):
     return jnp.concatenate([values, values[:, LANES:]], axis=1)
+
+
+def conv_kernel(taps, above_ref, input_ref, below_ref, hits_ref, notes_ref, weight_ref, *rest):
+    padded_ref, hidden_ref, slope_ref, sent_ref, held_ref, done = rest
+    row_count, chan_count = input_ref.shape
+    copies = []
+    for k in range(taps):
+        rows = pl.ds(k * chan_count, chan_count)
+        copies.append(pltpu.make_async_copy(weight_ref.at[rows], held_ref.at[rows], done.at[k]))
+        copies[-1].start()
+    values = jnp.concatenate([above_ref[...], input_ref[...], below_ref[...]], axis=0).astype(
+        jnp.float32
+    )
+    inverse = lax.rsqrt(jnp.mean(values * values, axis=1, keepdims=True) + 1e-05)
+    normed = values * inverse
+    padded_ref[...] = normed.astype(jnp.bfloat16)
+    preact = jnp.zeros((row_count, hidden_ref.shape[1]), jnp.float32)
+    for k in range(taps):
+        column = normed[k * DILATION : k * DILATION + row_count].astype(jnp.bfloat16)
+        copies[k].wait()
+        preact = preact + jnp.dot(
+            column,
+            held_ref[k * chan_count : (k + 1) * chan_count, :],
+            preferred_element_type=jnp.float32,
+        )
+    normal_cdf = 0.5 * (1.0 + lax.erf(preact * (1.0 / math.sqrt(2.0))))
+    density = jnp.exp(-0.5 * preact * preact) * (1.0 / math.sqrt(2.0 * math.pi))
+    hidden = (preact * normal_cdf).astype(jnp.bfloat16)
+    hidden_ref[...] = hidden
+    slope_ref[...] = normal_cdf + preact * density
+    out_count = hidden_ref.shape[1]
+    sent_ref[:, :out_count] = jnp.dot(
+        hits_ref[...], hidden, preferred_element_type=jnp.float32
+    ).astype(jnp.bfloat16)
+    sent_ref[:, out_count:] = notes_ref[...]
 
 
 def pair_kernel(got_ref, hidden_ref, first_ref, second_ref, cotangent_ref, *outs):
@@ -220,25 +255,25 @@
     def normalise(field):
         values = field.astype(jnp.float32)
         inverse = lax.rsqrt(jnp.mean(values * values, axis=1, keepdims=True) + 1e-05)
-        return values, inverse, (values * inverse).astype(jnp.bfloat16)
-
-    _, padded_inverse, padded = normalise(padded_input)
-    norm_inverse = padded_inverse[reach_rows : reach_rows + row_count]
-
-    def tap_columns(field):
-        return jnp.concatenate(
-            [field[k * DILATION : k * DILATION + row_count] for k in range(tap_count)], axis=1
-        )
-
-    columns = tap_columns(padded)
-    preact = jnp.dot(columns, conv_weight, preferred_element_type=jnp.float32)
-    hidden = jax.nn.gelu(preact, approximate=False).astype(jnp.bfloat16)
-    slope = gelu_slope(preact)
-    hidden, slope = lax.optimization_barrier((hidden, slope))
-
-    sent = jnp.concatenate(
-        [jnp.dot(hits, hidden, preferred_element_type=jnp.float32).astype(jnp.bfloat16), notes], axis=1
-    )
+        return (values * inverse).astype(jnp.bfloat16)
+
+    spec = pl.BlockSpec(memory_space=pltpu.VMEM)
+    padded, hidden, slope, sent = pl.pallas_call(
+        functools.partial(conv_kernel, tap_count),
+        out_shape=(
+            jax.ShapeDtypeStruct((row_count + 2 * reach_rows, chan_count), jnp.bfloat16),
+            jax.ShapeDtypeStruct((row_count, out_count), jnp.bfloat16),
+            jax.ShapeDtypeStruct((row_count, out_count), jnp.float32),
+            jax.ShapeDtypeStruct((slots, out_count + LANES), jnp.bfloat16),
+        ),
+        in_specs=[spec] * 5 + [pl.BlockSpec(memory_space=pl.ANY)],
+        out_specs=(spec,) * 4,
+        scratch_shapes=[
+            pltpu.VMEM(conv_weight.shape, jnp.bfloat16),
+            pltpu.SemaphoreType.DMA((tap_count,)),
+        ],
+        compiler_params=pltpu.CompilerParams(vmem_limit_bytes=KERNEL_VMEM),
+    )(above, activations[0], below, hits, notes, conv_weight)
     got = lax.all_to_all(
         sent.reshape(shards, capacity, out_count + LANES),
         "seq",
@@ -276,9 +311,10 @@
     hidden_grad = part + contract_rows(hits, donor_grad)
     preact_grad = (hidden_grad * slope).astype(jnp.bfloat16)
     grad_peers = dp_columns(preact_grad, col_width)
+    grad_above, grad_below = seq_halo(preact_grad, reach_rows)
 
     normed_all = jnp.concatenate(
-        [padded] + [normalise(peer)[2] for peer in padded_peers[1:]], axis=0
+        [padded] + [normalise(peer) for peer in padded_peers[1:]], axis=0
     ).T
     ys, zs, xs = SEQ_GRID
     row_total = tap_count * chan_count + out_count
@@ -293,7 +329,6 @@
         KERNEL_VMEM,
         [pltpu.VMEM((row_total, LANES), jnp.float32)],
     )(normed_all, head_term, *grad_peers)
-    term, halo_source = lax.optimization_barrier((term, preact_grad))
     terms = lax.all_to_all(
         term.reshape(ys * xs, chunk, LANES),
         "seq",
@@ -326,15 +361,18 @@
     weight_grads = jnp.concatenate([total[:share], others], axis=1)
 
     input_grad = data_grad(
-        activations[0], norm_inverse, halo_source, conv_weight, reach_rows, tap_count
+        activations[0], grad_above, preact_grad, grad_below, conv_weight, tap_count
     )
     return (input_grad.astype(jnp.bfloat16)[None], weight_grads)
 
 
-def data_grad(inputs, norm_inverse, preact_grad, conv_weight, reach_rows, tap_count):
+def data_grad(inputs, grad_above, preact_grad, grad_below, conv_weight, tap_count):
+    reach_rows = grad_above.shape[0]
     row_count, chan_count = inputs.shape
     input_values = inputs.astype(jnp.float32)
-    grad_above, grad_below = seq_halo(preact_grad, reach_rows)
+    norm_inverse = lax.rsqrt(
+        jnp.mean(input_values * input_values, axis=1, keepdims=True) + 1e-05
+    )
     grad_padded = jnp.concatenate([grad_above, preact_grad, grad_below], axis=0)
     spread = lax.dot_general(
         grad_padded, conv_weight, (((1,), (1,)), ((), ())), preferred_element_type=jnp.float32

time: 157 us -> 157 us (level)
  the two profiles are of different devices: /device:TPU:6 before, /device:TPU:24 now
where the time goes in v7:
time: 157 us; the launch traced here: 154 us
  starting transfers between devices  55.6 us (35%)
  waiting for transfers between devices  54 us (34%)
  other arithmetic  16.5 us (11%)
  local copies, waits for them, and re-layouts  12.5 us (8%)
  Pallas kernels  9.01 us (6%)
  matrix products  5.76 us (4%)
    ppermute x2, waiting for transfers between devices, seq_halo(): lax.ppermute(cells[-width:], 'seq', [(i, i + 1) for i in range(count - 1)])  18.2 us
    ppermute x2, starting transfers between devices, seq_halo(): lax.ppermute(cells[:width], 'seq', [(i + 1, i) for i in range(count - 1)])  18.2 us
    all_to_all x1, waiting for transfers between devices, per_device(): lax.all_to_all(sent.reshape(shards, capacity, out_count + LANES), 'seq',...  12.5 us
    ppermute x2, waiting for transfers between devices, swap_z(): return lax.ppermute(field, 'dp', [(0, 2), (1, 3), (2, 0), (3, 1)])  9.43 us
    all_to_all x1, waiting for transfers between devices, per_device(): lax.all_to_all(folded, 'seq', split_axis=0, concat_axis=0, tiled=True, ax...  7.7 us
    all_to_all x1, starting transfers between devices, per_device(): lax.all_to_all(back.reshape(shards, capacity, out_count), 'seq', split_ax...  7.62 us
    all_to_all x1, starting transfers between devices, per_device(): lax.all_to_all(term.reshape(ys * xs, chunk, LANES), 'seq', split_axis=0,...  7.14 us
    all_to_all x1, starting transfers between devices, per_device(): lax.all_to_all(sent.reshape(shards, capacity, out_count + LANES), 'seq',...  6.42 us
  transfers between devices with their start and end apart: 20, of which 8 were waited for; matrix products, arithmetic and copies ran while one was open for 18% of the time, Pallas kernels for 3%

profile of v7, /device:TPU:24, one launch (start us, length us, event | category | flops | bytes accessed | tf_op | source)
XLA Modules:
  0.0 154.5 jit_solution(8464284659174305866)
XLA Ops:
  1.9 10.6 %collective-permute-start.1 = (bf16[16,768]{0,1:T(8,128)(2,1)S(1)}, bf16[16,768]{0,1:T(8,128)(2,1)S(1)}, u32[]{:S(2)}, u32[]{:S(2)}) collective-permute-start(bf16[16,768]{0,1:T(8,128)(2,1)S(1)} %get-tuple-element.39), channel_id=1, source_target_pairs={{1,0},{2,1},{3,2},{4,3},{5,4},{6,5},{7,6},{8,7},{9,8},{10,9},{11,1... | collective-permute-start | bytes 73736 | tf_op jit(solution)/shard_map/ppermute | solution.py:33
  12.5 1.9 %collective-permute-start = (bf16[16,768]{0,1:T(8,128)(2,1)S(1)}, bf16[16,768]{0,1:T(8,128)(2,1)S(1)}, u32[]{:S(2)}, u32[]{:S(2)}) collective-permute-start(bf16[16,768]{0,1:T(8,128)(2,1)S(1)} %get-tuple-element.40), channel_id=1, source_target_pairs={{0,1},{1,2},{2,3},{3,4},{4,5},{5,6},{6,7},{7,8},{8,9},{9,10},{10,1... | collective-permute-start | bytes 73736 | tf_op jit(solution)/shard_map/ppermute | solution.py:32
  17.6 3.3 %collective-permute-done.1 = bf16[16,768]{0,1:T(8,128)(2,1)S(1)} collective-permute-done((bf16[16,768]{0,1:T(8,128)(2,1)S(1)}, bf16[16,768]{0,1:T(8,128)(2,1)S(1)}, u32[]{:S(2)}, u32[]{:S(2)}) %collective-permute-start.1) | collective-permute-done | bytes 24608 | tf_op jit(solution)/shard_map/ppermute | solution.py:33
  20.9 8.8 %collective-permute-done = bf16[16,768]{0,1:T(8,128)(2,1)S(1)} collective-permute-done((bf16[16,768]{0,1:T(8,128)(2,1)S(1)}, bf16[16,768]{0,1:T(8,128)(2,1)S(1)}, u32[]{:S(2)}, u32[]{:S(2)}) %collective-permute-start) | collective-permute-done | bytes 24608 | tf_op jit(solution)/shard_map/ppermute | solution.py:32
  31.2 2.7 %copy-done = bf16[3840,768]{1,0:T(8,128)(2,1)S(1)} copy-done((bf16[3840,768]{1,0:T(8,128)(2,1)S(1)}, bf16[3840,768]{1,0:T(8,128)(2,1)}, u32[]{:S(2)}) %copy-start) | copy-done | bytes 5898264
  33.8 3.1 %shard_map.104 = (bf16[160,768]{1,0:T(8,128)(2,1)S(1)}, bf16[128,768]{1,0:T(8,128)(2,1)S(1)}, f32[128,768]{1,0:T(8,128)S(1)}, bf16[256,896]{1,0:T(8,128)(2,1)S(1)}) custom-call(bf16[16,768]{1,0:T(8,128)(2,1)S(1)} %copy.27.above_ref, bf16[128,768]{1,0:T(8,128)(2,1)S(1)} %bitcast.22, bf16[16,768]{1,0:T(8,128)(2,1)S(1)} %copy.29.below_ref, ...), custom_call_target="tpu_custom_call" | custom-call | tf_op jit(solution)/shard_map/pallas_call | solution.py:261
  37.8 6.4 %all-to-all-start = ((bf16[64,4,896]{2,1,0:T(4,128)(2,1)}), bf16[64,4,896]{2,1,0:T(4,128)(2,1)S(1)}, u32[]{:S(2)}, u32[]{:S(2)}) async-start(bf16[64,4,896]{2,1,0:T(4,128)(2,1)} %reshape.84), calls=%async_computation | async-start | bytes 917504 | tf_op jit(solution)/shard_map/all_to_all | solution.py:277
  47.5 1.8 %fusion.4 = bf16[160,768]{0,1:T(8,128)(2,1)} fusion(bf16[160,768]{0,1:T(8,128)(2,1)} %collective-permute-done.5, f32[160]{0:T(256)S(1)} %add_rsqrt_fusion.1), kind=kLoop, calls=%fused_computation.12 | loop fusion | flops 368640 | bytes 492160 | tf_op jit(solution)/shard_map/convert_element_type | solution.py:258
  49.3 12.5 %all-to-all-done = bf16[64,4,896]{2,1,0:T(4,128)(2,1)S(1)} async-done(((bf16[64,4,896]{2,1,0:T(4,128)(2,1)}), bf16[64,4,896]{2,1,0:T(4,128)(2,1)S(1)}, u32[]{:S(2)}, u32[]{:S(2)}) %all-to-all-start) | async-done | bytes 458784 | tf_op jit(solution)/shard_map/all_to_all | solution.py:277
  65.9 7.6 %all-to-all-start.1 = ((bf16[64,4,768]{2,1,0:T(4,128)(2,1)}), bf16[64,4,768]{2,1,0:T(4,128)(2,1)}, u32[]{:S(2)}, u32[]{:S(2)}) async-start(bf16[64,4,768]{2,1,0:T(4,128)(2,1)} %reshape.87), calls=%async_computation.1 | async-start | bytes 786432 | tf_op jit(solution)/shard_map/all_to_all | solution.py:296
  73.5 1.8 %fusion.2 = bf16[160,768]{0,1:T(8,128)(2,1)} fusion(bf16[160,768]{0,1:T(8,128)(2,1)} %collective-permute-done.4, f32[160]{0:T(256)S(1)} %add_rsqrt_fusion.2), kind=kLoop, calls=%fused_computation.10 | loop fusion | flops 368640 | bytes 492160 | tf_op jit(solution)/shard_map/convert_element_type | solution.py:258
  77.3 1.8 %fusion.6 = bf16[160,768]{0,1:T(8,128)(2,1)} fusion(bf16[160,768]{0,1:T(8,128)(2,1)} %collective-permute-done.6, f32[160]{0:T(256)S(1)} %add_rsqrt_fusion), kind=kLoop, calls=%fused_computation.14 | loop fusion | flops 368640 | bytes 492160 | tf_op jit(solution)/shard_map/convert_element_type | solution.py:258
  82.3 9.4 %collective-permute-done.8.refs_2_ = bf16[256,768]{1,0:T(8,128)(2,1)S(1)} collective-permute-done((bf16[256,768]{1,0:T(8,128)(2,1)S(1)}, bf16[256,768]{1,0:T(8,128)(2,1)S(1)}, u32[]{:S(2)}, u32[]{:S(2)}) %collective-permute-start.8) | collective-permute-done | bytes 393248 | tf_op jit(solution)/shard_map/ppermute | solution.py:42
  91.7 1.9 %reshape.88 = bf16[256,768]{1,0:T(8,128)(2,1)} reshape(bf16[64,4,768]{2,1,0:T(4,128)(2,1)} %all-to-all-done.1) | data formatting | bytes 786432 | tf_op jit(solution)/shard_map/reshape | solution.py:302
  97.3 2.0 %maximum_bitcast_fusion.refs_0_ = bf16[768,640]{1,0:T(8,128)(2,1)S(1)} fusion(bf16[160,768]{0,1:T(8,128)(2,1)} %fusion.6, bf16[160,768]{0,1:T(8,128)(2,1)} %fusion.4, bf16[160,768]{0,1:T(8,128)(2,1)} %fusion.2, bf16[160,768]{0,1:T(8,128)(2,1)} %copy.35), kind=kLoop, calls=%fused_computation.2 | loop fusion | flops 3932160 | bytes 1966080 | tf_op jit(solution)/shard_map/transpose | solution.py:318
  101.0 3.0 %shard_map.107 = bf16[6912,128]{1,0:T(8,128)(2,1)} custom-call(bf16[768,640]{1,0:T(8,128)(2,1)S(1)} %maximum_bitcast_fusion.refs_0_, bf16[768,192]{1,0:T(8,128)(2,1)S(1)} %shard_map.106.refs_1_, bf16[128,192]{1,0:T(8,128)(2,1)S(1)} %get-tuple-element.36.refs_2_, bf16[128,192]{1,0:T(8,128)(2,1)S(1)} %collective-permute-done.13.refs_3_, ...), custom_call_target="tpu_custom_call" | custom-call | tf_op jit(solution)/shard_map/pallas_call | solution.py:323
  104.0 7.1 %all-to-all-start.2 = ((bf16[16,432,128]{2,1,0:T(8,128)(2,1)}), bf16[16,432,128]{2,1,0:T(8,128)(2,1)S(1)}, u32[]{:S(2)}, u32[]{:S(2)}) async-start(bf16[16,432,128]{2,1,0:T(8,128)(2,1)} %bitcast.9), calls=%async_computation.2 | async-start | bytes 3538944 | tf_op jit(solution)/shard_map/all_to_all | solution.py:332
  111.1 3.4 %collective-permute-start.2 = (bf16[16,768]{1,0:T(8,128)(2,1)S(1)}, bf16[16,768]{1,0:T(8,128)(2,1)S(1)}, u32[]{:S(2)}, u32[]{:S(2)}) collective-permute-start(bf16[16,768]{1,0:T(8,128)(2,1)S(1)} %get-tuple-element.37), channel_id=1, source_target_pairs={{0,1},{1,2},{2,3},{3,4},{4,5},{5,6},{6,7},{7,8},{8,9},{9,10},{10,1... | collective-permute-start | bytes 73736 | tf_op jit(solution)/shard_map/ppermute | solution.py:32
  114.5 7.6 %collective-permute-start.3 = (bf16[16,768]{1,0:T(8,128)(2,1)S(1)}, bf16[16,768]{1,0:T(8,128)(2,1)S(1)}, u32[]{:S(2)}, u32[]{:S(2)}) collective-permute-start(bf16[16,768]{1,0:T(8,128)(2,1)S(1)} %get-tuple-element.38), channel_id=1, source_target_pairs={{1,0},{2,1},{3,2},{4,3},{5,4},{6,5},{7,6},{8,7},{9,8},{10,9},{11,1... | collective-permute-start | bytes 73736 | tf_op jit(solution)/shard_map/ppermute | solution.py:33
  122.1 9.4 %collective-permute-done.2 = bf16[16,768]{1,0:T(8,128)(2,1)S(1)} collective-permute-done((bf16[16,768]{1,0:T(8,128)(2,1)S(1)}, bf16[16,768]{1,0:T(8,128)(2,1)S(1)}, u32[]{:S(2)}, u32[]{:S(2)}) %collective-permute-start.2) | collective-permute-done | bytes 24608 | tf_op jit(solution)/shard_map/ppermute | solution.py:32
  131.6 1.9 %collective-permute-done.3 = bf16[16,768]{1,0:T(8,128)(2,1)S(1)} collective-permute-done((bf16[16,768]{1,0:T(8,128)(2,1)S(1)}, bf16[16,768]{1,0:T(8,128)(2,1)S(1)}, u32[]{:S(2)}, u32[]{:S(2)}) %collective-permute-start.3) | collective-permute-done | bytes 24608 | tf_op jit(solution)/shard_map/ppermute | solution.py:33
  133.5 4.4 %fusion.12 = f32[160,3840]{0,1:T(8,128)S(1)} fusion(bf16[3840,768]{1,0:T(8,128)(2,1)} %weight_ref.1, bf16[16,768]{1,0:T(8,128)(2,1)S(1)} %collective-permute-done.3, bf16[128,768]{1,0:T(8,128)(2,1)S(1)} %multiply_convert_fusion, bf16[16,768]{1,0:T(8,128)(2,1)S(1)} %collective-permute-done.2), kind=kOutput, calls=%fused_computation.30 | convolution fusion | flops 944455680 | bytes 8601600 | tf_op jit(solution)/shard_map/dot_general | solution.py:377
  139.3 5.8 %all-to-all-start.3 = ((bf16[4,144,128]{2,1,0:T(8,128)(2,1)}), bf16[4,144,128]{2,1,0:T(8,128)(2,1)S(1)}, u32[]{:S(2)}, u32[]{:S(2)}) async-start(bf16[4,144,128]{2,1,0:T(8,128)(2,1)} %shard_map.108), calls=%async_computation.3 | async-start | bytes 294912 | tf_op jit(solution)/shard_map/all_to_all | solution.py:348
  146.0 7.7 %all-to-all-done.3 = bf16[4,144,128]{2,1,0:T(8,128)(2,1)S(1)} async-done(((bf16[4,144,128]{2,1,0:T(8,128)(2,1)}), bf16[4,144,128]{2,1,0:T(8,128)(2,1)S(1)}, u32[]{:S(2)}, u32[]{:S(2)}) %all-to-all-start.3) | async-done | bytes 147488 | tf_op jit(solution)/shard_map/all_to_all | solution.py:348
  (88 shorter events, 27.4 us)
Async XLA Ops:
  0.6 30.5 %copy-start.2 = (bf16[1,128,768]{2,1,0:T(8,128)(2,1)S(1)}, bf16[1,128,768]{2,1,0:T(8,128)(2,1)}, u32[]{:S(2)}) copy-start(bf16[1,128,768]{2,1,0:T(8,128)(2,1)} %param.9) | copy-start | bytes 589828
  0.6 30.2 %copy-start.10 = (bf16[768]{0:T(1024)(128)(2,1)S(1)}, bf16[768]{0:T(1024)(128)(2,1)}, u32[]{:S(2)}) copy-start(bf16[768]{0:T(1024)(128)(2,1)} %param.12) | copy-start | bytes 4612
  1.8 29.3 %copy-start.8 = (bf16[1,128,768]{1,2,0:T(8,128)(2,1)}, bf16[1,128,768]{1,2,0:T(8,128)(2,1)S(1)}, u32[]{:S(2)}) copy-start(bf16[1,128,768]{1,2,0:T(8,128)(2,1)S(1)} %copy.24) | copy-start | bytes 589828
  1.9 18.9 %collective-permute-start.1 = (bf16[16,768]{0,1:T(8,128)(2,1)S(1)}, bf16[16,768]{0,1:T(8,128)(2,1)S(1)}, u32[]{:S(2)}, u32[]{:S(2)}) collective-permute-start(bf16[16,768]{0,1:T(8,128)(2,1)S(1)} %get-tuple-element.39), channel_id=1, source_target_pairs={{1,0},{2,1},{3,2},{4,3},{5,4},{6,5},{7,6},{8,7},{9,8},{10,9},{11,1... | collective-permute-start | bytes 73736 | tf_op jit(solution)/shard_map/ppermute | solution.py:33
  12.5 17.1 %collective-permute-start = (bf16[16,768]{0,1:T(8,128)(2,1)S(1)}, bf16[16,768]{0,1:T(8,128)(2,1)S(1)}, u32[]{:S(2)}, u32[]{:S(2)}) collective-permute-start(bf16[16,768]{0,1:T(8,128)(2,1)S(1)} %get-tuple-element.40), channel_id=1, source_target_pairs={{0,1},{1,2},{2,3},{3,4},{4,5},{5,6},{6,7},{7,8},{8,9},{9,10},{10,1... | collective-permute-start | bytes 73736 | tf_op jit(solution)/shard_map/ppermute | solution.py:32
  30.7 14.5 %collective-permute-start.5 = (bf16[160,768]{0,1:T(8,128)(2,1)}, bf16[160,768]{0,1:T(8,128)(2,1)}, u32[]{:S(2)}, u32[]{:S(2)}) collective-permute-start(bf16[160,768]{0,1:T(8,128)(2,1)} %pad_maximum_fusion), channel_id=1, source_target_pairs={{0,128},{64,192},{128,0},{192,64},{1,129},{65,193},{129,1},{193,65... | collective-permute-start | bytes 737288 | tf_op jit(solution)/shard_map/ppermute | solution.py:42
  30.7 15.6 %collective-permute-start.4 = (bf16[160,768]{0,1:T(8,128)(2,1)}, bf16[160,768]{0,1:T(8,128)(2,1)}, u32[]{:S(2)}, u32[]{:S(2)}) collective-permute-start(bf16[160,768]{0,1:T(8,128)(2,1)} %pad_maximum_fusion), channel_id=1, source_target_pairs={{0,64},{64,0},{128,192},{192,128},{1,65},{65,1},{129,193},{193,129... | collective-permute-start | bytes 737288 | tf_op jit(solution)/shard_map/ppermute | solution.py:38
  37.8 24.1 %copy-start.5 = (bf16[1,128,768]{2,1,0:T(8,128)(2,1)S(1)}, bf16[1,128,768]{2,1,0:T(8,128)(2,1)}, u32[]{:S(2)}) copy-start(bf16[1,128,768]{2,1,0:T(8,128)(2,1)} %param.13) | copy-start | bytes 589828
  37.8 24.0 %all-to-all-start = ((bf16[64,4,896]{2,1,0:T(4,128)(2,1)}), bf16[64,4,896]{2,1,0:T(4,128)(2,1)S(1)}, u32[]{:S(2)}, u32[]{:S(2)}) async-start(bf16[64,4,896]{2,1,0:T(4,128)(2,1)} %reshape.84), calls=%async_computation | async-start | bytes 917504 | tf_op jit(solution)/shard_map/all_to_all | solution.py:277
  45.2 30.1 %collective-permute-start.6 = (bf16[160,768]{0,1:T(8,128)(2,1)}, bf16[160,768]{0,1:T(8,128)(2,1)}, u32[]{:S(2)}, u32[]{:S(2)}) collective-permute-start(bf16[160,768]{0,1:T(8,128)(2,1)} %collective-permute-done.5), channel_id=1, source_target_pairs={{0,64},{64,0},{128,192},{192,128},{1,65},{65,1},{129,193},{193,129... | collective-permute-start | bytes 737288 | tf_op jit(solution)/shard_map/ppermute | solution.py:38
  65.9 25.8 %all-to-all-start.1 = ((bf16[64,4,768]{2,1,0:T(4,128)(2,1)}), bf16[64,4,768]{2,1,0:T(4,128)(2,1)}, u32[]{:S(2)}, u32[]{:S(2)}) async-start(bf16[64,4,768]{2,1,0:T(4,128)(2,1)} %reshape.87), calls=%async_computation.1 | async-start | bytes 786432 | tf_op jit(solution)/shard_map/all_to_all | solution.py:296
  76.5 15.2 %collective-permute-start.8 = (bf16[256,768]{1,0:T(8,128)(2,1)S(1)}, bf16[256,768]{1,0:T(8,128)(2,1)S(1)}, u32[]{:S(2)}, u32[]{:S(2)}) collective-permute-start(bf16[256,768]{1,0:T(8,128)(2,1)S(1)} %get-tuple-element.20.refs_0_), channel_id=1, source_target_pairs={{0,128},{64,192},{128,0},{192,64},{1,129},{65,193},{129,1},{193,65... | collective-permute-start | bytes 1179656 | tf_op jit(solution)/shard_map/ppermute | solution.py:42
  79.1 20.2 %collective-permute-start.7 = (bf16[256,768]{1,0:T(8,128)(2,1)S(1)}, bf16[256,768]{1,0:T(8,128)(2,1)S(1)}, u32[]{:S(2)}, u32[]{:S(2)}) collective-permute-start(bf16[256,768]{1,0:T(8,128)(2,1)S(1)} %get-tuple-element.20.refs_0_), channel_id=1, source_target_pairs={{0,64},{64,0},{128,192},{192,128},{1,65},{65,1},{129,193},{193,129... | collective-permute-start | bytes 1179656 | tf_op jit(solution)/shard_map/ppermute | solution.py:38
  80.1 14.9 %collective-permute-start.12 = (bf16[256,192]{1,0:T(8,128)(2,1)}, bf16[256,192]{1,0:T(8,128)(2,1)S(1)}, u32[]{:S(2)}, u32[]{:S(2)}) collective-permute-start(bf16[256,192]{1,0:T(8,128)(2,1)} %get-tuple-element.29), channel_id=1, source_target_pairs={{0,192},{64,128},{128,64},{192,0},{1,193},{65,129},{129,65},{193,1... | collective-permute-start | bytes 294920 | tf_op jit(solution)/shard_map/ppermute | solution.py:57
  81.5 15.0 %collective-permute-start.11 = (bf16[256,192]{1,0:T(8,128)(2,1)}, bf16[256,192]{1,0:T(8,128)(2,1)S(1)}, u32[]{:S(2)}, u32[]{:S(2)}) collective-permute-start(bf16[256,192]{1,0:T(8,128)(2,1)} %get-tuple-element.30), channel_id=1, source_target_pairs={{0,128},{64,192},{128,0},{192,64},{1,129},{65,193},{129,1},{193,65... | collective-permute-start | bytes 294920 | tf_op jit(solution)/shard_map/ppermute | solution.py:57
  82.3 15.0 %collective-permute-start.10 = (bf16[256,192]{1,0:T(8,128)(2,1)}, bf16[256,192]{1,0:T(8,128)(2,1)S(1)}, u32[]{:S(2)}, u32[]{:S(2)}) collective-permute-start(bf16[256,192]{1,0:T(8,128)(2,1)} %get-tuple-element.31), channel_id=1, source_target_pairs={{0,64},{64,0},{128,192},{192,128},{1,65},{65,1},{129,193},{193,129... | collective-permute-start | bytes 294920 | tf_op jit(solution)/shard_map/ppermute | solution.py:57
  91.7 7.7 %collective-permute-start.9 = (bf16[256,768]{1,0:T(8,128)(2,1)S(1)}, bf16[256,768]{1,0:T(8,128)(2,1)S(1)}, u32[]{:S(2)}, u32[]{:S(2)}) collective-permute-start(bf16[256,768]{1,0:T(8,128)(2,1)S(1)} %collective-permute-done.8.refs_2_), channel_id=1, source_target_pairs={{0,64},{64,0},{128,192},{192,128},{1,65},{65,1},{129,193},{193,129... | collective-permute-start | bytes 1179656 | tf_op jit(solution)/shard_map/ppermute | solution.py:38
  95.1 5.0 %collective-permute-start.15 = (bf16[128,192]{1,0:T(8,128)(2,1)S(1)}, bf16[128,192]{1,0:T(8,128)(2,1)S(1)}, u32[]{:S(2)}, u32[]{:S(2)}) collective-permute-start(bf16[128,192]{1,0:T(8,128)(2,1)S(1)} %get-tuple-element.33), channel_id=1, source_target_pairs={{0,192},{64,128},{128,64},{192,0},{1,193},{65,129},{129,65},{193,1... | collective-permute-start | bytes 147464 | tf_op jit(solution)/shard_map/ppermute | solution.py:57
  96.6 4.4 %collective-permute-start.14 = (bf16[128,192]{1,0:T(8,128)(2,1)S(1)}, bf16[128,192]{1,0:T(8,128)(2,1)S(1)}, u32[]{:S(2)}, u32[]{:S(2)}) collective-permute-start(bf16[128,192]{1,0:T(8,128)(2,1)S(1)} %get-tuple-element.34), channel_id=1, source_target_pairs={{0,128},{64,192},{128,0},{192,64},{1,129},{65,193},{129,1},{193,65... | collective-permute-start | bytes 147464 | tf_op jit(solution)/shard_map/ppermute | solution.py:57
  97.3 3.7 %collective-permute-start.13 = (bf16[128,192]{1,0:T(8,128)(2,1)S(1)}, bf16[128,192]{1,0:T(8,128)(2,1)S(1)}, u32[]{:S(2)}, u32[]{:S(2)}) collective-permute-start(bf16[128,192]{1,0:T(8,128)(2,1)S(1)} %get-tuple-element.35), channel_id=1, source_target_pairs={{0,64},{64,0},{128,192},{192,128},{1,65},{65,1},{129,193},{193,129... | collective-permute-start | bytes 147464 | tf_op jit(solution)/shard_map/ppermute | solution.py:57
  104.0 34.5 %all-to-all-start.2 = ((bf16[16,432,128]{2,1,0:T(8,128)(2,1)}), bf16[16,432,128]{2,1,0:T(8,128)(2,1)S(1)}, u32[]{:S(2)}, u32[]{:S(2)}) async-start(bf16[16,432,128]{2,1,0:T(8,128)(2,1)} %bitcast.9), calls=%async_computation.2 | async-start | bytes 3538944 | tf_op jit(solution)/shard_map/all_to_all | solution.py:332
  111.1 20.5 %collective-permute-start.2 = (bf16[16,768]{1,0:T(8,128)(2,1)S(1)}, bf16[16,768]{1,0:T(8,128)(2,1)S(1)}, u32[]{:S(2)}, u32[]{:S(2)}) collective-permute-start(bf16[16,768]{1,0:T(8,128)(2,1)S(1)} %get-tuple-element.37), channel_id=1, source_target_pairs={{0,1},{1,2},{2,3},{3,4},{4,5},{5,6},{6,7},{7,8},{8,9},{9,10},{10,1... | collective-permute-start | bytes 73736 | tf_op jit(solution)/shard_map/ppermute | solution.py:32
  114.5 19.0 %collective-permute-start.3 = (bf16[16,768]{1,0:T(8,128)(2,1)S(1)}, bf16[16,768]{1,0:T(8,128)(2,1)S(1)}, u32[]{:S(2)}, u32[]{:S(2)}) collective-permute-start(bf16[16,768]{1,0:T(8,128)(2,1)S(1)} %get-tuple-element.38), channel_id=1, source_target_pairs={{1,0},{2,1},{3,2},{4,3},{5,4},{6,5},{7,6},{8,7},{9,8},{10,9},{11,1... | collective-permute-start | bytes 73736 | tf_op jit(solution)/shard_map/ppermute | solution.py:33
  139.3 14.4 %all-to-all-start.3 = ((bf16[4,144,128]{2,1,0:T(8,128)(2,1)}), bf16[4,144,128]{2,1,0:T(8,128)(2,1)S(1)}, u32[]{:S(2)}, u32[]{:S(2)}) async-start(bf16[4,144,128]{2,1,0:T(8,128)(2,1)} %shard_map.108), calls=%async_computation.3 | async-start | bytes 294912 | tf_op jit(solution)/shard_map/all_to_all | solution.py:348
  (7 other events, 76.1 us)

commit v8 on v7

--- a/solution.py
+++ b/solution.py
@@ -64,8 +64,14 @@
 
 
 def conv_kernel(taps, above_ref, input_ref, below_ref, hits_ref, notes_ref, weight_ref, *rest):
-    padded_ref, hidden_ref, slope_ref, sent_ref, held_ref, done = rest
+    padded_out, hidden_out, slope_out, sent_ref, held_ref, padded_ref, hidden_ref, slope_ref, done = rest
     row_count, chan_count = input_ref.shape
+    leaving = [
+        pltpu.make_async_copy(source, target, done.at[taps + index])
+        for index, (source, target) in enumerate(
+            ((padded_ref, padded_out), (hidden_ref, hidden_out), (slope_ref, slope_out))
+        )
+    ]
     copies = []
     for k in range(taps):
         rows = pl.ds(k * chan_count, chan_count)
@@ -77,6 +83,7 @@
     inverse = lax.rsqrt(jnp.mean(values * values, axis=1, keepdims=True) + 1e-05)
     normed = values * inverse
     padded_ref[...] = normed.astype(jnp.bfloat16)
+    leaving[0].start()
     preact = jnp.zeros((row_count, hidden_ref.shape[1]), jnp.float32)
     for k in range(taps):
         column = normed[k * DILATION : k * DILATION + row_count].astype(jnp.bfloat16)
@@ -90,22 +97,40 @@
     density = jnp.exp(-0.5 * preact * preact) * (1.0 / math.sqrt(2.0 * math.pi))
     hidden = (preact * normal_cdf).astype(jnp.bfloat16)
     hidden_ref[...] = hidden
+    leaving[1].start()
     slope_ref[...] = normal_cdf + preact * density
+    leaving[2].start()
     out_count = hidden_ref.shape[1]
     sent_ref[:, :out_count] = jnp.dot(
         hits_ref[...], hidden, preferred_element_type=jnp.float32
     ).astype(jnp.bfloat16)
     sent_ref[:, out_count:] = notes_ref[...]
-
-
-def pair_kernel(got_ref, hidden_ref, first_ref, second_ref, cotangent_ref, *outs):
-    back_ref, part_ref, feature_ref, delta_ref = outs
+    for copy in leaving:
+        copy.wait()
+
+
+def turn_kernel(own_ref, *refs):
+    peers, out_ref = refs[:-1], refs[-1]
+    pieces = [own_ref[...].astype(jnp.float32)]
+    for peer in peers:
+        values = peer[...].astype(jnp.float32)
+        inverse = lax.rsqrt(jnp.mean(values * values, axis=1, keepdims=True) + 1e-05)
+        pieces.append(values * inverse)
+    out_ref[...] = jnp.concatenate(pieces, axis=0).T.astype(jnp.bfloat16)
+
+
+def pair_kernel(got_ref, hidden_in, first_ref, second_ref, cotangent_ref, *rest):
+    back_ref, part_out, feature_ref, delta_ref, hidden_ref, part_ref, done = rest
+    hidden_copy = pltpu.make_async_copy(hidden_in, hidden_ref, done.at[0])
+    part_copy = pltpu.make_async_copy(part_ref, part_out, done.at[1])
+    hidden_copy.start()
     chan_count = hidden_ref.shape[1]
     slots = got_ref.shape[0]
     note = got_ref[:, chan_count:].astype(jnp.float32)
     score = note[:, 1:2] + note[:, 2:3] + note[:, 3:4]
     row_ids = lax.broadcasted_iota(jnp.int32, (slots, hidden_ref.shape[0]), 1).astype(jnp.float32)
     hits = (note[:, 0:1] == row_ids).astype(jnp.float32).astype(jnp.bfloat16)
+    hidden_copy.wait()
     accept = jnp.dot(hits, hidden_ref[...], preferred_element_type=jnp.float32)
     donor = got_ref[:, :chan_count].astype(jnp.float32)
     feature = (donor * accept).astype(jnp.bfloat16)
@@ -118,9 +143,11 @@
     feature_grad = lax.dot_general(
         delta, first_ref[...], (((1,), (1,)), ((), ())), preferred_element_type=jnp.float32
     )
-    back_ref[...] = (feature_grad * accept).astype(jnp.bfloat16)
     accept_grad = (feature_grad * donor).astype(jnp.bfloat16)
     part_ref[...] = cotangent_ref[...].astype(jnp.float32) + contract_rows(hits, accept_grad)
+    part_copy.start()
+    back_ref[...] = (feature_grad * accept).astype(jnp.bfloat16)
+    part_copy.wait()
 
 
 def head_kernel(scale, *refs):
@@ -252,12 +279,7 @@
     core_input, z_input = swap_core(padded_input), swap_z(padded_input)
     padded_peers = padded_input, core_input, z_input, swap_core(z_input)
 
-    def normalise(field):
-        values = field.astype(jnp.float32)
-        inverse = lax.rsqrt(jnp.mean(values * values, axis=1, keepdims=True) + 1e-05)
-        return (values * inverse).astype(jnp.bfloat16)
-
-    spec = pl.BlockSpec(memory_space=pltpu.VMEM)
+    spec, far = pl.BlockSpec(memory_space=pltpu.VMEM), pl.BlockSpec(memory_space=pltpu.HBM)
     padded, hidden, slope, sent = pl.pallas_call(
         functools.partial(conv_kernel, tap_count),
         out_shape=(
@@ -266,11 +288,14 @@
             jax.ShapeDtypeStruct((row_count, out_count), jnp.float32),
             jax.ShapeDtypeStruct((slots, out_count + LANES), jnp.bfloat16),
         ),
-        in_specs=[spec] * 5 + [pl.BlockSpec(memory_space=pl.ANY)],
-        out_specs=(spec,) * 4,
+        in_specs=[spec] * 5 + [far],
+        out_specs=(far,) * 3 + (spec,),
         scratch_shapes=[
             pltpu.VMEM(conv_weight.shape, jnp.bfloat16),
-            pltpu.SemaphoreType.DMA((tap_count,)),
+            pltpu.VMEM((row_count + 2 * reach_rows, chan_count), jnp.bfloat16),
+            pltpu.VMEM((row_count, out_count), jnp.bfloat16),
+            pltpu.VMEM((row_count, out_count), jnp.float32),
+            pltpu.SemaphoreType.DMA((tap_count + 3,)),
         ],
         compiler_params=pltpu.CompilerParams(vmem_limit_bytes=KERNEL_VMEM),
     )(above, activations[0], below, hits, notes, conv_weight)
@@ -282,16 +307,22 @@
         tiled=True,
     ).reshape(slots, out_count + LANES)
     slot_shape = jax.ShapeDtypeStruct((slots, out_count), jnp.bfloat16)
-    back, part, feature, delta = in_vmem(
+    back, part, feature, delta = pl.pallas_call(
         pair_kernel,
-        (
+        out_shape=(
             slot_shape,
             jax.ShapeDtypeStruct((row_count, out_count), jnp.float32),
             slot_shape,
             slot_shape,
         ),
-        5,
-        KERNEL_VMEM,
+        in_specs=[spec, far, spec, spec, spec],
+        out_specs=(spec, far, spec, spec),
+        scratch_shapes=[
+            pltpu.VMEM((row_count, out_count), jnp.bfloat16),
+            pltpu.VMEM((row_count, out_count), jnp.float32),
+            pltpu.SemaphoreType.DMA((2,)),
+        ],
+        compiler_params=pltpu.CompilerParams(vmem_limit_bytes=KERNEL_VMEM),
     )(got, hidden, head_first, head_second.reshape(1, out_count), hidden_cotangent[0])
     donor_grad = lax.all_to_all(
         back.reshape(shards, capacity, out_count),
@@ -311,11 +342,13 @@
     hidden_grad = part + contract_rows(hits, donor_grad)
     preact_grad = (hidden_grad * slope).astype(jnp.bfloat16)
     grad_peers = dp_columns(preact_grad, col_width)
-    grad_above, grad_below = seq_halo(preact_grad, reach_rows)
-
-    normed_all = jnp.concatenate(
-        [padded] + [normalise(peer) for peer in padded_peers[1:]], axis=0
-    ).T
+
+    normed_all = in_vmem(
+        turn_kernel,
+        jax.ShapeDtypeStruct((chan_count, dp_count * (row_count + 2 * reach_rows)), jnp.bfloat16),
+        4,
+        KERNEL_VMEM,
+    )(padded, *padded_peers[1:])
     ys, zs, xs = SEQ_GRID
     row_total = tap_count * chan_count + out_count
     share = row_total // shards
@@ -339,6 +372,8 @@
             [(y * zs + z) * xs + x for y in range(ys) for x in range(xs)] for z in range(zs)
         ],
     )
+    own_grad = row_grad(preact_grad, conv_weight, tap_count)
+    terms, halo_source, own_grad = lax.optimization_barrier((terms, preact_grad, own_grad))
     folded = in_vmem(
         functools.partial(fold_kernel, share, zs),
         jax.ShapeDtypeStruct((zs, 2 * share, LANES), jnp.bfloat16),
@@ -360,35 +395,52 @@
     others = jnp.where(upper, total[share:, LANES // 2 :], total[share:, : LANES // 2])
     weight_grads = jnp.concatenate([total[:share], others], axis=1)
 
-    input_grad = data_grad(
-        activations[0], grad_above, preact_grad, grad_below, conv_weight, tap_count
+    grad_above, grad_below = seq_halo(halo_source, reach_rows)
+    input_grad = norm_grad(
+        activations[0], own_grad + edge_grad(grad_above, grad_below, conv_weight, row_count)
     )
     return (input_grad.astype(jnp.bfloat16)[None], weight_grads)
 
 
-def data_grad(inputs, grad_above, preact_grad, grad_below, conv_weight, tap_count):
-    reach_rows = grad_above.shape[0]
-    row_count, chan_count = inputs.shape
-    input_values = inputs.astype(jnp.float32)
-    norm_inverse = lax.rsqrt(
-        jnp.mean(input_values * input_values, axis=1, keepdims=True) + 1e-05
-    )
-    grad_padded = jnp.concatenate([grad_above, preact_grad, grad_below], axis=0)
-    spread = lax.dot_general(
-        grad_padded, conv_weight, (((1,), (1,)), ((), ())), preferred_element_type=jnp.float32
-    )
-    normed_grad = spread[2 * reach_rows : 2 * reach_rows + row_count, 0:chan_count]
-    for tap_index in range(1, tap_count):
-        first_row = 2 * reach_rows - tap_index * DILATION
-        normed_grad = (
-            normed_grad
-            + spread[
-                first_row : first_row + row_count,
-                tap_index * chan_count : (tap_index + 1) * chan_count,
-            ]
-        )
-    return norm_inverse * normed_grad - input_values * norm_inverse**3 * jnp.mean(
-        normed_grad * input_values, axis=1, keepdims=True
+def against_weights(grads, conv_weight):
+    return lax.dot_general(
+        grads, conv_weight, (((1,), (1,)), ((), ())), preferred_element_type=jnp.float32
+    )
+
+
+def row_grad(preact_grad, conv_weight, tap_count):
+    chan_count = conv_weight.shape[0] // tap_count
+    reach = (tap_count - 1) // 2 * DILATION
+    row_count = preact_grad.shape[0]
+    spread = jnp.pad(against_weights(preact_grad, conv_weight), ((reach, reach), (0, 0)))
+    total = None
+    for k in range(tap_count):
+        first = 2 * reach - k * DILATION
+        term = spread[first : first + row_count, k * chan_count : (k + 1) * chan_count]
+        total = term if total is None else total + term
+    return total
+
+
+def edge_grad(grad_above, grad_below, conv_weight, row_count):
+    width = grad_above.shape[0]
+    chan_count = grad_above.shape[1]
+    spread = against_weights(jnp.concatenate([grad_above, grad_below], axis=0), conv_weight)
+
+    def tap(k):
+        return spread[:, k * chan_count : (k + 1) * chan_count]
+
+    none = jnp.zeros((width - DILATION, chan_count), jnp.float32)
+    top = tap(4)[:width] + jnp.concatenate([tap(3)[DILATION:width], none], axis=0)
+    bottom = tap(0)[width:] + jnp.concatenate([none, tap(1)[width : 2 * width - DILATION]], axis=0)
+    middle = jnp.zeros((row_count - 2 * width, chan_count), jnp.float32)
+    return jnp.concatenate([top, middle, bottom], axis=0)
+
+
+def norm_grad(inputs, normed_grad):
+    values = inputs.astype(jnp.float32)
+    inverse = lax.rsqrt(jnp.mean(values * values, axis=1, keepdims=True) + 1e-05)
+    return inverse * normed_grad - values * inverse**3 * jnp.mean(
+        normed_grad * values, axis=1, keepdims=True
     )
 
 

time: 157 us -> 168 us (1.070)
  other arithmetic: 16.5 us -> 6.84 us
  waiting for transfers between devices: 54 us -> 63.2 us
  matrix products: 5.76 us -> 10.6 us
  starting transfers between devices: 55.6 us -> 59 us
  Pallas kernels: 9.01 us -> 11.9 us
    all_to_all x1, waiting for transfers between devices: 0.01 us -> 21.9 us  [per_device(): lax.all_to_all(term.reshape(ys * xs, chunk, LANES), 'seq', split_axis=0,...]
    ppermute x2, waiting for transfers between devices: 18.2 us -> 0.01 us  [seq_halo(): lax.ppermute(cells[-width:], 'seq', [(i, i + 1) for i in range(count - 1)])]
    ppermute x2, waiting for transfers between devices: 9.43 us -> 18 us  [swap_z(): return lax.ppermute(field, 'dp', [(0, 2), (1, 3), (2, 0), (3, 1)])]
    convert_element_type x3 -> x0, other arithmetic: 5.47 us -> none  [normalise(): return (values * inverse).astype(jnp.bfloat16)]
    ppermute x2, waiting for transfers between devices: 5.19 us -> 0.01 us  [seq_halo(): lax.ppermute(cells[:width], 'seq', [(i + 1, i) for i in range(count - 1)])]
    dot_general x1 -> x2, matrix products: 4.39 us -> 9.21 us  [against_weights(): lax.dot_general(grads, conv_weight, (((1,), (1,)), ((), ())), preferred_e...]
    all_to_all x1, waiting for transfers between devices: 7.7 us -> 3.13 us  [per_device(): lax.all_to_all(folded, 'seq', split_axis=0, concat_axis=0, tiled=True, ax...]
    all_to_all x1, starting transfers between devices: 6.42 us -> 10.8 us  [per_device(): lax.all_to_all(sent.reshape(shards, capacity, out_count + LANES), 'seq',...]
  transfers between devices with their start and end apart: 20 -> 20, of which waited for: 8 -> 6; matrix products, arithmetic and copies ran while one was open for 18% -> 12% of each run, Pallas kernels for 3% -> 2%
where the time goes in v8:
time: 168 us; the launch traced here: 166 us
  waiting for transfers between devices  63.2 us (38%)
  starting transfers between devices  59 us (35%)
  local copies, waits for them, and re-layouts  13.2 us (8%)
  Pallas kernels  11.9 us (7%)
  matrix products  10.6 us (6%)
  other arithmetic  6.84 us (4%)
    all_to_all x1, waiting for transfers between devices, per_device(): lax.all_to_all(term.reshape(ys * xs, chunk, LANES), 'seq', split_axis=0,...  21.9 us
    ppermute x2, starting transfers between devices, seq_halo(): lax.ppermute(cells[:width], 'seq', [(i + 1, i) for i in range(count - 1)])  18.1 us
    ppermute x2, waiting for transfers between devices, swap_z(): return lax.ppermute(field, 'dp', [(0, 2), (1, 3), (2, 0), (3, 1)])  18 us
    all_to_all x1, waiting for transfers between devices, per_device(): lax.all_to_all(sent.reshape(shards, capacity, out_count + LANES), 'seq',...  15.5 us
    all_to_all x1, starting transfers between devices, per_device(): lax.all_to_all(sent.reshape(shards, capacity, out_count + LANES), 'seq',...  10.8 us
    dot_general x2, matrix products, against_weights(): lax.dot_general(grads, conv_weight, (((1,), (1,)), ((), ())), preferred_e...  9.21 us
    all_to_all x1, starting transfers between devices, per_device(): lax.all_to_all(back.reshape(shards, capacity, out_count), 'seq', split_ax...  7.62 us
    unnamed x26, local copies, waits for them, and re-layouts  7.56 us
  transfers between devices with their start and end apart: 20, of which 6 were waited for; matrix products, arithmetic and copies ran while one was open for 12% of the time, Pallas kernels for 2%

profile of v8, /device:TPU:24, one launch (start us, length us, event | category | flops | bytes accessed | tf_op | source)
XLA Modules:
  0.0 165.7 jit_solution(5977832204867083283)
XLA Ops:
  1.4 3.4 %collective-permute-start = (bf16[16,768]{1,0:T(8,128)(2,1)S(1)}, bf16[16,768]{1,0:T(8,128)(2,1)S(1)}, u32[]{:S(2)}, u32[]{:S(2)}) collective-permute-start(bf16[16,768]{1,0:T(8,128)(2,1)S(1)} %get-tuple-element.45), channel_id=1, source_target_pairs={{0,1},{1,2},{2,3},{3,4},{4,5},{5,6},{6,7},{7,8},{8,9},{9,10},{10,1... | collective-permute-start | bytes 73736 | tf_op jit(solution)/shard_map/ppermute | solution.py:32
  4.8 9.1 %collective-permute-start.1 = (bf16[16,768]{1,0:T(8,128)(2,1)S(1)}, bf16[16,768]{1,0:T(8,128)(2,1)S(1)}, u32[]{:S(2)}, u32[]{:S(2)}) collective-permute-start(bf16[16,768]{1,0:T(8,128)(2,1)S(1)} %get-tuple-element.44), channel_id=1, source_target_pairs={{1,0},{2,1},{3,2},{4,3},{5,4},{6,5},{7,6},{8,7},{9,8},{10,9},{11,1... | collective-permute-start | bytes 73736 | tf_op jit(solution)/shard_map/ppermute | solution.py:33
  17.3 2.7 %copy-done = bf16[3840,768]{1,0:T(8,128)(2,1)S(1)} copy-done((bf16[3840,768]{1,0:T(8,128)(2,1)S(1)}, bf16[3840,768]{1,0:T(8,128)(2,1)}, u32[]{:S(2)}) %copy-start) | copy-done | bytes 5898264
  20.8 4.0 %shard_map.104 = (bf16[160,768]{1,0:T(8,128)(2,1)S(1)}, bf16[128,768]{1,0:T(8,128)(2,1)S(1)}, f32[128,768]{1,0:T(8,128)S(1)}, bf16[256,896]{1,0:T(8,128)(2,1)S(1)}) custom-call(bf16[16,768]{1,0:T(8,128)(2,1)S(1)} %collective-permute-done.above_ref, bf16[128,768]{1,0:T(8,128)(2,1)S(1)} %bitcast.21, bf16[16,768]{1,0:T(8,128)(2,1)S(1)} %collective-permute-done.1.below_ref, ...), custom_call_target="tpu_custom_call" | custom-call | tf_op jit(solution)/shard_map/pallas_call | solution.py:283
  27.1 10.8 %all-to-all-start = ((bf16[64,4,896]{2,1,0:T(4,128)(2,1)}), bf16[64,4,896]{2,1,0:T(4,128)(2,1)S(1)}, u32[]{:S(2)}, u32[]{:S(2)}) async-start(bf16[64,4,896]{2,1,0:T(4,128)(2,1)} %reshape.60), calls=%async_computation | async-start | bytes 917504 | tf_op jit(solution)/shard_map/all_to_all | solution.py:302
  37.9 15.5 %all-to-all-done = bf16[64,4,896]{2,1,0:T(4,128)(2,1)S(1)} async-done(((bf16[64,4,896]{2,1,0:T(4,128)(2,1)}), bf16[64,4,896]{2,1,0:T(4,128)(2,1)S(1)}, u32[]{:S(2)}, u32[]{:S(2)}) %all-to-all-start) | async-done | bytes 458784 | tf_op jit(solution)/shard_map/all_to_all | solution.py:302
  55.4 1.9 %shard_map.106 = (bf16[256,768]{1,0:T(8,128)(2,1)S(1)}, f32[128,768]{1,0:T(8,128)S(1)}, bf16[256,768]{1,0:T(8,128)(2,1)S(1)}, bf16[256,768]{1,0:T(8,128)(2,1)S(1)}) custom-call(bf16[256,896]{1,0:T(8,128)(2,1)S(1)} %reshape.61.got_ref, bf16[128,768]{1,0:T(8,128)(2,1)S(1)} %copy-done.9, bf16[768,768]{1,0:T(8,128)(2,1)S(1)} %copy-done.3, ...), custom_call_target="tpu_custom_call" | custom-call | tf_op jit(solution)/shard_map/pallas_call | solution.py:310
  58.9 7.6 %all-to-all-start.1 = ((bf16[64,4,768]{2,1,0:T(4,128)(2,1)}), bf16[64,4,768]{2,1,0:T(4,128)(2,1)}, u32[]{:S(2)}, u32[]{:S(2)}) async-start(bf16[64,4,768]{2,1,0:T(4,128)(2,1)} %reshape.63), calls=%async_computation.1 | async-start | bytes 786432 | tf_op jit(solution)/shard_map/all_to_all | solution.py:327
  69.4 18.0 %collective-permute-done.3.refs_1_ = bf16[160,768]{1,0:T(8,128)(2,1)S(1)} collective-permute-done((bf16[160,768]{1,0:T(8,128)(2,1)}, bf16[160,768]{1,0:T(8,128)(2,1)S(1)}, u32[]{:S(2)}, u32[]{:S(2)}) %collective-permute-start.3) | collective-permute-done | bytes 245792 | tf_op jit(solution)/shard_map/ppermute | solution.py:42
  89.1 1.9 %reshape.64 = bf16[256,768]{1,0:T(8,128)(2,1)} reshape(bf16[64,4,768]{2,1,0:T(4,128)(2,1)} %all-to-all-done.1) | data formatting | bytes 786432 | tf_op jit(solution)/shard_map/reshape | solution.py:333
  90.9 1.2 fusion.42
  93.7 1.7 collective-permute-start.9
  96.8 3.1 %collective-permute-done.9.refs_6_ = bf16[256,192]{1,0:T(8,128)(2,1)S(1)} collective-permute-done((bf16[256,192]{1,0:T(8,128)(2,1)S(1)}, bf16[256,192]{1,0:T(8,128)(2,1)S(1)}, u32[]{:S(2)}, u32[]{:S(2)}) %collective-permute-start.9) | collective-permute-done | bytes 98336 | tf_op jit(solution)/shard_map/ppermute | solution.py:57
  100.3 1.4 shard_map.105.refs_0_
  102.5 1.5 collective-permute-done.13.refs_5_
  103.9 3.0 %shard_map.108 = bf16[6912,128]{1,0:T(8,128)(2,1)} custom-call(bf16[768,640]{1,0:T(8,128)(2,1)S(1)} %shard_map.105.refs_0_, bf16[768,192]{1,0:T(8,128)(2,1)S(1)} %shard_map.107.refs_1_, bf16[128,192]{1,0:T(8,128)(2,1)S(1)} %get-tuple-element.43.refs_2_, bf16[128,192]{1,0:T(8,128)(2,1)S(1)} %collective-permute-done.11.refs_3_, ...), custom_call_target="tpu_custom_call" | custom-call | tf_op jit(solution)/shard_map/pallas_call | solution.py:356
  106.9 7.1 %all-to-all-start.2 = ((bf16[16,432,128]{2,1,0:T(8,128)(2,1)}), bf16[16,432,128]{2,1,0:T(8,128)(2,1)S(1)}, u32[]{:S(2)}, u32[]{:S(2)}) async-start(bf16[16,432,128]{2,1,0:T(8,128)(2,1)} %bitcast.6), calls=%async_computation.2 | async-start | bytes 3538944 | tf_op jit(solution)/shard_map/all_to_all | solution.py:365
  114.0 4.7 %fusion.43 = f32[128,3840]{1,0:T(8,128)S(1)} fusion(bf16[128,768]{1,0:T(8,128)(2,1)S(1)} %copy-done.11, bf16[3840,768]{1,0:T(8,128)(2,1)} %weight_ref.1), kind=kOutput, calls=%fused_computation.83 | convolution fusion | flops 754974720 | bytes 8060928 | tf_op jit(solution)/shard_map/dot_general | solution.py:406
  118.8 21.9 %all-to-all-done.2.terms_ref = bf16[16,432,128]{2,1,0:T(8,128)(2,1)S(1)} async-done(((bf16[16,432,128]{2,1,0:T(8,128)(2,1)}), bf16[16,432,128]{2,1,0:T(8,128)(2,1)S(1)}, u32[]{:S(2)}, u32[]{:S(2)}) %all-to-all-start.2) | async-done | bytes 1769504 | tf_op jit(solution)/shard_map/all_to_all | solution.py:365
  140.8 1.9 %collective-permute-start.14 = (bf16[16,768]{1,0:T(8,128)(2,1)S(1)}, bf16[16,768]{1,0:T(8,128)(2,1)S(1)}, u32[]{:S(2)}, u32[]{:S(2)}) collective-permute-start(bf16[16,768]{1,0:T(8,128)(2,1)S(1)} %get-tuple-element.38), channel_id=1, source_target_pairs={{0,1},{1,2},{2,3},{3,4},{4,5},{5,6},{6,7},{7,8},{8,9},{9,10},{10,1... | collective-permute-start | bytes 73736 | tf_op jit(solution)/shard_map/ppermute | solution.py:32
  142.7 9.0 %collective-permute-start.15 = (bf16[16,768]{1,0:T(8,128)(2,1)S(1)}, bf16[16,768]{1,0:T(8,128)(2,1)S(1)}, u32[]{:S(2)}, u32[]{:S(2)}) collective-permute-start(bf16[16,768]{1,0:T(8,128)(2,1)S(1)} %get-tuple-element.39), channel_id=1, source_target_pairs={{1,0},{2,1},{3,2},{4,3},{5,4},{6,5},{7,6},{8,7},{9,8},{10,9},{11,1... | collective-permute-start | bytes 73736 | tf_op jit(solution)/shard_map/ppermute | solution.py:33
  152.8 3.4 %all-to-all-start.3 = ((bf16[4,144,128]{2,1,0:T(8,128)(2,1)}), bf16[4,144,128]{2,1,0:T(8,128)(2,1)S(1)}, u32[]{:S(2)}, u32[]{:S(2)}) async-start(bf16[4,144,128]{2,1,0:T(8,128)(2,1)} %shard_map.109), calls=%async_computation.3 | async-start | bytes 294912 | tf_op jit(solution)/shard_map/all_to_all | solution.py:383
  156.2 4.5 %fusion.18 = f32[32,3840]{1,0:T(8,128)S(1)} fusion(bf16[3840,768]{1,0:T(8,128)(2,1)} %weight_ref.1, bf16[16,768]{1,0:T(8,128)(2,1)S(1)} %collective-permute-done.15, bf16[16,768]{1,0:T(8,128)(2,1)S(1)} %collective-permute-done.14), kind=kOutput, calls=%fused_computation.39 | convolution fusion | flops 188841984 | bytes 6438912 | tf_op jit(solution)/shard_map/dot_general | solution.py:406
  161.8 3.1 %all-to-all-done.3 = bf16[4,144,128]{2,1,0:T(8,128)(2,1)S(1)} async-done(((bf16[4,144,128]{2,1,0:T(8,128)(2,1)}), bf16[4,144,128]{2,1,0:T(8,128)(2,1)S(1)}, u32[]{:S(2)}, u32[]{:S(2)}) %all-to-all-start.3) | async-done | bytes 147488 | tf_op jit(solution)/shard_map/all_to_all | solution.py:383
  (84 shorter events, 22.2 us)
Async XLA Ops:
  0.6 37.2 %copy-start.12 = (bf16[768]{0:T(1024)(128)(2,1)S(1)}, bf16[768]{0:T(1024)(128)(2,1)}, u32[]{:S(2)}) copy-start(bf16[768]{0:T(1024)(128)(2,1)} %param.12) | copy-start | bytes 4612
  1.4 15.8 %collective-permute-start = (bf16[16,768]{1,0:T(8,128)(2,1)S(1)}, bf16[16,768]{1,0:T(8,128)(2,1)S(1)}, u32[]{:S(2)}, u32[]{:S(2)}) collective-permute-start(bf16[16,768]{1,0:T(8,128)(2,1)S(1)} %get-tuple-element.45), channel_id=1, source_target_pairs={{0,1},{1,2},{2,3},{3,4},{4,5},{5,6},{6,7},{7,8},{8,9},{9,10},{10,1... | collective-permute-start | bytes 73736 | tf_op jit(solution)/shard_map/ppermute | solution.py:32
  4.8 12.4 %collective-permute-start.1 = (bf16[16,768]{1,0:T(8,128)(2,1)S(1)}, bf16[16,768]{1,0:T(8,128)(2,1)S(1)}, u32[]{:S(2)}, u32[]{:S(2)}) collective-permute-start(bf16[16,768]{1,0:T(8,128)(2,1)S(1)} %get-tuple-element.44), channel_id=1, source_target_pairs={{1,0},{2,1},{3,2},{4,3},{5,4},{6,5},{7,6},{8,7},{9,8},{10,9},{11,1... | collective-permute-start | bytes 73736 | tf_op jit(solution)/shard_map/ppermute | solution.py:33
  20.8 32.7 %copy-start.3 = (bf16[768,768]{1,0:T(8,128)(2,1)S(1)}, bf16[768,768]{1,0:T(8,128)(2,1)}, u32[]{:S(2)}) copy-start(bf16[768,768]{1,0:T(8,128)(2,1)} %first_ref.1) | copy-start | bytes 3538948
  20.8 46.6 %copy-start.2 = (bf16[1,128,768]{2,1,0:T(8,128)(2,1)S(1)}, bf16[1,128,768]{2,1,0:T(8,128)(2,1)}, u32[]{:S(2)}) copy-start(bf16[1,128,768]{2,1,0:T(8,128)(2,1)} %param.9) | copy-start | bytes 589828
  27.1 26.3 %all-to-all-start = ((bf16[64,4,896]{2,1,0:T(4,128)(2,1)}), bf16[64,4,896]{2,1,0:T(4,128)(2,1)S(1)}, u32[]{:S(2)}, u32[]{:S(2)}) async-start(bf16[64,4,896]{2,1,0:T(4,128)(2,1)} %reshape.60), calls=%async_computation | async-start | bytes 917504 | tf_op jit(solution)/shard_map/all_to_all | solution.py:302
  58.0 42.3 %copy-start.6 = (bf16[160,768]{1,0:T(8,128)(2,1)S(1)}, bf16[160,768]{1,0:T(8,128)(2,1)}, u32[]{:S(2)}) copy-start(bf16[160,768]{1,0:T(8,128)(2,1)} %copy-done.5) | copy-start | bytes 737284
  58.9 30.2 %all-to-all-start.1 = ((bf16[64,4,768]{2,1,0:T(4,128)(2,1)}), bf16[64,4,768]{2,1,0:T(4,128)(2,1)}, u32[]{:S(2)}, u32[]{:S(2)}) async-start(bf16[64,4,768]{2,1,0:T(4,128)(2,1)} %reshape.63), calls=%async_computation.1 | async-start | bytes 786432 | tf_op jit(solution)/shard_map/all_to_all | solution.py:327
  66.5 22.3 %collective-permute-start.6 = (bf16[256,768]{1,0:T(8,128)(2,1)S(1)}, bf16[256,768]{1,0:T(8,128)(2,1)S(1)}, u32[]{:S(2)}, u32[]{:S(2)}) collective-permute-start(bf16[256,768]{1,0:T(8,128)(2,1)S(1)} %get-tuple-element.20.refs_0_), channel_id=1, source_target_pairs={{0,128},{64,192},{128,0},{192,64},{1,129},{65,193},{129,1},{193,65... | collective-permute-start | bytes 1179656 | tf_op jit(solution)/shard_map/ppermute | solution.py:42
  68.2 19.2 %collective-permute-start.3 = (bf16[160,768]{1,0:T(8,128)(2,1)}, bf16[160,768]{1,0:T(8,128)(2,1)S(1)}, u32[]{:S(2)}, u32[]{:S(2)}) collective-permute-start(bf16[160,768]{1,0:T(8,128)(2,1)} %pad_maximum_fusion), channel_id=1, source_target_pairs={{0,128},{64,192},{128,0},{192,64},{1,129},{65,193},{129,1},{193,65... | collective-permute-start | bytes 737288 | tf_op jit(solution)/shard_map/ppermute | solution.py:42
  69.3 23.9 %collective-permute-start.2 = (bf16[160,768]{1,0:T(8,128)(2,1)}, bf16[160,768]{1,0:T(8,128)(2,1)S(1)}, u32[]{:S(2)}, u32[]{:S(2)}) collective-permute-start(bf16[160,768]{1,0:T(8,128)(2,1)} %pad_maximum_fusion), channel_id=1, source_target_pairs={{0,64},{64,0},{128,192},{192,128},{1,65},{65,1},{129,193},{193,129... | collective-permute-start | bytes 737288 | tf_op jit(solution)/shard_map/ppermute | solution.py:38
  87.4 6.3 %collective-permute-start.4 = (bf16[160,768]{1,0:T(8,128)(2,1)S(1)}, bf16[160,768]{1,0:T(8,128)(2,1)}, u32[]{:S(2)}, u32[]{:S(2)}) collective-permute-start(bf16[160,768]{1,0:T(8,128)(2,1)S(1)} %collective-permute-done.3.refs_1_), channel_id=1, source_target_pairs={{0,64},{64,0},{128,192},{192,128},{1,65},{65,1},{129,193},{193,129... | collective-permute-start | bytes 737288 | tf_op jit(solution)/shard_map/ppermute | solution.py:38
  87.4 14.4 %collective-permute-start.5 = (bf16[256,768]{1,0:T(8,128)(2,1)S(1)}, bf16[256,768]{1,0:T(8,128)(2,1)S(1)}, u32[]{:S(2)}, u32[]{:S(2)}) collective-permute-start(bf16[256,768]{1,0:T(8,128)(2,1)S(1)} %get-tuple-element.20.refs_0_), channel_id=1, source_target_pairs={{0,64},{64,0},{128,192},{192,128},{1,65},{65,1},{129,193},{193,129... | collective-permute-start | bytes 1179656 | tf_op jit(solution)/shard_map/ppermute | solution.py:38
  88.8 6.7 %collective-permute-start.10 = (bf16[256,192]{1,0:T(8,128)(2,1)}, bf16[256,192]{1,0:T(8,128)(2,1)S(1)}, u32[]{:S(2)}, u32[]{:S(2)}) collective-permute-start(bf16[256,192]{1,0:T(8,128)(2,1)} %get-tuple-element.34), channel_id=1, source_target_pairs={{0,192},{64,128},{128,64},{192,0},{1,193},{65,129},{129,65},{193,1... | collective-permute-start | bytes 294920 | tf_op jit(solution)/shard_map/ppermute | solution.py:57
  88.8 12.9 %collective-permute-start.7 = (bf16[256,768]{1,0:T(8,128)(2,1)S(1)}, bf16[256,768]{1,0:T(8,128)(2,1)S(1)}, u32[]{:S(2)}, u32[]{:S(2)}) collective-permute-start(bf16[256,768]{1,0:T(8,128)(2,1)S(1)} %collective-permute-done.6.refs_2_), channel_id=1, source_target_pairs={{0,64},{64,0},{128,192},{192,128},{1,65},{65,1},{129,193},{193,129... | collective-permute-start | bytes 1179656 | tf_op jit(solution)/shard_map/ppermute | solution.py:38
  93.3 2.7 %collective-permute-start.8 = (bf16[256,192]{1,0:T(8,128)(2,1)}, bf16[256,192]{1,0:T(8,128)(2,1)S(1)}, u32[]{:S(2)}, u32[]{:S(2)}) collective-permute-start(bf16[256,192]{1,0:T(8,128)(2,1)} %get-tuple-element.36), channel_id=1, source_target_pairs={{0,64},{64,0},{128,192},{192,128},{1,65},{65,1},{129,193},{193,129... | collective-permute-start | bytes 294920 | tf_op jit(solution)/shard_map/ppermute | solution.py:57
  93.7 6.2 %collective-permute-start.9 = (bf16[256,192]{1,0:T(8,128)(2,1)S(1)}, bf16[256,192]{1,0:T(8,128)(2,1)S(1)}, u32[]{:S(2)}, u32[]{:S(2)}) collective-permute-start(bf16[256,192]{1,0:T(8,128)(2,1)S(1)} %get-tuple-element.35), channel_id=1, source_target_pairs={{0,128},{64,192},{128,0},{192,64},{1,129},{65,193},{129,1},{193,65... | collective-permute-start | bytes 294920 | tf_op jit(solution)/shard_map/ppermute | solution.py:57
  95.5 6.9 %collective-permute-start.11 = (bf16[128,192]{1,0:T(8,128)(2,1)S(1)}, bf16[128,192]{1,0:T(8,128)(2,1)S(1)}, u32[]{:S(2)}, u32[]{:S(2)}) collective-permute-start(bf16[128,192]{1,0:T(8,128)(2,1)S(1)} %get-tuple-element.42), channel_id=1, source_target_pairs={{0,64},{64,0},{128,192},{192,128},{1,65},{65,1},{129,193},{193,129... | collective-permute-start | bytes 147464 | tf_op jit(solution)/shard_map/ppermute | solution.py:57
  95.9 6.5 %collective-permute-start.12 = (bf16[128,192]{1,0:T(8,128)(2,1)S(1)}, bf16[128,192]{1,0:T(8,128)(2,1)S(1)}, u32[]{:S(2)}, u32[]{:S(2)}) collective-permute-start(bf16[128,192]{1,0:T(8,128)(2,1)S(1)} %get-tuple-element.41), channel_id=1, source_target_pairs={{0,128},{64,192},{128,0},{192,64},{1,129},{65,193},{129,1},{193,65... | collective-permute-start | bytes 147464 | tf_op jit(solution)/shard_map/ppermute | solution.py:57
  99.9 4.0 %collective-permute-start.13 = (bf16[128,192]{1,0:T(8,128)(2,1)S(1)}, bf16[128,192]{1,0:T(8,128)(2,1)S(1)}, u32[]{:S(2)}, u32[]{:S(2)}) collective-permute-start(bf16[128,192]{1,0:T(8,128)(2,1)S(1)} %get-tuple-element.40), channel_id=1, source_target_pairs={{0,192},{64,128},{128,64},{192,0},{1,193},{65,129},{129,65},{193,1... | collective-permute-start | bytes 147464 | tf_op jit(solution)/shard_map/ppermute | solution.py:57
  106.9 33.9 %all-to-all-start.2 = ((bf16[16,432,128]{2,1,0:T(8,128)(2,1)}), bf16[16,432,128]{2,1,0:T(8,128)(2,1)S(1)}, u32[]{:S(2)}, u32[]{:S(2)}) async-start(bf16[16,432,128]{2,1,0:T(8,128)(2,1)} %bitcast.6), calls=%async_computation.2 | async-start | bytes 3538944 | tf_op jit(solution)/shard_map/all_to_all | solution.py:365
  140.8 15.4 %collective-permute-start.14 = (bf16[16,768]{1,0:T(8,128)(2,1)S(1)}, bf16[16,768]{1,0:T(8,128)(2,1)S(1)}, u32[]{:S(2)}, u32[]{:S(2)}) collective-permute-start(bf16[16,768]{1,0:T(8,128)(2,1)S(1)} %get-tuple-element.38), channel_id=1, source_target_pairs={{0,1},{1,2},{2,3},{3,4},{4,5},{5,6},{6,7},{7,8},{8,9},{9,10},{10,1... | collective-permute-start | bytes 73736 | tf_op jit(solution)/shard_map/ppermute | solution.py:32
  142.7 13.5 %collective-permute-start.15 = (bf16[16,768]{1,0:T(8,128)(2,1)S(1)}, bf16[16,768]{1,0:T(8,128)(2,1)S(1)}, u32[]{:S(2)}, u32[]{:S(2)}) collective-permute-start(bf16[16,768]{1,0:T(8,128)(2,1)S(1)} %get-tuple-element.39), channel_id=1, source_target_pairs={{1,0},{2,1},{3,2},{4,3},{5,4},{6,5},{7,6},{8,7},{9,8},{10,9},{11,1... | collective-permute-start | bytes 73736 | tf_op jit(solution)/shard_map/ppermute | solution.py:33
  152.8 12.2 %all-to-all-start.3 = ((bf16[4,144,128]{2,1,0:T(8,128)(2,1)}), bf16[4,144,128]{2,1,0:T(8,128)(2,1)S(1)}, u32[]{:S(2)}, u32[]{:S(2)}) async-start(bf16[4,144,128]{2,1,0:T(8,128)(2,1)} %shard_map.109), calls=%async_computation.3 | async-start | bytes 294912 | tf_op jit(solution)/shard_map/all_to_all | solution.py:383
  (9 other events, 28.4 us)

commit v9 on v8

--- a/solution.py
+++ b/solution.py
@@ -40,12 +40,6 @@
 
 def swap_z(field):
     return lax.ppermute(field, "dp", [(0, 2), (1, 3), (2, 0), (3, 1)])
-
-
-def dp_peers(field):
-    core = swap_core(field)
-    z_side = swap_z(field)
-    return field, core, z_side, swap_core(z_side)
 
 
 def dp_columns(field, width):
@@ -150,15 +144,16 @@
     part_copy.wait()
 
 
-def head_kernel(scale, *refs):
-    term = contract_rows(refs[4][...], refs[0][...])
-    for feature, delta in zip(refs[1:4], refs[5:8], strict=True):
-        term = term + contract_rows(delta[...], feature[...])
-    refs[8][...] = (term.T * scale).astype(jnp.bfloat16)
+def head_kernel(scale, feature_ref, feature_core_ref, *refs):
+    for own, core, out in zip(refs[0:2], refs[2:4], refs[4:6], strict=True):
+        term = contract_rows(own[...], feature_ref[...]) + contract_rows(
+            core[...], feature_core_ref[...]
+        )
+        out[...] = (term.T * scale).astype(jnp.bfloat16)
 
 
 def weight_kernel(scale, taps, grid, *refs):
-    normed_ref, head_ref, grads, out_ref, tail_ref = refs[0], refs[1], refs[2:6], refs[6], refs[7]
+    normed_ref, heads, grads, out_ref, tail_ref = refs[0], refs[1:3], refs[3:7], refs[7], refs[8]
     ys, zs, xs = grid
     chan_count = normed_ref.shape[0]
     width = 2 * LANES
@@ -191,7 +186,8 @@
             k * chan_count,
             jnp.dot(normed_ref[...], shifted, preferred_element_type=jnp.float32) * scale,
         )
-    put(taps * chan_count, tail_twice(head_ref[...].astype(jnp.float32)))
+    head_term = heads[0][...].astype(jnp.float32) + heads[1][...].astype(jnp.float32)
+    put(taps * chan_count, tail_twice(head_term))
     low = lax.broadcasted_iota(jnp.int32, (share, LANES), 1) < LANES // 2
     for y in range(ys):
         for x in range(xs):
@@ -331,17 +327,25 @@
         concat_axis=0,
         tiled=True,
     ).reshape(slots, out_count)
-    feature_peers = dp_peers(feature)
-    delta_peers = dp_columns(delta, col_width)
-    head_term = in_vmem(
+    own_place = lax.axis_index("dp")
+    delta_cols = [
+        lax.dynamic_slice_in_dim(delta, (own_place ^ flip) * col_width, col_width, axis=1)
+        for flip in (0, 2, 1, 3)
+    ]
+    feature_core = swap_core(feature)
+    delta_core = [swap_core(piece) for piece in delta_cols[2:]]
+    head_shape = jax.ShapeDtypeStruct((out_count, col_width), jnp.bfloat16)
+    head_kept, head_away = in_vmem(
         functools.partial(head_kernel, 1.0 / math.sqrt(dp_count * pair_count * shards)),
-        jax.ShapeDtypeStruct((out_count, col_width), jnp.bfloat16),
-        8,
+        (head_shape, head_shape),
+        6,
         KERNEL_VMEM,
-    )(*feature_peers, *delta_peers)
+    )(feature, feature_core, *delta_cols[:2], *delta_core)
+    head_got = swap_z(head_away)
     hidden_grad = part + contract_rows(hits, donor_grad)
     preact_grad = (hidden_grad * slope).astype(jnp.bfloat16)
     grad_peers = dp_columns(preact_grad, col_width)
+    grad_above, grad_below = seq_halo(preact_grad, reach_rows)
 
     normed_all = in_vmem(
         turn_kernel,
@@ -358,10 +362,10 @@
             weight_kernel, 1.0 / math.sqrt(dp_count * row_count * shards), tap_count, SEQ_GRID
         ),
         jax.ShapeDtypeStruct((ys * xs * chunk, LANES), jnp.bfloat16),
-        6,
+        7,
         KERNEL_VMEM,
         [pltpu.VMEM((row_total, LANES), jnp.float32)],
-    )(normed_all, head_term, *grad_peers)
+    )(normed_all, head_kept, head_got, *grad_peers)
     terms = lax.all_to_all(
         term.reshape(ys * xs, chunk, LANES),
         "seq",
@@ -372,8 +376,6 @@
             [(y * zs + z) * xs + x for y in range(ys) for x in range(xs)] for z in range(zs)
         ],
     )
-    own_grad = row_grad(preact_grad, conv_weight, tap_count)
-    terms, halo_source, own_grad = lax.optimization_barrier((terms, preact_grad, own_grad))
     folded = in_vmem(
         functools.partial(fold_kernel, share, zs),
         jax.ShapeDtypeStruct((zs, 2 * share, LANES), jnp.bfloat16),
@@ -395,52 +397,35 @@
     others = jnp.where(upper, total[share:, LANES // 2 :], total[share:, : LANES // 2])
     weight_grads = jnp.concatenate([total[:share], others], axis=1)
 
-    grad_above, grad_below = seq_halo(halo_source, reach_rows)
-    input_grad = norm_grad(
-        activations[0], own_grad + edge_grad(grad_above, grad_below, conv_weight, row_count)
+    input_grad = data_grad(
+        activations[0], grad_above, preact_grad, grad_below, conv_weight, tap_count
     )
     return (input_grad.astype(jnp.bfloat16)[None], weight_grads)
 
 
-def against_weights(grads, conv_weight):
-    return lax.dot_general(
-        grads, conv_weight, (((1,), (1,)), ((), ())), preferred_element_type=jnp.float32
-    )
-
-
-def row_grad(preact_grad, conv_weight, tap_count):
-    chan_count = conv_weight.shape[0] // tap_count
-    reach = (tap_count - 1) // 2 * DILATION
-    row_count = preact_grad.shape[0]
-    spread = jnp.pad(against_weights(preact_grad, conv_weight), ((reach, reach), (0, 0)))
-    total = None
-    for k in range(tap_count):
-        first = 2 * reach - k * DILATION
-        term = spread[first : first + row_count, k * chan_count : (k + 1) * chan_count]
-        total = term if total is None else total + term
-    return total
-
-
-def edge_grad(grad_above, grad_below, conv_weight, row_count):
-    width = grad_above.shape[0]
-    chan_count = grad_above.shape[1]
-    spread = against_weights(jnp.concatenate([grad_above, grad_below], axis=0), conv_weight)
-
-    def tap(k):
-        return spread[:, k * chan_count : (k + 1) * chan_count]
-
-    none = jnp.zeros((width - DILATION, chan_count), jnp.float32)
-    top = tap(4)[:width] + jnp.concatenate([tap(3)[DILATION:width], none], axis=0)
-    bottom = tap(0)[width:] + jnp.concatenate([none, tap(1)[width : 2 * width - DILATION]], axis=0)
-    middle = jnp.zeros((row_count - 2 * width, chan_count), jnp.float32)
-    return jnp.concatenate([top, middle, bottom], axis=0)
-
-
-def norm_grad(inputs, normed_grad):
-    values = inputs.astype(jnp.float32)
-    inverse = lax.rsqrt(jnp.mean(values * values, axis=1, keepdims=True) + 1e-05)
-    return inverse * normed_grad - values * inverse**3 * jnp.mean(
-        normed_grad * values, axis=1, keepdims=True
+def data_grad(inputs, grad_above, preact_grad, grad_below, conv_weight, tap_count):
+    reach_rows = grad_above.shape[0]
+    row_count, chan_count = inputs.shape
+    input_values = inputs.astype(jnp.float32)
+    norm_inverse = lax.rsqrt(
+        jnp.mean(input_values * input_values, axis=1, keepdims=True) + 1e-05
+    )
+    grad_padded = jnp.concatenate([grad_above, preact_grad, grad_below], axis=0)
+    spread = lax.dot_general(
+        grad_padded, conv_weight, (((1,), (1,)), ((), ())), preferred_element_type=jnp.float32
+    )
+    normed_grad = spread[2 * reach_rows : 2 * reach_rows + row_count, 0:chan_count]
+    for tap_index in range(1, tap_count):
+        first_row = 2 * reach_rows - tap_index * DILATION
+        normed_grad = (
+            normed_grad
+            + spread[
+                first_row : first_row + row_count,
+                tap_index * chan_count : (tap_index + 1) * chan_count,
+            ]
+        )
+    return norm_inverse * normed_grad - input_values * norm_inverse**3 * jnp.mean(
+        normed_grad * input_values, axis=1, keepdims=True
     )
 
 

time: 168 us -> 152 us (0.905)
  the two profiles are of different devices: /device:TPU:24 before, /device:TPU:6 now
where the time goes in v9:
time: 152 us; the launch traced here: 151 us
  waiting for transfers between devices  63.9 us (42%)
  starting transfers between devices  52.8 us (35%)
  Pallas kernels  11.8 us (8%)
  local copies, waits for them, and re-layouts  11.1 us (7%)
  other arithmetic  5.72 us (4%)
  matrix products  5.13 us (3%)
    ppermute x2, waiting for transfers between devices, seq_halo(): lax.ppermute(cells[-width:], 'seq', [(i, i + 1) for i in range(count - 1)])  19.7 us
    ppermute x2, waiting for transfers between devices, swap_z(): return lax.ppermute(field, 'dp', [(0, 2), (1, 3), (2, 0), (3, 1)])  16.3 us
    all_to_all x1, waiting for transfers between devices, per_device(): lax.all_to_all(sent.reshape(shards, capacity, out_count + LANES), 'seq',...  14.1 us
    all_to_all x1, starting transfers between devices, per_device(): lax.all_to_all(sent.reshape(shards, capacity, out_count + LANES), 'seq',...  12.6 us
    ppermute x2, starting transfers between devices, seq_halo(): lax.ppermute(cells[-width:], 'seq', [(i, i + 1) for i in range(count - 1)])  8.98 us
    all_to_all x1, starting transfers between devices, per_device(): lax.all_to_all(back.reshape(shards, capacity, out_count), 'seq', split_ax...  8.94 us
    all_to_all x1, waiting for transfers between devices, per_device(): lax.all_to_all(folded, 'seq', split_axis=0, concat_axis=0, tiled=True, ax...  8.21 us
    all_to_all x1, starting transfers between devices, per_device(): lax.all_to_all(term.reshape(ys * xs, chunk, LANES), 'seq', split_axis=0,...  7.33 us
  transfers between devices with their start and end apart: 18, of which 8 were waited for; matrix products, arithmetic and copies ran while one was open for 8% of the time, Pallas kernels for 1%

profile of v9, /device:TPU:6, one launch (start us, length us, event | category | flops | bytes accessed | tf_op | source)
XLA Modules:
  0.0 151.4 jit_solution(11592536226602837440)
XLA Ops:
  1.4 5.1 %collective-permute-start = (bf16[16,768]{1,0:T(8,128)(2,1)S(1)}, bf16[16,768]{1,0:T(8,128)(2,1)S(1)}, u32[]{:S(2)}, u32[]{:S(2)}) collective-permute-start(bf16[16,768]{1,0:T(8,128)(2,1)S(1)} %get-tuple-element.40), channel_id=1, source_target_pairs={{0,1},{1,2},{2,3},{3,4},{4,5},{5,6},{6,7},{7,8},{8,9},{9,10},{10,1... | collective-permute-start | bytes 73736 | tf_op jit(solution)/shard_map/ppermute | solution.py:32
  6.5 1.9 %collective-permute-start.1 = (bf16[16,768]{1,0:T(8,128)(2,1)S(1)}, bf16[16,768]{1,0:T(8,128)(2,1)S(1)}, u32[]{:S(2)}, u32[]{:S(2)}) collective-permute-start(bf16[16,768]{1,0:T(8,128)(2,1)S(1)} %get-tuple-element.39), channel_id=1, source_target_pairs={{1,0},{2,1},{3,2},{4,3},{5,4},{6,5},{7,6},{8,7},{9,8},{10,9},{11,1... | collective-permute-start | bytes 73736 | tf_op jit(solution)/shard_map/ppermute | solution.py:33
  11.7 3.7 %collective-permute-done.1.below_ref = bf16[16,768]{1,0:T(8,128)(2,1)S(1)} collective-permute-done((bf16[16,768]{1,0:T(8,128)(2,1)S(1)}, bf16[16,768]{1,0:T(8,128)(2,1)S(1)}, u32[]{:S(2)}, u32[]{:S(2)}) %collective-permute-start.1) | collective-permute-done | bytes 24608 | tf_op jit(solution)/shard_map/ppermute | solution.py:33
  15.4 2.7 %copy-done = bf16[3840,768]{1,0:T(8,128)(2,1)S(1)} copy-done((bf16[3840,768]{1,0:T(8,128)(2,1)S(1)}, bf16[3840,768]{1,0:T(8,128)(2,1)}, u32[]{:S(2)}) %copy-start) | copy-done | bytes 5898264
  19.0 4.0 %shard_map.104 = (bf16[160,768]{1,0:T(8,128)(2,1)S(1)}, bf16[128,768]{1,0:T(8,128)(2,1)S(1)}, f32[128,768]{1,0:T(8,128)S(1)}, bf16[256,896]{1,0:T(8,128)(2,1)S(1)}) custom-call(bf16[16,768]{1,0:T(8,128)(2,1)S(1)} %collective-permute-done.above_ref, bf16[128,768]{1,0:T(8,128)(2,1)S(1)} %bitcast.19, bf16[16,768]{1,0:T(8,128)(2,1)S(1)} %collective-permute-done.1.below_ref, ...), custom_call_target="tpu_custom_call" | custom-call | tf_op jit(solution)/shard_map/pallas_call | solution.py:279
  24.6 12.6 %all-to-all-start = ((bf16[64,4,896]{2,1,0:T(4,128)(2,1)}), bf16[64,4,896]{2,1,0:T(4,128)(2,1)S(1)}, u32[]{:S(2)}, u32[]{:S(2)}) async-start(bf16[64,4,896]{2,1,0:T(4,128)(2,1)} %reshape.60), calls=%async_computation | async-start | bytes 917504 | tf_op jit(solution)/shard_map/all_to_all | solution.py:298
  37.3 14.1 %all-to-all-done = bf16[64,4,896]{2,1,0:T(4,128)(2,1)S(1)} async-done(((bf16[64,4,896]{2,1,0:T(4,128)(2,1)}), bf16[64,4,896]{2,1,0:T(4,128)(2,1)S(1)}, u32[]{:S(2)}, u32[]{:S(2)}) %all-to-all-start) | async-done | bytes 458784 | tf_op jit(solution)/shard_map/all_to_all | solution.py:298
  53.3 1.9 %shard_map.105 = (bf16[256,768]{1,0:T(8,128)(2,1)S(1)}, f32[128,768]{1,0:T(8,128)S(1)}, bf16[256,768]{1,0:T(8,128)(2,1)S(1)}, bf16[256,768]{1,0:T(8,128)(2,1)S(1)}) custom-call(bf16[256,896]{1,0:T(8,128)(2,1)S(1)} %reshape.61.got_ref, bf16[128,768]{1,0:T(8,128)(2,1)S(1)} %copy-done.10, bf16[768,768]{1,0:T(8,128)(2,1)S(1)} %copy-done.3, ...), custom_call_target="tpu_custom_call" | custom-call | tf_op jit(solution)/shard_map/pallas_call | solution.py:306
  56.9 8.9 %all-to-all-start.1 = ((bf16[64,4,768]{2,1,0:T(4,128)(2,1)}), bf16[64,4,768]{2,1,0:T(4,128)(2,1)}, u32[]{:S(2)}, u32[]{:S(2)}) async-start(bf16[64,4,768]{2,1,0:T(4,128)(2,1)} %reshape.63), calls=%async_computation.1 | async-start | bytes 786432 | tf_op jit(solution)/shard_map/all_to_all | solution.py:323
  68.6 9.8 %collective-permute-done.5.refs_1_ = bf16[160,768]{1,0:T(8,128)(2,1)S(1)} collective-permute-done((bf16[160,768]{1,0:T(8,128)(2,1)}, bf16[160,768]{1,0:T(8,128)(2,1)S(1)}, u32[]{:S(2)}, u32[]{:S(2)}) %collective-permute-start.5) | collective-permute-done | bytes 245792 | tf_op jit(solution)/shard_map/ppermute | solution.py:42
  78.4 1.5 %shard_map.107 = (bf16[768,192]{1,0:T(8,128)(2,1)S(1)}, bf16[768,192]{1,0:T(8,128)(2,1)}) custom-call(bf16[256,768]{1,0:T(8,128)(2,1)S(1)} %copy-done.5, bf16[256,768]{1,0:T(8,128)(2,1)S(1)} %collective-permute-done.7.feature_core_ref, bf16[256,192]{1,0:T(8,128)(2,1)S(1)} %get-tuple-element.32.refs_0_, bf16[256,192]{1,0:T(8,128)(2,1)S(1)} %get-tuple-element.31.refs_1_, ...), custom_call_target="tpu_custom_call" | custom-call | tf_op jit(solution)/shard_map/pallas_call | solution.py:338
  79.9 1.6 %collective-permute-start.10 = (bf16[768,192]{1,0:T(8,128)(2,1)}, bf16[768,192]{1,0:T(8,128)(2,1)S(1)}, u32[]{:S(2)}, u32[]{:S(2)}) collective-permute-start(bf16[768,192]{1,0:T(8,128)(2,1)} %get-tuple-element.25), channel_id=1, source_target_pairs={{0,128},{64,192},{128,0},{192,64},{1,129},{65,193},{129,1},{193,65... | collective-permute-start | bytes 884744 | tf_op jit(solution)/shard_map/ppermute | solution.py:42
  81.5 1.1 reshape.64
  83.9 1.2 collective-permute-start.13
  85.6 6.5 %collective-permute-done.10.refs_2_ = bf16[768,192]{1,0:T(8,128)(2,1)S(1)} collective-permute-done((bf16[768,192]{1,0:T(8,128)(2,1)}, bf16[768,192]{1,0:T(8,128)(2,1)S(1)}, u32[]{:S(2)}, u32[]{:S(2)}) %collective-permute-start.10) | collective-permute-done | bytes 294944 | tf_op jit(solution)/shard_map/ppermute | solution.py:42
  92.1 1.4 collective-permute-done.12.refs_5_
  94.0 3.0 %shard_map.108 = bf16[6912,128]{1,0:T(8,128)(2,1)} custom-call(bf16[768,640]{1,0:T(8,128)(2,1)S(1)} %shard_map.106.refs_0_, bf16[768,192]{1,0:T(8,128)(2,1)S(1)} %get-tuple-element.24.refs_1_, bf16[768,192]{1,0:T(8,128)(2,1)S(1)} %collective-permute-done.10.refs_2_, bf16[128,192]{1,0:T(8,128)(2,1)S(1)} %get-tuple-element.36.refs_3_, ...), custom_call_target="tpu_custom_call" | custom-call | tf_op jit(solution)/shard_map/pallas_call | solution.py:360
  97.0 7.3 %all-to-all-start.2 = ((bf16[16,432,128]{2,1,0:T(8,128)(2,1)}), bf16[16,432,128]{2,1,0:T(8,128)(2,1)S(1)}, u32[]{:S(2)}, u32[]{:S(2)}) async-start(bf16[16,432,128]{2,1,0:T(8,128)(2,1)} %bitcast.7), calls=%async_computation.2 | async-start | bytes 3538944 | tf_op jit(solution)/shard_map/all_to_all | solution.py:369
  104.3 3.9 %collective-permute-start.2 = (bf16[16,768]{1,0:T(8,128)(2,1)S(1)}, bf16[16,768]{1,0:T(8,128)(2,1)S(1)}, u32[]{:S(2)}, u32[]{:S(2)}) collective-permute-start(bf16[16,768]{1,0:T(8,128)(2,1)S(1)} %get-tuple-element.37), channel_id=1, source_target_pairs={{0,1},{1,2},{2,3},{3,4},{4,5},{5,6},{6,7},{7,8},{8,9},{9,10},{10,1... | collective-permute-start | bytes 73736 | tf_op jit(solution)/shard_map/ppermute | solution.py:32
  108.2 1.9 %collective-permute-start.3 = (bf16[16,768]{1,0:T(8,128)(2,1)S(1)}, bf16[16,768]{1,0:T(8,128)(2,1)S(1)}, u32[]{:S(2)}, u32[]{:S(2)}) collective-permute-start(bf16[16,768]{1,0:T(8,128)(2,1)S(1)} %get-tuple-element.38), channel_id=1, source_target_pairs={{1,0},{2,1},{3,2},{4,3},{5,4},{6,5},{7,6},{8,7},{9,8},{10,9},{11,1... | collective-permute-start | bytes 73736 | tf_op jit(solution)/shard_map/ppermute | solution.py:33
  110.2 19.7 %collective-permute-done.2 = bf16[16,768]{1,0:T(8,128)(2,1)S(1)} collective-permute-done((bf16[16,768]{1,0:T(8,128)(2,1)S(1)}, bf16[16,768]{1,0:T(8,128)(2,1)S(1)}, u32[]{:S(2)}, u32[]{:S(2)}) %collective-permute-start.2) | collective-permute-done | bytes 24608 | tf_op jit(solution)/shard_map/ppermute | solution.py:32
  129.9 4.7 %fusion.6 = f32[160,3840]{1,0:T(8,128)S(1)} fusion(bf16[3840,768]{1,0:T(8,128)(2,1)} %weight_ref.1, bf16[16,768]{1,0:T(8,128)(2,1)S(1)} %collective-permute-done.3, bf16[128,768]{1,0:T(8,128)(2,1)S(1)} %multiply_convert_fusion, bf16[16,768]{1,0:T(8,128)(2,1)S(1)} %collective-permute-done.2), kind=kOutput, calls=%fused_computation.16 | convolution fusion | flops 944455680 | bytes 8601600 | tf_op jit(solution)/shard_map/dot_general | solution.py:414
  135.8 5.8 %all-to-all-start.3 = ((bf16[4,144,128]{2,1,0:T(8,128)(2,1)}), bf16[4,144,128]{2,1,0:T(8,128)(2,1)S(1)}, u32[]{:S(2)}, u32[]{:S(2)}) async-start(bf16[4,144,128]{2,1,0:T(8,128)(2,1)} %shard_map.109), calls=%async_computation.3 | async-start | bytes 294912 | tf_op jit(solution)/shard_map/all_to_all | solution.py:385
  142.5 8.2 %all-to-all-done.3 = bf16[4,144,128]{2,1,0:T(8,128)(2,1)S(1)} async-done(((bf16[4,144,128]{2,1,0:T(8,128)(2,1)}), bf16[4,144,128]{2,1,0:T(8,128)(2,1)S(1)}, u32[]{:S(2)}, u32[]{:S(2)}) %all-to-all-start.3) | async-done | bytes 147488 | tf_op jit(solution)/shard_map/all_to_all | solution.py:385
  (80 shorter events, 17.7 us)
Async XLA Ops:
  1.4 10.3 %collective-permute-start = (bf16[16,768]{1,0:T(8,128)(2,1)S(1)}, bf16[16,768]{1,0:T(8,128)(2,1)S(1)}, u32[]{:S(2)}, u32[]{:S(2)}) collective-permute-start(bf16[16,768]{1,0:T(8,128)(2,1)S(1)} %get-tuple-element.40), channel_id=1, source_target_pairs={{0,1},{1,2},{2,3},{3,4},{4,5},{5,6},{6,7},{7,8},{8,9},{9,10},{10,1... | collective-permute-start | bytes 73736 | tf_op jit(solution)/shard_map/ppermute | solution.py:32
  6.5 8.9 %collective-permute-start.1 = (bf16[16,768]{1,0:T(8,128)(2,1)S(1)}, bf16[16,768]{1,0:T(8,128)(2,1)S(1)}, u32[]{:S(2)}, u32[]{:S(2)}) collective-permute-start(bf16[16,768]{1,0:T(8,128)(2,1)S(1)} %get-tuple-element.39), channel_id=1, source_target_pairs={{1,0},{2,1},{3,2},{4,3},{5,4},{6,5},{7,6},{8,7},{9,8},{10,9},{11,1... | collective-permute-start | bytes 73736 | tf_op jit(solution)/shard_map/ppermute | solution.py:33
  19.0 18.2 %copy-start.15 = (bf16[768]{0:T(1024)(128)(2,1)S(1)}, bf16[768]{0:T(1024)(128)(2,1)}, u32[]{:S(2)}) copy-start(bf16[768]{0:T(1024)(128)(2,1)} %param.12) | copy-start | bytes 4612
  23.7 27.8 %copy-start.3 = (bf16[768,768]{1,0:T(8,128)(2,1)S(1)}, bf16[768,768]{1,0:T(8,128)(2,1)}, u32[]{:S(2)}) copy-start(bf16[768,768]{1,0:T(8,128)(2,1)} %first_ref.1) | copy-start | bytes 3538948
  24.6 26.8 %all-to-all-start = ((bf16[64,4,896]{2,1,0:T(4,128)(2,1)}), bf16[64,4,896]{2,1,0:T(4,128)(2,1)S(1)}, u32[]{:S(2)}, u32[]{:S(2)}) async-start(bf16[64,4,896]{2,1,0:T(4,128)(2,1)} %reshape.60), calls=%async_computation | async-start | bytes 917504 | tf_op jit(solution)/shard_map/all_to_all | solution.py:298
  37.2 28.7 %copy-start.2 = (bf16[1,128,768]{2,1,0:T(8,128)(2,1)S(1)}, bf16[1,128,768]{2,1,0:T(8,128)(2,1)}, u32[]{:S(2)}) copy-start(bf16[1,128,768]{2,1,0:T(8,128)(2,1)} %param.9) | copy-start | bytes 589828
  37.2 28.7 %copy-start.12 = (bf16[16,768]{1,0:T(8,128)(2,1)S(1)}, bf16[16,768]{1,0:T(8,128)(2,1)}, u32[]{:S(2)}) copy-start(bf16[16,768]{1,0:T(8,128)(2,1)} %copy-done.11) | copy-start | bytes 73732
  37.2 28.7 %copy-start.14 = (bf16[16,768]{1,0:T(8,128)(2,1)S(1)}, bf16[16,768]{1,0:T(8,128)(2,1)}, u32[]{:S(2)}) copy-start(bf16[16,768]{1,0:T(8,128)(2,1)} %copy-done.13) | copy-start | bytes 73732
  56.0 22.4 %copy-start.5 = (bf16[256,768]{1,0:T(8,128)(2,1)S(1)}, bf16[256,768]{1,0:T(8,128)(2,1)}, u32[]{:S(2)}) copy-start(bf16[256,768]{1,0:T(8,128)(2,1)} %copy-done.4) | copy-start | bytes 1179652
  56.9 24.7 %all-to-all-start.1 = ((bf16[64,4,768]{2,1,0:T(4,128)(2,1)}), bf16[64,4,768]{2,1,0:T(4,128)(2,1)}, u32[]{:S(2)}, u32[]{:S(2)}) async-start(bf16[64,4,768]{2,1,0:T(4,128)(2,1)} %reshape.63), calls=%async_computation.1 | async-start | bytes 786432 | tf_op jit(solution)/shard_map/all_to_all | solution.py:323
  65.8 12.5 %collective-permute-start.7 = (bf16[256,768]{1,0:T(8,128)(2,1)}, bf16[256,768]{1,0:T(8,128)(2,1)S(1)}, u32[]{:S(2)}, u32[]{:S(2)}) collective-permute-start(bf16[256,768]{1,0:T(8,128)(2,1)} %copy-done.4), channel_id=1, source_target_pairs={{0,64},{64,0},{128,192},{192,128},{1,65},{65,1},{129,193},{193,129... | collective-permute-start | bytes 1179656 | tf_op jit(solution)/shard_map/ppermute | solution.py:38
  66.7 11.7 %collective-permute-start.5 = (bf16[160,768]{1,0:T(8,128)(2,1)}, bf16[160,768]{1,0:T(8,128)(2,1)S(1)}, u32[]{:S(2)}, u32[]{:S(2)}) collective-permute-start(bf16[160,768]{1,0:T(8,128)(2,1)} %pad_maximum_fusion), channel_id=1, source_target_pairs={{0,128},{64,192},{128,0},{192,64},{1,129},{65,193},{129,1},{193,65... | collective-permute-start | bytes 737288 | tf_op jit(solution)/shard_map/ppermute | solution.py:42
  67.8 10.6 %collective-permute-start.8 = (bf16[256,192]{1,0:T(8,128)(2,1)S(1)}, bf16[256,192]{1,0:T(8,128)(2,1)S(1)}, u32[]{:S(2)}, u32[]{:S(2)}) collective-permute-start(bf16[256,192]{1,0:T(8,128)(2,1)S(1)} %get-tuple-element.30), channel_id=1, source_target_pairs={{0,64},{64,0},{128,192},{192,128},{1,65},{65,1},{129,193},{193,129... | collective-permute-start | bytes 294920 | tf_op jit(solution)/shard_map/ppermute | solution.py:38
  68.0 10.3 %collective-permute-start.9 = (bf16[256,192]{1,0:T(8,128)(2,1)S(1)}, bf16[256,192]{1,0:T(8,128)(2,1)S(1)}, u32[]{:S(2)}, u32[]{:S(2)}) collective-permute-start(bf16[256,192]{1,0:T(8,128)(2,1)S(1)} %get-tuple-element.29), channel_id=1, source_target_pairs={{0,64},{64,0},{128,192},{192,128},{1,65},{65,1},{129,193},{193,129... | collective-permute-start | bytes 294920 | tf_op jit(solution)/shard_map/ppermute | solution.py:38
  68.4 15.5 %collective-permute-start.4 = (bf16[160,768]{1,0:T(8,128)(2,1)}, bf16[160,768]{1,0:T(8,128)(2,1)S(1)}, u32[]{:S(2)}, u32[]{:S(2)}) collective-permute-start(bf16[160,768]{1,0:T(8,128)(2,1)} %pad_maximum_fusion), channel_id=1, source_target_pairs={{0,64},{64,0},{128,192},{192,128},{1,65},{65,1},{129,193},{193,129... | collective-permute-start | bytes 737288 | tf_op jit(solution)/shard_map/ppermute | solution.py:38
  78.4 6.7 %collective-permute-start.6 = (bf16[160,768]{1,0:T(8,128)(2,1)S(1)}, bf16[160,768]{1,0:T(8,128)(2,1)S(1)}, u32[]{:S(2)}, u32[]{:S(2)}) collective-permute-start(bf16[160,768]{1,0:T(8,128)(2,1)S(1)} %collective-permute-done.5.refs_1_), channel_id=1, source_target_pairs={{0,64},{64,0},{128,192},{192,128},{1,65},{65,1},{129,193},{193,129... | collective-permute-start | bytes 737288 | tf_op jit(solution)/shard_map/ppermute | solution.py:38
  79.9 12.2 %collective-permute-start.10 = (bf16[768,192]{1,0:T(8,128)(2,1)}, bf16[768,192]{1,0:T(8,128)(2,1)S(1)}, u32[]{:S(2)}, u32[]{:S(2)}) collective-permute-start(bf16[768,192]{1,0:T(8,128)(2,1)} %get-tuple-element.25), channel_id=1, source_target_pairs={{0,128},{64,192},{128,0},{192,64},{1,129},{65,193},{129,1},{193,65... | collective-permute-start | bytes 884744 | tf_op jit(solution)/shard_map/ppermute | solution.py:42
  83.1 9.0 %collective-permute-start.11 = (bf16[128,192]{1,0:T(8,128)(2,1)S(1)}, bf16[128,192]{1,0:T(8,128)(2,1)S(1)}, u32[]{:S(2)}, u32[]{:S(2)}) collective-permute-start(bf16[128,192]{1,0:T(8,128)(2,1)S(1)} %get-tuple-element.35), channel_id=1, source_target_pairs={{0,64},{64,0},{128,192},{192,128},{1,65},{65,1},{129,193},{193,129... | collective-permute-start | bytes 147464 | tf_op jit(solution)/shard_map/ppermute | solution.py:51
  83.4 10.1 %collective-permute-start.12 = (bf16[128,192]{1,0:T(8,128)(2,1)S(1)}, bf16[128,192]{1,0:T(8,128)(2,1)S(1)}, u32[]{:S(2)}, u32[]{:S(2)}) collective-permute-start(bf16[128,192]{1,0:T(8,128)(2,1)S(1)} %get-tuple-element.34), channel_id=1, source_target_pairs={{0,128},{64,192},{128,0},{192,64},{1,129},{65,193},{129,1},{193,65... | collective-permute-start | bytes 147464 | tf_op jit(solution)/shard_map/ppermute | solution.py:51
  83.9 10.1 %collective-permute-start.13 = (bf16[128,192]{1,0:T(8,128)(2,1)S(1)}, bf16[128,192]{1,0:T(8,128)(2,1)S(1)}, u32[]{:S(2)}, u32[]{:S(2)}) collective-permute-start(bf16[128,192]{1,0:T(8,128)(2,1)S(1)} %get-tuple-element.33), channel_id=1, source_target_pairs={{0,192},{64,128},{128,64},{192,0},{1,193},{65,129},{129,65},{193,1... | collective-permute-start | bytes 147464 | tf_op jit(solution)/shard_map/ppermute | solution.py:51
  97.0 37.9 %all-to-all-start.2 = ((bf16[16,432,128]{2,1,0:T(8,128)(2,1)}), bf16[16,432,128]{2,1,0:T(8,128)(2,1)S(1)}, u32[]{:S(2)}, u32[]{:S(2)}) async-start(bf16[16,432,128]{2,1,0:T(8,128)(2,1)} %bitcast.7), calls=%async_computation.2 | async-start | bytes 3538944 | tf_op jit(solution)/shard_map/all_to_all | solution.py:369
  104.3 25.6 %collective-permute-start.2 = (bf16[16,768]{1,0:T(8,128)(2,1)S(1)}, bf16[16,768]{1,0:T(8,128)(2,1)S(1)}, u32[]{:S(2)}, u32[]{:S(2)}) collective-permute-start(bf16[16,768]{1,0:T(8,128)(2,1)S(1)} %get-tuple-element.37), channel_id=1, source_target_pairs={{0,1},{1,2},{2,3},{3,4},{4,5},{5,6},{6,7},{7,8},{8,9},{9,10},{10,1... | collective-permute-start | bytes 73736 | tf_op jit(solution)/shard_map/ppermute | solution.py:32
  108.2 21.7 %collective-permute-start.3 = (bf16[16,768]{1,0:T(8,128)(2,1)S(1)}, bf16[16,768]{1,0:T(8,128)(2,1)S(1)}, u32[]{:S(2)}, u32[]{:S(2)}) collective-permute-start(bf16[16,768]{1,0:T(8,128)(2,1)S(1)} %get-tuple-element.38), channel_id=1, source_target_pairs={{1,0},{2,1},{3,2},{4,3},{5,4},{6,5},{7,6},{8,7},{9,8},{10,9},{11,1... | collective-permute-start | bytes 73736 | tf_op jit(solution)/shard_map/ppermute | solution.py:33
  135.8 14.8 %all-to-all-start.3 = ((bf16[4,144,128]{2,1,0:T(8,128)(2,1)}), bf16[4,144,128]{2,1,0:T(8,128)(2,1)S(1)}, u32[]{:S(2)}, u32[]{:S(2)}) async-start(bf16[4,144,128]{2,1,0:T(8,128)(2,1)} %shard_map.109), calls=%async_computation.3 | async-start | bytes 294912 | tf_op jit(solution)/shard_map/all_to_all | solution.py:385
  (10 other events, 44.0 us)

commit v10 on v9

--- a/solution.py
+++ b/solution.py
@@ -57,9 +57,12 @@
     return jnp.concatenate([values, values[:, LANES:]], axis=1)
 
 
-def conv_kernel(taps, above_ref, input_ref, below_ref, hits_ref, notes_ref, weight_ref, *rest):
-    padded_out, hidden_out, slope_out, sent_ref, held_ref, padded_ref, hidden_ref, slope_ref, done = rest
+def conv_kernel(taps, above_ref, below_ref, hits_ref, notes_ref, input_in, weight_ref, *rest):
+    padded_out, hidden_out, slope_out, sent_ref = rest[:4]
+    held_ref, input_ref, padded_ref, hidden_ref, slope_ref, done = rest[4:]
     row_count, chan_count = input_ref.shape
+    input_copy = pltpu.make_async_copy(input_in, input_ref, done.at[taps + 3])
+    input_copy.start()
     leaving = [
         pltpu.make_async_copy(source, target, done.at[taps + index])
         for index, (source, target) in enumerate(
@@ -71,6 +74,7 @@
         rows = pl.ds(k * chan_count, chan_count)
         copies.append(pltpu.make_async_copy(weight_ref.at[rows], held_ref.at[rows], done.at[k]))
         copies[-1].start()
+    input_copy.wait()
     values = jnp.concatenate([above_ref[...], input_ref[...], below_ref[...]], axis=0).astype(
         jnp.float32
     )
@@ -113,11 +117,14 @@
     out_ref[...] = jnp.concatenate(pieces, axis=0).T.astype(jnp.bfloat16)
 
 
-def pair_kernel(got_ref, hidden_in, first_ref, second_ref, cotangent_ref, *rest):
-    back_ref, part_out, feature_ref, delta_ref, hidden_ref, part_ref, done = rest
+def pair_kernel(got_ref, hidden_in, first_ref, second_ref, cotangent_in, *rest):
+    back_ref, part_out, feature_ref, delta_ref = rest[:4]
+    hidden_ref, cotangent_ref, part_ref, done = rest[4:]
+    cotangent_copy = pltpu.make_async_copy(cotangent_in, cotangent_ref, done.at[2])
     hidden_copy = pltpu.make_async_copy(hidden_in, hidden_ref, done.at[0])
     part_copy = pltpu.make_async_copy(part_ref, part_out, done.at[1])
     hidden_copy.start()
+    cotangent_copy.start()
     chan_count = hidden_ref.shape[1]
     slots = got_ref.shape[0]
     note = got_ref[:, chan_count:].astype(jnp.float32)
@@ -138,6 +145,7 @@
         delta, first_ref[...], (((1,), (1,)), ((), ())), preferred_element_type=jnp.float32
     )
     accept_grad = (feature_grad * donor).astype(jnp.bfloat16)
+    cotangent_copy.wait()
     part_ref[...] = cotangent_ref[...].astype(jnp.float32) + contract_rows(hits, accept_grad)
     part_copy.start()
     back_ref[...] = (feature_grad * accept).astype(jnp.bfloat16)
@@ -209,6 +217,10 @@
         out_ref[z, share:, :] = total[first : first + share].astype(jnp.bfloat16)
 
 
+def in_hbm(field):
+    return pltpu.with_memory_space_constraint(field, pltpu.HBM)
+
+
 def in_vmem(kernel, shapes, count, limit, scratch=()):
     spec = pl.BlockSpec(memory_space=pltpu.VMEM)
     return pl.pallas_call(
@@ -279,22 +291,23 @@
     padded, hidden, slope, sent = pl.pallas_call(
         functools.partial(conv_kernel, tap_count),
         out_shape=(
-            jax.ShapeDtypeStruct((row_count + 2 * reach_rows, chan_count), jnp.bfloat16),
-            jax.ShapeDtypeStruct((row_count, out_count), jnp.bfloat16),
-            jax.ShapeDtypeStruct((row_count, out_count), jnp.float32),
+            pltpu.HBM((row_count + 2 * reach_rows, chan_count), jnp.bfloat16),
+            pltpu.HBM((row_count, out_count), jnp.bfloat16),
+            pltpu.HBM((row_count, out_count), jnp.float32),
             jax.ShapeDtypeStruct((slots, out_count + LANES), jnp.bfloat16),
         ),
-        in_specs=[spec] * 5 + [far],
+        in_specs=[spec] * 4 + [far] * 2,
         out_specs=(far,) * 3 + (spec,),
         scratch_shapes=[
             pltpu.VMEM(conv_weight.shape, jnp.bfloat16),
+            pltpu.VMEM((row_count, chan_count), jnp.bfloat16),
             pltpu.VMEM((row_count + 2 * reach_rows, chan_count), jnp.bfloat16),
             pltpu.VMEM((row_count, out_count), jnp.bfloat16),
             pltpu.VMEM((row_count, out_count), jnp.float32),
-            pltpu.SemaphoreType.DMA((tap_count + 3,)),
+            pltpu.SemaphoreType.DMA((tap_count + 4,)),
         ],
         compiler_params=pltpu.CompilerParams(vmem_limit_bytes=KERNEL_VMEM),
-    )(above, activations[0], below, hits, notes, conv_weight)
+    )(above, below, hits, notes, in_hbm(activations[0]), in_hbm(conv_weight))
     got = lax.all_to_all(
         sent.reshape(shards, capacity, out_count + LANES),
         "seq",
@@ -311,15 +324,22 @@
             slot_shape,
             slot_shape,
         ),
-        in_specs=[spec, far, spec, spec, spec],
+        in_specs=[spec, far, spec, spec, far],
         out_specs=(spec, far, spec, spec),
         scratch_shapes=[
             pltpu.VMEM((row_count, out_count), jnp.bfloat16),
+            pltpu.VMEM((row_count, out_count), jnp.bfloat16),
             pltpu.VMEM((row_count, out_count), jnp.float32),
-            pltpu.SemaphoreType.DMA((2,)),
+            pltpu.SemaphoreType.DMA((3,)),
         ],
         compiler_params=pltpu.CompilerParams(vmem_limit_bytes=KERNEL_VMEM),
-    )(got, hidden, head_first, head_second.reshape(1, out_count), hidden_cotangent[0])
+    )(
+        got,
+        in_hbm(hidden),
+        head_first,
+        head_second.reshape(1, out_count),
+        in_hbm(hidden_cotangent[0]),
+    )
     donor_grad = lax.all_to_all(
         back.reshape(shards, capacity, out_count),
         "seq",

time: 152 us -> 146 us (0.961)
  local copies, waits for them, and re-layouts: 11.1 us -> 3.16 us
    unnamed x32 -> x10, local copies, waits for them, and re-layouts: 6.93 us -> 0.02 us
where the time goes in v10:
time: 146 us; the launch traced here: 145 us
  waiting for transfers between devices  64.6 us (44%)
  starting transfers between devices  52.2 us (36%)
  Pallas kernels  12.7 us (9%)
  other arithmetic  6.69 us (5%)
  matrix products  5.13 us (4%)
  local copies, waits for them, and re-layouts  3.16 us (2%)
    ppermute x2, waiting for transfers between devices, seq_halo(): lax.ppermute(cells[-width:], 'seq', [(i, i + 1) for i in range(count - 1)])  19.7 us
    ppermute x2, waiting for transfers between devices, swap_z(): return lax.ppermute(field, 'dp', [(0, 2), (1, 3), (2, 0), (3, 1)])  17.1 us
    all_to_all x1, waiting for transfers between devices, per_device(): lax.all_to_all(sent.reshape(shards, capacity, out_count + LANES), 'seq',...  14.1 us
    all_to_all x1, starting transfers between devices, per_device(): lax.all_to_all(sent.reshape(shards, capacity, out_count + LANES), 'seq',...  12.6 us
    ppermute x2, starting transfers between devices, seq_halo(): lax.ppermute(cells[-width:], 'seq', [(i, i + 1) for i in range(count - 1)])  8.88 us
    all_to_all x1, starting transfers between devices, per_device(): lax.all_to_all(back.reshape(shards, capacity, out_count), 'seq', split_ax...  8.75 us
    all_to_all x1, waiting for transfers between devices, per_device(): lax.all_to_all(folded, 'seq', split_axis=0, concat_axis=0, tiled=True, ax...  8.21 us
    all_to_all x1, starting transfers between devices, per_device(): lax.all_to_all(term.reshape(ys * xs, chunk, LANES), 'seq', split_axis=0,...  7.33 us
  transfers between devices with their start and end apart: 18, of which 8 were waited for; matrix products, arithmetic and copies ran while one was open for 8% of the time, Pallas kernels for 1%

profile of v10, /device:TPU:6, one launch (start us, length us, event | category | flops | bytes accessed | tf_op | source)
XLA Modules:
  0.0 145.5 jit_solution(1900084185222252013)
XLA Ops:
  1.4 5.1 %collective-permute-start = (bf16[16,768]{1,0:T(8,128)(2,1)S(1)}, bf16[16,768]{1,0:T(8,128)(2,1)S(1)}, u32[]{:S(2)}, u32[]{:S(2)}) collective-permute-start(bf16[16,768]{1,0:T(8,128)(2,1)S(1)} %get-tuple-element.40), channel_id=1, source_target_pairs={{0,1},{1,2},{2,3},{3,4},{4,5},{5,6},{6,7},{7,8},{8,9},{9,10},{10,1... | collective-permute-start | bytes 73736 | tf_op jit(solution)/shard_map/ppermute | solution.py:32
  6.5 1.9 %collective-permute-start.1 = (bf16[16,768]{1,0:T(8,128)(2,1)S(1)}, bf16[16,768]{1,0:T(8,128)(2,1)S(1)}, u32[]{:S(2)}, u32[]{:S(2)}) collective-permute-start(bf16[16,768]{1,0:T(8,128)(2,1)S(1)} %get-tuple-element.39), channel_id=1, source_target_pairs={{1,0},{2,1},{3,2},{4,3},{5,4},{6,5},{7,6},{8,7},{9,8},{10,9},{11,1... | collective-permute-start | bytes 73736 | tf_op jit(solution)/shard_map/ppermute | solution.py:33
  8.4 0.9 convert_reduce_fusion.1
  11.7 3.7 %collective-permute-done.1.below_ref = bf16[16,768]{1,0:T(8,128)(2,1)S(1)} collective-permute-done((bf16[16,768]{1,0:T(8,128)(2,1)S(1)}, bf16[16,768]{1,0:T(8,128)(2,1)S(1)}, u32[]{:S(2)}, u32[]{:S(2)}) %collective-permute-start.1) | collective-permute-done | bytes 24608 | tf_op jit(solution)/shard_map/ppermute | solution.py:33
  15.4 4.2 %shard_map.104 = (bf16[160,768]{1,0:T(8,128)(2,1)}, bf16[128,768]{1,0:T(8,128)(2,1)}, f32[128,768]{1,0:T(8,128)}, bf16[256,896]{1,0:T(8,128)(2,1)S(1)}) custom-call(bf16[16,768]{1,0:T(8,128)(2,1)S(1)} %collective-permute-done.above_ref, bf16[16,768]{1,0:T(8,128)(2,1)S(1)} %collective-permute-done.1.below_ref, bf16[256,128]{1,0:T(8,128)(2,1)S(1)} %fusion.13.hits_ref, ...), custom_call_target="tpu_custom_call" | custom-call | tf_op jit(solution)/shard_map/pallas_call | solution.py:291
  20.5 12.6 %all-to-all-start = ((bf16[64,4,896]{2,1,0:T(4,128)(2,1)}), bf16[64,4,896]{2,1,0:T(4,128)(2,1)S(1)}, u32[]{:S(2)}, u32[]{:S(2)}) async-start(bf16[64,4,896]{2,1,0:T(4,128)(2,1)} %reshape.60), calls=%async_computation | async-start | bytes 917504 | tf_op jit(solution)/shard_map/all_to_all | solution.py:311
  33.2 14.1 %all-to-all-done = bf16[64,4,896]{2,1,0:T(4,128)(2,1)S(1)} async-done(((bf16[64,4,896]{2,1,0:T(4,128)(2,1)}), bf16[64,4,896]{2,1,0:T(4,128)(2,1)S(1)}, u32[]{:S(2)}, u32[]{:S(2)}) %all-to-all-start) | async-done | bytes 458784 | tf_op jit(solution)/shard_map/all_to_all | solution.py:311
  47.4 2.6 %shard_map.105 = (bf16[256,768]{1,0:T(8,128)(2,1)S(1)}, f32[128,768]{1,0:T(8,128)S(1)}, bf16[256,768]{1,0:T(8,128)(2,1)S(1)}, bf16[256,768]{1,0:T(8,128)(2,1)S(1)}) custom-call(bf16[256,896]{1,0:T(8,128)(2,1)S(1)} %reshape.61.got_ref, bf16[128,768]{1,0:T(8,128)(2,1)} %get-tuple-element.17.hidden_in, bf16[768,768]{1,0:T(8,128)(2,1)S(1)} %copy-done, ...), custom_call_target="tpu_custom_call" | custom-call | tf_op jit(solution)/shard_map/pallas_call | solution.py:319
  50.9 8.7 %all-to-all-start.1 = ((bf16[64,4,768]{2,1,0:T(4,128)(2,1)}), bf16[64,4,768]{2,1,0:T(4,128)(2,1)S(1)}, u32[]{:S(2)}, u32[]{:S(2)}) async-start(bf16[64,4,768]{2,1,0:T(4,128)(2,1)} %reshape.63), calls=%async_computation.1 | async-start | bytes 786432 | tf_op jit(solution)/shard_map/all_to_all | solution.py:343
  59.8 1.7 %pad_maximum_fusion = bf16[160,768]{1,0:T(8,128)(2,1)} fusion(bf16[16,768]{1,0:T(8,128)(2,1)S(1)} %collective-permute-done.1.below_ref, bf16[128,768]{1,0:T(8,128)(2,1)} %bitcast.20, bf16[16,768]{1,0:T(8,128)(2,1)S(1)} %collective-permute-done.above_ref), kind=kLoop, calls=%fused_computation.22 | loop fusion | flops 737280 | bytes 491520 | tf_op jit(solution)/shard_map/concatenate | solution.py:286
  63.0 9.5 %collective-permute-done.5.refs_1_ = bf16[160,768]{1,0:T(8,128)(2,1)S(1)} collective-permute-done((bf16[160,768]{1,0:T(8,128)(2,1)}, bf16[160,768]{1,0:T(8,128)(2,1)S(1)}, u32[]{:S(2)}, u32[]{:S(2)}) %collective-permute-start.5) | collective-permute-done | bytes 245792 | tf_op jit(solution)/shard_map/ppermute | solution.py:42
  72.5 1.5 %shard_map.107 = (bf16[768,192]{1,0:T(8,128)(2,1)S(1)}, bf16[768,192]{1,0:T(8,128)(2,1)}) custom-call(bf16[256,768]{1,0:T(8,128)(2,1)S(1)} %get-tuple-element.22.feature_ref, bf16[256,768]{1,0:T(8,128)(2,1)S(1)} %collective-permute-done.7.feature_core_ref, bf16[256,192]{1,0:T(8,128)(2,1)S(1)} %get-tuple-element.32.refs_0_, ...), custom_call_target="tpu_custom_call" | custom-call | tf_op jit(solution)/shard_map/pallas_call | solution.py:358
  74.0 1.6 %collective-permute-start.10 = (bf16[768,192]{1,0:T(8,128)(2,1)}, bf16[768,192]{1,0:T(8,128)(2,1)S(1)}, u32[]{:S(2)}, u32[]{:S(2)}) collective-permute-start(bf16[768,192]{1,0:T(8,128)(2,1)} %get-tuple-element.25), channel_id=1, source_target_pairs={{0,128},{64,192},{128,0},{192,64},{1,129},{65,193},{129,1},{193,65... | collective-permute-start | bytes 884744 | tf_op jit(solution)/shard_map/ppermute | solution.py:42
  76.9 1.2 collective-permute-start.13
  78.6 7.6 %collective-permute-done.10.refs_2_ = bf16[768,192]{1,0:T(8,128)(2,1)S(1)} collective-permute-done((bf16[768,192]{1,0:T(8,128)(2,1)}, bf16[768,192]{1,0:T(8,128)(2,1)S(1)}, u32[]{:S(2)}, u32[]{:S(2)}) %collective-permute-start.10) | collective-permute-done | bytes 294944 | tf_op jit(solution)/shard_map/ppermute | solution.py:42
  86.2 1.4 collective-permute-done.12.refs_5_
  88.0 3.0 %shard_map.108 = bf16[6912,128]{1,0:T(8,128)(2,1)} custom-call(bf16[768,640]{1,0:T(8,128)(2,1)S(1)} %shard_map.106.refs_0_, bf16[768,192]{1,0:T(8,128)(2,1)S(1)} %get-tuple-element.24.refs_1_, bf16[768,192]{1,0:T(8,128)(2,1)S(1)} %collective-permute-done.10.refs_2_, bf16[128,192]{1,0:T(8,128)(2,1)S(1)} %get-tuple-element.36.refs_3_, ...), custom_call_target="tpu_custom_call" | custom-call | tf_op jit(solution)/shard_map/pallas_call | solution.py:380
  91.0 7.3 %all-to-all-start.2 = ((bf16[16,432,128]{2,1,0:T(8,128)(2,1)}), bf16[16,432,128]{2,1,0:T(8,128)(2,1)S(1)}, u32[]{:S(2)}, u32[]{:S(2)}) async-start(bf16[16,432,128]{2,1,0:T(8,128)(2,1)} %bitcast.7), calls=%async_computation.2 | async-start | bytes 3538944 | tf_op jit(solution)/shard_map/all_to_all | solution.py:389
  98.4 3.8 %collective-permute-start.2 = (bf16[16,768]{1,0:T(8,128)(2,1)S(1)}, bf16[16,768]{1,0:T(8,128)(2,1)S(1)}, u32[]{:S(2)}, u32[]{:S(2)}) collective-permute-start(bf16[16,768]{1,0:T(8,128)(2,1)S(1)} %get-tuple-element.37), channel_id=1, source_target_pairs={{0,1},{1,2},{2,3},{3,4},{4,5},{5,6},{6,7},{7,8},{8,9},{9,10},{10,1... | collective-permute-start | bytes 73736 | tf_op jit(solution)/shard_map/ppermute | solution.py:32
  102.2 2.0 %collective-permute-start.3 = (bf16[16,768]{1,0:T(8,128)(2,1)S(1)}, bf16[16,768]{1,0:T(8,128)(2,1)S(1)}, u32[]{:S(2)}, u32[]{:S(2)}) collective-permute-start(bf16[16,768]{1,0:T(8,128)(2,1)S(1)} %get-tuple-element.38), channel_id=1, source_target_pairs={{1,0},{2,1},{3,2},{4,3},{5,4},{6,5},{7,6},{8,7},{9,8},{10,9},{11,1... | collective-permute-start | bytes 73736 | tf_op jit(solution)/shard_map/ppermute | solution.py:33
  104.3 19.7 %collective-permute-done.2 = bf16[16,768]{1,0:T(8,128)(2,1)S(1)} collective-permute-done((bf16[16,768]{1,0:T(8,128)(2,1)S(1)}, bf16[16,768]{1,0:T(8,128)(2,1)S(1)}, u32[]{:S(2)}, u32[]{:S(2)}) %collective-permute-start.2) | collective-permute-done | bytes 24608 | tf_op jit(solution)/shard_map/ppermute | solution.py:32
  124.0 4.7 %fusion.6 = f32[160,3840]{1,0:T(8,128)S(1)} fusion(bf16[3840,768]{1,0:T(8,128)(2,1)} %weight_ref.1, bf16[16,768]{1,0:T(8,128)(2,1)S(1)} %collective-permute-done.3, bf16[128,768]{1,0:T(8,128)(2,1)S(1)} %multiply_convert_fusion, bf16[16,768]{1,0:T(8,128)(2,1)S(1)} %collective-permute-done.2), kind=kOutput, calls=%fused_computation.16 | convolution fusion | flops 944455680 | bytes 8601600 | tf_op jit(solution)/shard_map/dot_general | solution.py:434
  129.9 5.8 %all-to-all-start.3 = ((bf16[4,144,128]{2,1,0:T(8,128)(2,1)}), bf16[4,144,128]{2,1,0:T(8,128)(2,1)S(1)}, u32[]{:S(2)}, u32[]{:S(2)}) async-start(bf16[4,144,128]{2,1,0:T(8,128)(2,1)} %shard_map.109), calls=%async_computation.3 | async-start | bytes 294912 | tf_op jit(solution)/shard_map/all_to_all | solution.py:405
  136.5 8.2 %all-to-all-done.3 = bf16[4,144,128]{2,1,0:T(8,128)(2,1)S(1)} async-done(((bf16[4,144,128]{2,1,0:T(8,128)(2,1)}), bf16[4,144,128]{2,1,0:T(8,128)(2,1)S(1)}, u32[]{:S(2)}, u32[]{:S(2)}) %all-to-all-start.3) | async-done | bytes 147488 | tf_op jit(solution)/shard_map/all_to_all | solution.py:405
  (58 shorter events, 11.6 us)
Async XLA Ops:
  1.4 10.3 %collective-permute-start = (bf16[16,768]{1,0:T(8,128)(2,1)S(1)}, bf16[16,768]{1,0:T(8,128)(2,1)S(1)}, u32[]{:S(2)}, u32[]{:S(2)}) collective-permute-start(bf16[16,768]{1,0:T(8,128)(2,1)S(1)} %get-tuple-element.40), channel_id=1, source_target_pairs={{0,1},{1,2},{2,3},{3,4},{4,5},{5,6},{6,7},{7,8},{8,9},{9,10},{10,1... | collective-permute-start | bytes 73736 | tf_op jit(solution)/shard_map/ppermute | solution.py:32
  6.5 8.9 %collective-permute-start.1 = (bf16[16,768]{1,0:T(8,128)(2,1)S(1)}, bf16[16,768]{1,0:T(8,128)(2,1)S(1)}, u32[]{:S(2)}, u32[]{:S(2)}) collective-permute-start(bf16[16,768]{1,0:T(8,128)(2,1)S(1)} %get-tuple-element.39), channel_id=1, source_target_pairs={{1,0},{2,1},{3,2},{4,3},{5,4},{6,5},{7,6},{8,7},{9,8},{10,9},{11,1... | collective-permute-start | bytes 73736 | tf_op jit(solution)/shard_map/ppermute | solution.py:33
  15.4 17.8 %copy-start.4 = (bf16[768]{0:T(1024)(128)(2,1)S(1)}, bf16[768]{0:T(1024)(128)(2,1)}, u32[]{:S(2)}) copy-start(bf16[768]{0:T(1024)(128)(2,1)} %param.12) | copy-start | bytes 4612
  19.6 27.8 %copy-start = (bf16[768,768]{1,0:T(8,128)(2,1)S(1)}, bf16[768,768]{1,0:T(8,128)(2,1)}, u32[]{:S(2)}) copy-start(bf16[768,768]{1,0:T(8,128)(2,1)} %first_ref.1) | copy-start | bytes 3538948
  20.5 26.8 %all-to-all-start = ((bf16[64,4,896]{2,1,0:T(4,128)(2,1)}), bf16[64,4,896]{2,1,0:T(4,128)(2,1)S(1)}, u32[]{:S(2)}, u32[]{:S(2)}) async-start(bf16[64,4,896]{2,1,0:T(4,128)(2,1)} %reshape.60), calls=%async_computation | async-start | bytes 917504 | tf_op jit(solution)/shard_map/all_to_all | solution.py:311
  50.9 24.6 %all-to-all-start.1 = ((bf16[64,4,768]{2,1,0:T(4,128)(2,1)}), bf16[64,4,768]{2,1,0:T(4,128)(2,1)S(1)}, u32[]{:S(2)}, u32[]{:S(2)}) async-start(bf16[64,4,768]{2,1,0:T(4,128)(2,1)} %reshape.63), calls=%async_computation.1 | async-start | bytes 786432 | tf_op jit(solution)/shard_map/all_to_all | solution.py:343
  59.7 16.2 %copy-start.3 = (f32[128,768]{1,0:T(8,128)S(1)}, f32[128,768]{1,0:T(8,128)}, u32[]{:S(2)}) copy-start(f32[128,768]{1,0:T(8,128)} %get-tuple-element.20) | copy-start | bytes 1179652
  59.7 12.8 %collective-permute-start.7 = (bf16[256,768]{1,0:T(8,128)(2,1)S(1)}, bf16[256,768]{1,0:T(8,128)(2,1)S(1)}, u32[]{:S(2)}, u32[]{:S(2)}) collective-permute-start(bf16[256,768]{1,0:T(8,128)(2,1)S(1)} %get-tuple-element.22.feature_ref), channel_id=1, source_target_pairs={{0,64},{64,0},{128,192},{192,128},{1,65},{65,1},{129,193},{193,129... | collective-permute-start | bytes 1179656 | tf_op jit(solution)/shard_map/ppermute | solution.py:38
  61.5 11.0 %collective-permute-start.5 = (bf16[160,768]{1,0:T(8,128)(2,1)}, bf16[160,768]{1,0:T(8,128)(2,1)S(1)}, u32[]{:S(2)}, u32[]{:S(2)}) collective-permute-start(bf16[160,768]{1,0:T(8,128)(2,1)} %pad_maximum_fusion), channel_id=1, source_target_pairs={{0,128},{64,192},{128,0},{192,64},{1,129},{65,193},{129,1},{193,65... | collective-permute-start | bytes 737288 | tf_op jit(solution)/shard_map/ppermute | solution.py:42
  62.2 15.9 %copy-start.1 = (bf16[160,768]{1,0:T(8,128)(2,1)S(1)}, bf16[160,768]{1,0:T(8,128)(2,1)}, u32[]{:S(2)}) copy-start(bf16[160,768]{1,0:T(8,128)(2,1)} %get-tuple-element.21.own_ref) | copy-start | bytes 737284
  62.2 10.3 %collective-permute-start.8 = (bf16[256,192]{1,0:T(8,128)(2,1)S(1)}, bf16[256,192]{1,0:T(8,128)(2,1)S(1)}, u32[]{:S(2)}, u32[]{:S(2)}) collective-permute-start(bf16[256,192]{1,0:T(8,128)(2,1)S(1)} %get-tuple-element.30), channel_id=1, source_target_pairs={{0,64},{64,0},{128,192},{192,128},{1,65},{65,1},{129,193},{193,129... | collective-permute-start | bytes 294920 | tf_op jit(solution)/shard_map/ppermute | solution.py:38
  62.4 10.0 %collective-permute-start.9 = (bf16[256,192]{1,0:T(8,128)(2,1)S(1)}, bf16[256,192]{1,0:T(8,128)(2,1)S(1)}, u32[]{:S(2)}, u32[]{:S(2)}) collective-permute-start(bf16[256,192]{1,0:T(8,128)(2,1)S(1)} %get-tuple-element.29), channel_id=1, source_target_pairs={{0,64},{64,0},{128,192},{192,128},{1,65},{65,1},{129,193},{193,129... | collective-permute-start | bytes 294920 | tf_op jit(solution)/shard_map/ppermute | solution.py:38
  62.8 14.1 %collective-permute-start.4 = (bf16[160,768]{1,0:T(8,128)(2,1)}, bf16[160,768]{1,0:T(8,128)(2,1)S(1)}, u32[]{:S(2)}, u32[]{:S(2)}) collective-permute-start(bf16[160,768]{1,0:T(8,128)(2,1)} %pad_maximum_fusion), channel_id=1, source_target_pairs={{0,64},{64,0},{128,192},{192,128},{1,65},{65,1},{129,193},{193,129... | collective-permute-start | bytes 737288 | tf_op jit(solution)/shard_map/ppermute | solution.py:38
  72.4 5.7 %collective-permute-start.6 = (bf16[160,768]{1,0:T(8,128)(2,1)S(1)}, bf16[160,768]{1,0:T(8,128)(2,1)S(1)}, u32[]{:S(2)}, u32[]{:S(2)}) collective-permute-start(bf16[160,768]{1,0:T(8,128)(2,1)S(1)} %collective-permute-done.5.refs_1_), channel_id=1, source_target_pairs={{0,64},{64,0},{128,192},{192,128},{1,65},{65,1},{129,193},{193,129... | collective-permute-start | bytes 737288 | tf_op jit(solution)/shard_map/ppermute | solution.py:38
  74.0 12.2 %collective-permute-start.10 = (bf16[768,192]{1,0:T(8,128)(2,1)}, bf16[768,192]{1,0:T(8,128)(2,1)S(1)}, u32[]{:S(2)}, u32[]{:S(2)}) collective-permute-start(bf16[768,192]{1,0:T(8,128)(2,1)} %get-tuple-element.25), channel_id=1, source_target_pairs={{0,128},{64,192},{128,0},{192,64},{1,129},{65,193},{129,1},{193,65... | collective-permute-start | bytes 884744 | tf_op jit(solution)/shard_map/ppermute | solution.py:42
  76.1 10.0 %collective-permute-start.11 = (bf16[128,192]{1,0:T(8,128)(2,1)S(1)}, bf16[128,192]{1,0:T(8,128)(2,1)S(1)}, u32[]{:S(2)}, u32[]{:S(2)}) collective-permute-start(bf16[128,192]{1,0:T(8,128)(2,1)S(1)} %get-tuple-element.35), channel_id=1, source_target_pairs={{0,64},{64,0},{128,192},{192,128},{1,65},{65,1},{129,193},{193,129... | collective-permute-start | bytes 147464 | tf_op jit(solution)/shard_map/ppermute | solution.py:51
  76.4 11.1 %collective-permute-start.12 = (bf16[128,192]{1,0:T(8,128)(2,1)S(1)}, bf16[128,192]{1,0:T(8,128)(2,1)S(1)}, u32[]{:S(2)}, u32[]{:S(2)}) collective-permute-start(bf16[128,192]{1,0:T(8,128)(2,1)S(1)} %get-tuple-element.34), channel_id=1, source_target_pairs={{0,128},{64,192},{128,0},{192,64},{1,129},{65,193},{129,1},{193,65... | collective-permute-start | bytes 147464 | tf_op jit(solution)/shard_map/ppermute | solution.py:51
  76.9 11.1 %collective-permute-start.13 = (bf16[128,192]{1,0:T(8,128)(2,1)S(1)}, bf16[128,192]{1,0:T(8,128)(2,1)S(1)}, u32[]{:S(2)}, u32[]{:S(2)}) collective-permute-start(bf16[128,192]{1,0:T(8,128)(2,1)S(1)} %get-tuple-element.33), channel_id=1, source_target_pairs={{0,192},{64,128},{128,64},{192,0},{1,193},{65,129},{129,65},{193,1... | collective-permute-start | bytes 147464 | tf_op jit(solution)/shard_map/ppermute | solution.py:51
  91.0 38.0 %all-to-all-start.2 = ((bf16[16,432,128]{2,1,0:T(8,128)(2,1)}), bf16[16,432,128]{2,1,0:T(8,128)(2,1)S(1)}, u32[]{:S(2)}, u32[]{:S(2)}) async-start(bf16[16,432,128]{2,1,0:T(8,128)(2,1)} %bitcast.7), calls=%async_computation.2 | async-start | bytes 3538944 | tf_op jit(solution)/shard_map/all_to_all | solution.py:389
  98.4 25.6 %collective-permute-start.2 = (bf16[16,768]{1,0:T(8,128)(2,1)S(1)}, bf16[16,768]{1,0:T(8,128)(2,1)S(1)}, u32[]{:S(2)}, u32[]{:S(2)}) collective-permute-start(bf16[16,768]{1,0:T(8,128)(2,1)S(1)} %get-tuple-element.37), channel_id=1, source_target_pairs={{0,1},{1,2},{2,3},{3,4},{4,5},{5,6},{6,7},{7,8},{8,9},{9,10},{10,1... | collective-permute-start | bytes 73736 | tf_op jit(solution)/shard_map/ppermute | solution.py:32
  102.2 21.8 %collective-permute-start.3 = (bf16[16,768]{1,0:T(8,128)(2,1)S(1)}, bf16[16,768]{1,0:T(8,128)(2,1)S(1)}, u32[]{:S(2)}, u32[]{:S(2)}) collective-permute-start(bf16[16,768]{1,0:T(8,128)(2,1)S(1)} %get-tuple-element.38), channel_id=1, source_target_pairs={{1,0},{2,1},{3,2},{4,3},{5,4},{6,5},{7,6},{8,7},{9,8},{10,9},{11,1... | collective-permute-start | bytes 73736 | tf_op jit(solution)/shard_map/ppermute | solution.py:33
  104.3 24.5 %copy-start.2 = (bf16[1,128,768]{2,1,0:T(8,128)(2,1)S(1)}, bf16[1,128,768]{2,1,0:T(8,128)(2,1)}, u32[]{:S(2)}) copy-start(bf16[1,128,768]{2,1,0:T(8,128)(2,1)} %param.9) | copy-start | bytes 589828
  129.9 14.8 %all-to-all-start.3 = ((bf16[4,144,128]{2,1,0:T(8,128)(2,1)}), bf16[4,144,128]{2,1,0:T(8,128)(2,1)S(1)}, u32[]{:S(2)}, u32[]{:S(2)}) async-start(bf16[4,144,128]{2,1,0:T(8,128)(2,1)} %shard_map.109), calls=%async_computation.3 | async-start | bytes 294912 | tf_op jit(solution)/shard_map/all_to_all | solution.py:405

commit v11 on v10

--- a/solution.py
+++ b/solution.py
@@ -111,9 +111,7 @@
     peers, out_ref = refs[:-1], refs[-1]
     pieces = [own_ref[...].astype(jnp.float32)]
     for peer in peers:
-        values = peer[...].astype(jnp.float32)
-        inverse = lax.rsqrt(jnp.mean(values * values, axis=1, keepdims=True) + 1e-05)
-        pieces.append(values * inverse)
+        pieces.append(peer[...].astype(jnp.float32))
     out_ref[...] = jnp.concatenate(pieces, axis=0).T.astype(jnp.bfloat16)
 
 
@@ -283,10 +281,6 @@
     hits = (donor_slot[:, None] == row_ids[None, :]).astype(jnp.bfloat16)
     hits, notes = lax.optimization_barrier((hits, notes))
 
-    padded_input = jnp.concatenate([above, activations[0], below], axis=0)
-    core_input, z_input = swap_core(padded_input), swap_z(padded_input)
-    padded_peers = padded_input, core_input, z_input, swap_core(z_input)
-
     spec, far = pl.BlockSpec(memory_space=pltpu.VMEM), pl.BlockSpec(memory_space=pltpu.HBM)
     padded, hidden, slope, sent = pl.pallas_call(
         functools.partial(conv_kernel, tap_count),
@@ -308,6 +302,8 @@
         ],
         compiler_params=pltpu.CompilerParams(vmem_limit_bytes=KERNEL_VMEM),
     )(above, below, hits, notes, in_hbm(activations[0]), in_hbm(conv_weight))
+    core_input, z_input = swap_core(padded), swap_z(padded)
+    padded_peers = padded, core_input, z_input, swap_core(z_input)
     got = lax.all_to_all(
         sent.reshape(shards, capacity, out_count + LANES),
         "seq",

time: 146 us -> 145 us (level)
    concatenate x1 -> x0, other arithmetic: 1.68 us -> none  [per_device(): padded_input = jnp.concatenate([above, activations[0], below], axis=0)]
where the time goes in v11:
time: 145 us; the launch traced here: 144 us
  waiting for transfers between devices  63.2 us (44%)
  starting transfers between devices  53 us (37%)
  Pallas kernels  11.8 us (8%)
  other arithmetic  6.01 us (4%)
  matrix products  5.13 us (4%)
  local copies, waits for them, and re-layouts  4.15 us (3%)
    ppermute x2, waiting for transfers between devices, seq_halo(): lax.ppermute(cells[-width:], 'seq', [(i, i + 1) for i in range(count - 1)])  19.7 us
    ppermute x2, waiting for transfers between devices, swap_z(): return lax.ppermute(field, 'dp', [(0, 2), (1, 3), (2, 0), (3, 1)])  16.1 us
    all_to_all x1, waiting for transfers between devices, per_device(): lax.all_to_all(sent.reshape(shards, capacity, out_count + LANES), 'seq',...  14.1 us
    all_to_all x1, starting transfers between devices, per_device(): lax.all_to_all(sent.reshape(shards, capacity, out_count + LANES), 'seq',...  12.6 us
    ppermute x2, starting transfers between devices, seq_halo(): lax.ppermute(cells[-width:], 'seq', [(i, i + 1) for i in range(count - 1)])  9.01 us
    all_to_all x1, starting transfers between devices, per_device(): lax.all_to_all(back.reshape(shards, capacity, out_count), 'seq', split_ax...  8.96 us
    all_to_all x1, waiting for transfers between devices, per_device(): lax.all_to_all(folded, 'seq', split_axis=0, concat_axis=0, tiled=True, ax...  7.76 us
    all_to_all x1, starting transfers between devices, per_device(): lax.all_to_all(term.reshape(ys * xs, chunk, LANES), 'seq', split_axis=0,...  7.29 us
  transfers between devices with their start and end apart: 18, of which 8 were waited for; matrix products, arithmetic and copies ran while one was open for 8% of the time, Pallas kernels for 1%

profile of v11, /device:TPU:6, one launch (start us, length us, event | category | flops | bytes accessed | tf_op | source)
XLA Modules:
  0.0 144.2 jit_solution(11188762081148834015)
XLA Ops:
  1.4 5.1 %collective-permute-start = (bf16[16,768]{1,0:T(8,128)(2,1)S(1)}, bf16[16,768]{1,0:T(8,128)(2,1)S(1)}, u32[]{:S(2)}, u32[]{:S(2)}) collective-permute-start(bf16[16,768]{1,0:T(8,128)(2,1)S(1)} %get-tuple-element.40), channel_id=1, source_target_pairs={{0,1},{1,2},{2,3},{3,4},{4,5},{5,6},{6,7},{7,8},{8,9},{9,10},{10,1... | collective-permute-start | bytes 73736 | tf_op jit(solution)/shard_map/ppermute | solution.py:32
  6.5 1.9 %collective-permute-start.1 = (bf16[16,768]{1,0:T(8,128)(2,1)S(1)}, bf16[16,768]{1,0:T(8,128)(2,1)S(1)}, u32[]{:S(2)}, u32[]{:S(2)}) collective-permute-start(bf16[16,768]{1,0:T(8,128)(2,1)S(1)} %get-tuple-element.39), channel_id=1, source_target_pairs={{1,0},{2,1},{3,2},{4,3},{5,4},{6,5},{7,6},{8,7},{9,8},{10,9},{11,1... | collective-permute-start | bytes 73736 | tf_op jit(solution)/shard_map/ppermute | solution.py:33
  11.7 3.7 %collective-permute-done.1.below_ref = bf16[16,768]{1,0:T(8,128)(2,1)S(1)} collective-permute-done((bf16[16,768]{1,0:T(8,128)(2,1)S(1)}, bf16[16,768]{1,0:T(8,128)(2,1)S(1)}, u32[]{:S(2)}, u32[]{:S(2)}) %collective-permute-start.1) | collective-permute-done | bytes 24608 | tf_op jit(solution)/shard_map/ppermute | solution.py:33
  15.4 4.2 %shard_map.104 = (bf16[160,768]{1,0:T(8,128)(2,1)}, bf16[128,768]{1,0:T(8,128)(2,1)}, f32[128,768]{1,0:T(8,128)}, bf16[256,896]{1,0:T(8,128)(2,1)S(1)}) custom-call(bf16[16,768]{1,0:T(8,128)(2,1)S(1)} %collective-permute-done.above_ref, bf16[16,768]{1,0:T(8,128)(2,1)S(1)} %collective-permute-done.1.below_ref, bf16[256,128]{1,0:T(8,128)(2,1)S(1)} %fusion.13.hits_ref, ...), custom_call_target="tpu_custom_call" | custom-call | tf_op jit(solution)/shard_map/pallas_call | solution.py:285
  20.5 12.6 %all-to-all-start = ((bf16[64,4,896]{2,1,0:T(4,128)(2,1)}), bf16[64,4,896]{2,1,0:T(4,128)(2,1)S(1)}, u32[]{:S(2)}, u32[]{:S(2)}) async-start(bf16[64,4,896]{2,1,0:T(4,128)(2,1)} %reshape.60), calls=%async_computation | async-start | bytes 917504 | tf_op jit(solution)/shard_map/all_to_all | solution.py:307
  33.2 14.1 %all-to-all-done = bf16[64,4,896]{2,1,0:T(4,128)(2,1)S(1)} async-done(((bf16[64,4,896]{2,1,0:T(4,128)(2,1)}), bf16[64,4,896]{2,1,0:T(4,128)(2,1)S(1)}, u32[]{:S(2)}, u32[]{:S(2)}) %all-to-all-start) | async-done | bytes 458784 | tf_op jit(solution)/shard_map/all_to_all | solution.py:307
  47.4 2.6 %shard_map.105 = (bf16[256,768]{1,0:T(8,128)(2,1)S(1)}, f32[128,768]{1,0:T(8,128)S(1)}, bf16[256,768]{1,0:T(8,128)(2,1)S(1)}, bf16[256,768]{1,0:T(8,128)(2,1)S(1)}) custom-call(bf16[256,896]{1,0:T(8,128)(2,1)S(1)} %reshape.61.got_ref, bf16[128,768]{1,0:T(8,128)(2,1)} %get-tuple-element.17.hidden_in, bf16[768,768]{1,0:T(8,128)(2,1)S(1)} %copy-done, ...), custom_call_target="tpu_custom_call" | custom-call | tf_op jit(solution)/shard_map/pallas_call | solution.py:315
  50.9 9.0 %all-to-all-start.1 = ((bf16[64,4,768]{2,1,0:T(4,128)(2,1)}), bf16[64,4,768]{2,1,0:T(4,128)(2,1)}, u32[]{:S(2)}, u32[]{:S(2)}) async-start(bf16[64,4,768]{2,1,0:T(4,128)(2,1)} %reshape.63), calls=%async_computation.1 | async-start | bytes 786432 | tf_op jit(solution)/shard_map/all_to_all | solution.py:339
  60.0 0.9 collective-permute-start.5
  61.9 10.5 %collective-permute-done.5.refs_1_ = bf16[160,768]{1,0:T(8,128)(2,1)S(1)} collective-permute-done((bf16[160,768]{1,0:T(8,128)(2,1)S(1)}, bf16[160,768]{1,0:T(8,128)(2,1)S(1)}, u32[]{:S(2)}, u32[]{:S(2)}) %collective-permute-start.5) | collective-permute-done | bytes 245792 | tf_op jit(solution)/shard_map/ppermute | solution.py:42
  73.2 1.7 %collective-permute-start.10 = (bf16[768,192]{1,0:T(8,128)(2,1)S(1)}, bf16[768,192]{1,0:T(8,128)(2,1)S(1)}, u32[]{:S(2)}, u32[]{:S(2)}) collective-permute-start(bf16[768,192]{1,0:T(8,128)(2,1)S(1)} %get-tuple-element.25), channel_id=1, source_target_pairs={{0,128},{64,192},{128,0},{192,64},{1,129},{65,193},{129,1},{193,65... | collective-permute-start | bytes 884744 | tf_op jit(solution)/shard_map/ppermute | solution.py:42
  74.9 1.1 reshape.64
  76.2 1.1 multiply_convert_fusion
  78.2 1.2 collective-permute-start.13
  79.8 5.5 %collective-permute-done.10.refs_2_ = bf16[768,192]{1,0:T(8,128)(2,1)S(1)} collective-permute-done((bf16[768,192]{1,0:T(8,128)(2,1)S(1)}, bf16[768,192]{1,0:T(8,128)(2,1)S(1)}, u32[]{:S(2)}, u32[]{:S(2)}) %collective-permute-start.10) | collective-permute-done | bytes 294944 | tf_op jit(solution)/shard_map/ppermute | solution.py:42
  85.3 1.4 collective-permute-done.12.refs_5_
  87.2 3.0 %shard_map.108 = bf16[6912,128]{1,0:T(8,128)(2,1)} custom-call(bf16[768,640]{1,0:T(8,128)(2,1)S(1)} %shard_map.106.refs_0_, bf16[768,192]{1,0:T(8,128)(2,1)S(1)} %get-tuple-element.24.refs_1_, bf16[768,192]{1,0:T(8,128)(2,1)S(1)} %collective-permute-done.10.refs_2_, bf16[128,192]{1,0:T(8,128)(2,1)S(1)} %get-tuple-element.36.refs_3_, ...), custom_call_target="tpu_custom_call" | custom-call | tf_op jit(solution)/shard_map/pallas_call | solution.py:376
  90.2 7.3 %all-to-all-start.2 = ((bf16[16,432,128]{2,1,0:T(8,128)(2,1)}), bf16[16,432,128]{2,1,0:T(8,128)(2,1)S(1)}, u32[]{:S(2)}, u32[]{:S(2)}) async-start(bf16[16,432,128]{2,1,0:T(8,128)(2,1)} %bitcast.7), calls=%async_computation.2 | async-start | bytes 3538944 | tf_op jit(solution)/shard_map/all_to_all | solution.py:385
  97.5 3.9 %collective-permute-start.2 = (bf16[16,768]{1,0:T(8,128)(2,1)S(1)}, bf16[16,768]{1,0:T(8,128)(2,1)S(1)}, u32[]{:S(2)}, u32[]{:S(2)}) collective-permute-start(bf16[16,768]{1,0:T(8,128)(2,1)S(1)} %get-tuple-element.37), channel_id=1, source_target_pairs={{0,1},{1,2},{2,3},{3,4},{4,5},{5,6},{6,7},{7,8},{8,9},{9,10},{10,1... | collective-permute-start | bytes 73736 | tf_op jit(solution)/shard_map/ppermute | solution.py:32
  101.4 1.9 %collective-permute-start.3 = (bf16[16,768]{1,0:T(8,128)(2,1)S(1)}, bf16[16,768]{1,0:T(8,128)(2,1)S(1)}, u32[]{:S(2)}, u32[]{:S(2)}) collective-permute-start(bf16[16,768]{1,0:T(8,128)(2,1)S(1)} %get-tuple-element.38), channel_id=1, source_target_pairs={{1,0},{2,1},{3,2},{4,3},{5,4},{6,5},{7,6},{8,7},{9,8},{10,9},{11,1... | collective-permute-start | bytes 73736 | tf_op jit(solution)/shard_map/ppermute | solution.py:33
  103.4 19.7 %collective-permute-done.2 = bf16[16,768]{1,0:T(8,128)(2,1)S(1)} collective-permute-done((bf16[16,768]{1,0:T(8,128)(2,1)S(1)}, bf16[16,768]{1,0:T(8,128)(2,1)S(1)}, u32[]{:S(2)}, u32[]{:S(2)}) %collective-permute-start.2) | collective-permute-done | bytes 24608 | tf_op jit(solution)/shard_map/ppermute | solution.py:32
  123.1 4.7 %fusion.6 = f32[160,3840]{1,0:T(8,128)S(1)} fusion(bf16[3840,768]{1,0:T(8,128)(2,1)} %weight_ref.1, bf16[16,768]{1,0:T(8,128)(2,1)S(1)} %collective-permute-done.3, bf16[128,768]{1,0:T(8,128)(2,1)S(1)} %multiply_convert_fusion, bf16[16,768]{1,0:T(8,128)(2,1)S(1)} %collective-permute-done.2), kind=kOutput, calls=%fused_computation.16 | convolution fusion | flops 944455680 | bytes 8601600 | tf_op jit(solution)/shard_map/dot_general | solution.py:430
  129.0 5.9 %all-to-all-start.3 = ((bf16[4,144,128]{2,1,0:T(8,128)(2,1)}), bf16[4,144,128]{2,1,0:T(8,128)(2,1)S(1)}, u32[]{:S(2)}, u32[]{:S(2)}) async-start(bf16[4,144,128]{2,1,0:T(8,128)(2,1)} %shard_map.109), calls=%async_computation.3 | async-start | bytes 294912 | tf_op jit(solution)/shard_map/all_to_all | solution.py:401
  135.7 7.8 %all-to-all-done.3 = bf16[4,144,128]{2,1,0:T(8,128)(2,1)S(1)} async-done(((bf16[4,144,128]{2,1,0:T(8,128)(2,1)}), bf16[4,144,128]{2,1,0:T(8,128)(2,1)S(1)}, u32[]{:S(2)}, u32[]{:S(2)}) %all-to-all-start.3) | async-done | bytes 147488 | tf_op jit(solution)/shard_map/all_to_all | solution.py:401
  (55 shorter events, 12.4 us)
Async XLA Ops:
  1.4 10.3 %collective-permute-start = (bf16[16,768]{1,0:T(8,128)(2,1)S(1)}, bf16[16,768]{1,0:T(8,128)(2,1)S(1)}, u32[]{:S(2)}, u32[]{:S(2)}) collective-permute-start(bf16[16,768]{1,0:T(8,128)(2,1)S(1)} %get-tuple-element.40), channel_id=1, source_target_pairs={{0,1},{1,2},{2,3},{3,4},{4,5},{5,6},{6,7},{7,8},{8,9},{9,10},{10,1... | collective-permute-start | bytes 73736 | tf_op jit(solution)/shard_map/ppermute | solution.py:32
  6.5 8.9 %collective-permute-start.1 = (bf16[16,768]{1,0:T(8,128)(2,1)S(1)}, bf16[16,768]{1,0:T(8,128)(2,1)S(1)}, u32[]{:S(2)}, u32[]{:S(2)}) collective-permute-start(bf16[16,768]{1,0:T(8,128)(2,1)S(1)} %get-tuple-element.39), channel_id=1, source_target_pairs={{1,0},{2,1},{3,2},{4,3},{5,4},{6,5},{7,6},{8,7},{9,8},{10,9},{11,1... | collective-permute-start | bytes 73736 | tf_op jit(solution)/shard_map/ppermute | solution.py:33
  15.4 17.8 %copy-start.3 = (bf16[768]{0:T(1024)(128)(2,1)S(1)}, bf16[768]{0:T(1024)(128)(2,1)}, u32[]{:S(2)}) copy-start(bf16[768]{0:T(1024)(128)(2,1)} %param.12) | copy-start | bytes 4612
  19.6 27.8 %copy-start = (bf16[768,768]{1,0:T(8,128)(2,1)S(1)}, bf16[768,768]{1,0:T(8,128)(2,1)}, u32[]{:S(2)}) copy-start(bf16[768,768]{1,0:T(8,128)(2,1)} %first_ref.1) | copy-start | bytes 3538948
  20.5 26.8 %all-to-all-start = ((bf16[64,4,896]{2,1,0:T(4,128)(2,1)}), bf16[64,4,896]{2,1,0:T(4,128)(2,1)S(1)}, u32[]{:S(2)}, u32[]{:S(2)}) async-start(bf16[64,4,896]{2,1,0:T(4,128)(2,1)} %reshape.60), calls=%async_computation | async-start | bytes 917504 | tf_op jit(solution)/shard_map/all_to_all | solution.py:307
  33.2 26.8 %copy-start.1 = (bf16[160,768]{1,0:T(8,128)(2,1)S(1)}, bf16[160,768]{1,0:T(8,128)(2,1)}, u32[]{:S(2)}) copy-start(bf16[160,768]{1,0:T(8,128)(2,1)} %get-tuple-element.21.own_ref) | copy-start | bytes 737284
  50.9 24.0 %all-to-all-start.1 = ((bf16[64,4,768]{2,1,0:T(4,128)(2,1)}), bf16[64,4,768]{2,1,0:T(4,128)(2,1)}, u32[]{:S(2)}, u32[]{:S(2)}) async-start(bf16[64,4,768]{2,1,0:T(4,128)(2,1)} %reshape.63), calls=%async_computation.1 | async-start | bytes 786432 | tf_op jit(solution)/shard_map/all_to_all | solution.py:339
  59.9 12.6 %collective-permute-start.7 = (bf16[256,768]{1,0:T(8,128)(2,1)S(1)}, bf16[256,768]{1,0:T(8,128)(2,1)S(1)}, u32[]{:S(2)}, u32[]{:S(2)}) collective-permute-start(bf16[256,768]{1,0:T(8,128)(2,1)S(1)} %get-tuple-element.22.feature_ref), channel_id=1, source_target_pairs={{0,64},{64,0},{128,192},{192,128},{1,65},{65,1},{129,193},{193,129... | collective-permute-start | bytes 1179656 | tf_op jit(solution)/shard_map/ppermute | solution.py:38
  60.0 12.4 %collective-permute-start.5 = (bf16[160,768]{1,0:T(8,128)(2,1)S(1)}, bf16[160,768]{1,0:T(8,128)(2,1)S(1)}, u32[]{:S(2)}, u32[]{:S(2)}) collective-permute-start(bf16[160,768]{1,0:T(8,128)(2,1)S(1)} %copy-done.1), channel_id=1, source_target_pairs={{0,128},{64,192},{128,0},{192,64},{1,129},{65,193},{129,1},{193,65... | collective-permute-start | bytes 737288 | tf_op jit(solution)/shard_map/ppermute | solution.py:42
  61.2 11.3 %collective-permute-start.8 = (bf16[256,192]{1,0:T(8,128)(2,1)S(1)}, bf16[256,192]{1,0:T(8,128)(2,1)S(1)}, u32[]{:S(2)}, u32[]{:S(2)}) collective-permute-start(bf16[256,192]{1,0:T(8,128)(2,1)S(1)} %get-tuple-element.30), channel_id=1, source_target_pairs={{0,64},{64,0},{128,192},{192,128},{1,65},{65,1},{129,193},{193,129... | collective-permute-start | bytes 294920 | tf_op jit(solution)/shard_map/ppermute | solution.py:38
  61.4 11.1 %collective-permute-start.9 = (bf16[256,192]{1,0:T(8,128)(2,1)S(1)}, bf16[256,192]{1,0:T(8,128)(2,1)S(1)}, u32[]{:S(2)}, u32[]{:S(2)}) collective-permute-start(bf16[256,192]{1,0:T(8,128)(2,1)S(1)} %get-tuple-element.29), channel_id=1, source_target_pairs={{0,64},{64,0},{128,192},{192,128},{1,65},{65,1},{129,193},{193,129... | collective-permute-start | bytes 294920 | tf_op jit(solution)/shard_map/ppermute | solution.py:38
  61.8 16.5 %collective-permute-start.4 = (bf16[160,768]{1,0:T(8,128)(2,1)S(1)}, bf16[160,768]{1,0:T(8,128)(2,1)S(1)}, u32[]{:S(2)}, u32[]{:S(2)}) collective-permute-start(bf16[160,768]{1,0:T(8,128)(2,1)S(1)} %copy-done.1), channel_id=1, source_target_pairs={{0,64},{64,0},{128,192},{192,128},{1,65},{65,1},{129,193},{193,129... | collective-permute-start | bytes 737288 | tf_op jit(solution)/shard_map/ppermute | solution.py:38
  72.4 7.0 %collective-permute-start.6 = (bf16[160,768]{1,0:T(8,128)(2,1)S(1)}, bf16[160,768]{1,0:T(8,128)(2,1)S(1)}, u32[]{:S(2)}, u32[]{:S(2)}) collective-permute-start(bf16[160,768]{1,0:T(8,128)(2,1)S(1)} %collective-permute-done.5.refs_1_), channel_id=1, source_target_pairs={{0,64},{64,0},{128,192},{192,128},{1,65},{65,1},{129,193},{193,129... | collective-permute-start | bytes 737288 | tf_op jit(solution)/shard_map/ppermute | solution.py:38
  73.2 12.1 %collective-permute-start.10 = (bf16[768,192]{1,0:T(8,128)(2,1)S(1)}, bf16[768,192]{1,0:T(8,128)(2,1)S(1)}, u32[]{:S(2)}, u32[]{:S(2)}) collective-permute-start(bf16[768,192]{1,0:T(8,128)(2,1)S(1)} %get-tuple-element.25), channel_id=1, source_target_pairs={{0,128},{64,192},{128,0},{192,64},{1,129},{65,193},{129,1},{193,65... | collective-permute-start | bytes 884744 | tf_op jit(solution)/shard_map/ppermute | solution.py:42
  77.5 7.8 %collective-permute-start.11 = (bf16[128,192]{1,0:T(8,128)(2,1)S(1)}, bf16[128,192]{1,0:T(8,128)(2,1)S(1)}, u32[]{:S(2)}, u32[]{:S(2)}) collective-permute-start(bf16[128,192]{1,0:T(8,128)(2,1)S(1)} %get-tuple-element.35), channel_id=1, source_target_pairs={{0,64},{64,0},{128,192},{192,128},{1,65},{65,1},{129,193},{193,129... | collective-permute-start | bytes 147464 | tf_op jit(solution)/shard_map/ppermute | solution.py:51
  77.8 8.9 %collective-permute-start.12 = (bf16[128,192]{1,0:T(8,128)(2,1)S(1)}, bf16[128,192]{1,0:T(8,128)(2,1)S(1)}, u32[]{:S(2)}, u32[]{:S(2)}) collective-permute-start(bf16[128,192]{1,0:T(8,128)(2,1)S(1)} %get-tuple-element.34), channel_id=1, source_target_pairs={{0,128},{64,192},{128,0},{192,64},{1,129},{65,193},{129,1},{193,65... | collective-permute-start | bytes 147464 | tf_op jit(solution)/shard_map/ppermute | solution.py:51
  78.2 8.9 %collective-permute-start.13 = (bf16[128,192]{1,0:T(8,128)(2,1)S(1)}, bf16[128,192]{1,0:T(8,128)(2,1)S(1)}, u32[]{:S(2)}, u32[]{:S(2)}) collective-permute-start(bf16[128,192]{1,0:T(8,128)(2,1)S(1)} %get-tuple-element.33), channel_id=1, source_target_pairs={{0,192},{64,128},{128,64},{192,0},{1,193},{65,129},{129,65},{193,1... | collective-permute-start | bytes 147464 | tf_op jit(solution)/shard_map/ppermute | solution.py:51
  90.2 37.9 %all-to-all-start.2 = ((bf16[16,432,128]{2,1,0:T(8,128)(2,1)}), bf16[16,432,128]{2,1,0:T(8,128)(2,1)S(1)}, u32[]{:S(2)}, u32[]{:S(2)}) async-start(bf16[16,432,128]{2,1,0:T(8,128)(2,1)} %bitcast.7), calls=%async_computation.2 | async-start | bytes 3538944 | tf_op jit(solution)/shard_map/all_to_all | solution.py:385
  97.5 25.6 %collective-permute-start.2 = (bf16[16,768]{1,0:T(8,128)(2,1)S(1)}, bf16[16,768]{1,0:T(8,128)(2,1)S(1)}, u32[]{:S(2)}, u32[]{:S(2)}) collective-permute-start(bf16[16,768]{1,0:T(8,128)(2,1)S(1)} %get-tuple-element.37), channel_id=1, source_target_pairs={{0,1},{1,2},{2,3},{3,4},{4,5},{5,6},{6,7},{7,8},{8,9},{9,10},{10,1... | collective-permute-start | bytes 73736 | tf_op jit(solution)/shard_map/ppermute | solution.py:32
  101.4 21.7 %collective-permute-start.3 = (bf16[16,768]{1,0:T(8,128)(2,1)S(1)}, bf16[16,768]{1,0:T(8,128)(2,1)S(1)}, u32[]{:S(2)}, u32[]{:S(2)}) collective-permute-start(bf16[16,768]{1,0:T(8,128)(2,1)S(1)} %get-tuple-element.38), channel_id=1, source_target_pairs={{1,0},{2,1},{3,2},{4,3},{5,4},{6,5},{7,6},{8,7},{9,8},{10,9},{11,1... | collective-permute-start | bytes 73736 | tf_op jit(solution)/shard_map/ppermute | solution.py:33
  103.4 24.5 %copy-start.2 = (bf16[1,128,768]{2,1,0:T(8,128)(2,1)S(1)}, bf16[1,128,768]{2,1,0:T(8,128)(2,1)}, u32[]{:S(2)}) copy-start(bf16[1,128,768]{2,1,0:T(8,128)(2,1)} %param.9) | copy-start | bytes 589828
  129.0 14.5 %all-to-all-start.3 = ((bf16[4,144,128]{2,1,0:T(8,128)(2,1)}), bf16[4,144,128]{2,1,0:T(8,128)(2,1)S(1)}, u32[]{:S(2)}, u32[]{:S(2)}) async-start(bf16[4,144,128]{2,1,0:T(8,128)(2,1)} %shard_map.109), calls=%async_computation.3 | async-start | bytes 294912 | tf_op jit(solution)/shard_map/all_to_all | solution.py:401
